TPU v7x, 32 devices: a whole 2x2x4 slice. The times are simulated.
32 devices in a mesh: ctx: 8 (over z, y), head: 4 (over x, core).
Axes of the slice: x: 2, y: 2, z: 4, core: 2. Of those that a mesh axis runs over, the one named last changes fastest.
Arguments:
- queries: bfloat16 [8192, 2048], P('ctx', 'head'), may hold values from -6 to 6
- keys: bfloat16 [8192, 2048], P('ctx', 'head'), may hold values from -6 to 6
- values: bfloat16 [8192, 2048], P('ctx', 'head'), may hold values from -36 to 36
- mem_route: int32 [8192], P('ctx'), may hold values from 0 to 3
- head_gain: float32 [2048], P('head'), may hold values from 0.25 to 1.75
- residual_in: bfloat16 [8192, 2048], P(('ctx', 'head')), may hold values from -24 to 24
- ffn_gain: float32 [2048], replicated, may hold values from 0.25 to 1.75
- expert_ids: int32 [8192, 2], P(('ctx', 'head')), may hold values from 0 to 255, all different within a row; in each aligned block of 256 rows (0 to 255, 256 to 511, ...) at most 4 rows name the same one
- expert_gates: float32 [8192, 2], P(('ctx', 'head')), may hold values from 0.2 to 1
- w_gate: bfloat16 [256, 2048, 512], P(('ctx', 'head')), may hold values from -0.125 to 0.125
- w_up: bfloat16 [256, 2048, 512], P(('ctx', 'head')), may hold values from -0.125 to 0.125
- w_down: bfloat16 [256, 512, 2048], P(('ctx', 'head')), may hold values from -0.25 to 0.25
Outputs:
- layer_out: bfloat16 [8192, 2048], P(('ctx', 'head'))
Inputs may be any that keep to these rules, and one draw needn't show every extreme that they name: `expert_ids`: the two experts of a token differ. Among the 512 choices of the tokens of one device, no expert is named more than 4 times, a bound that some block reaches.
All inputs are finite; a program needn't handle non-finite values.
Results may differ from a plain program's by a relative error of at most 0.0095.
Values may be sent and summed in bfloat16 or wider, within the bound.
No kernel may reach another device: no remote copies, remote signals or barrier semaphores. Data moves between devices by JAX's collectives and lax.ppermute only.
A program may use at most 128 MiB of HBM per device.

v0:
```python
import functools

import jax
import jax.numpy as jnp
from jax import lax
from jax.experimental import pallas as pl
from jax.experimental.pallas import tpu as pltpu
from jax.sharding import PartitionSpec as P

HD = 128
M = 4
CAP = 4
PAIR = 2
GROUP_ROWS = PAIR * CAP
EPS = 1e-06
F32 = jnp.float32
BF16 = jnp.bfloat16


def params(**more):
    return pltpu.CompilerParams(vmem_limit_bytes=60 * 1024 * 1024, **more)


def contract(a, b, dims):
    return lax.dot_general(a, b, (dims, ((), ())), preferred_element_type=F32)


def state_kernel(key_ref, value_ref, route_ref, out_ref):
    keys_t = key_ref[...].T
    values = value_ref[...]
    route = route_ref[...]
    for m in range(M):
        mask = (route == m).astype(F32).astype(BF16)
        out_ref[pl.ds(m * HD, HD), :] = contract(keys_t * mask, values, ((1,), (0,))).astype(BF16)


def block_states(keys, values, route_row):
    length, width = keys.shape
    heads = width // HD
    return pl.pallas_call(
        state_kernel,
        name="block_states",
        grid=(heads,),
        in_specs=[
            pl.BlockSpec((length, HD), lambda h: (0, h)),
            pl.BlockSpec((length, HD), lambda h: (0, h)),
            pl.BlockSpec((1, length), lambda h: (0, 0)),
        ],
        out_specs=pl.BlockSpec((M * HD, HD), lambda h: (h, 0)),
        out_shape=jax.ShapeDtypeStruct((heads * M * HD, HD), BF16),
        compiler_params=params(),
    )(keys, values, route_row)


def prefix_kernel(ranks, piece_ref, out_ref):
    total = jnp.zeros(piece_ref.shape[1:], F32)
    for r in range(ranks):
        out_ref[r] = total.astype(BF16)
        if r + 1 < ranks:
            total = total + piece_ref[r].astype(F32)


def exclusive_prefix(pieces):
    return pl.pallas_call(
        functools.partial(prefix_kernel, pieces.shape[0]),
        name="exclusive_prefix",
        out_shape=jax.ShapeDtypeStruct(pieces.shape, BF16),
        compiler_params=params(),
    )(pieces)


def local_kernel(rows, query_ref, key_ref, value_ref, route_row_ref, route_col_ref, out_ref, weight_ref):
    length = query_ref.shape[0]

    @pl.when(pl.program_id(0) == 0)
    def _():
        route_row = route_row_ref[...]
        for i in range(length // rows):
            span = (i + 1) * rows
            column = route_col_ref[pl.ds(i * rows, rows), :]
            same = jnp.where(column == route_row[:, :span], 2.0, 1.0)
            t = lax.broadcasted_iota(jnp.int32, (rows, span), 0) + i * rows
            s = lax.broadcasted_iota(jnp.int32, (rows, span), 1)
            weight_ref[pl.ds(i * rows, rows), :span] = jnp.where(t >= s, same, 0.0)

    for i in range(length // rows):
        span = (i + 1) * rows
        query = query_ref[pl.ds(i * rows, rows), :]
        scores = contract(query, key_ref[:span, :], ((1,), (1,)))
        weighted = (scores * weight_ref[pl.ds(i * rows, rows), :span]).astype(BF16)
        out_ref[pl.ds(i * rows, rows), :] = contract(weighted, value_ref[:span, :], ((1,), (0,)))


def local_attention(queries, keys, values, route_row, route_col):
    length, width = queries.shape
    heads = width // HD
    rows = min(256, length)
    wide = pl.BlockSpec((length, HD), lambda h: (0, h))
    return pl.pallas_call(
        functools.partial(local_kernel, rows),
        name="local_attention",
        grid=(heads,),
        in_specs=[
            wide,
            wide,
            wide,
            pl.BlockSpec((1, length), lambda h: (0, 0)),
            pl.BlockSpec((length, 1), lambda h: (0, 0)),
        ],
        out_specs=wide,
        out_shape=jax.ShapeDtypeStruct((length, width), F32),
        scratch_shapes=[pltpu.VMEM((length, length), F32)],
        compiler_params=params(),
    )(queries, keys, values, route_row, route_col)


def mix_kernel(query_ref, state_ref, local_ref, route_col_ref, gain_ref, out_ref):
    parts, rows, _ = out_ref.shape
    query = query_ref[...]
    column = route_col_ref[...]
    wide = jnp.concatenate(
        [query * jnp.where(column == m, 2.0, 1.0).astype(BF16) for m in range(M)], axis=1
    )
    mixed = contract(wide, state_ref[...], ((1,), (0,))) + local_ref[...]
    scale = lax.rsqrt(jnp.mean(mixed * mixed, axis=-1, keepdims=True) + EPS)
    normed = (mixed * scale * gain_ref[...]).astype(BF16)
    for p in range(parts):
        out_ref[p] = normed[p * rows:(p + 1) * rows]


def mix_and_norm(queries, state, local, route_col, head_gain, parts):
    length, width = queries.shape
    heads = width // HD
    wide = pl.BlockSpec((length, HD), lambda h: (0, h))
    return pl.pallas_call(
        mix_kernel,
        name="mix_and_norm",
        grid=(heads,),
        in_specs=[
            wide,
            pl.BlockSpec((M * HD, HD), lambda h: (h, 0)),
            wide,
            pl.BlockSpec((length, 1), lambda h: (0, 0)),
            pl.BlockSpec((1, HD), lambda h: (0, h)),
        ],
        out_specs=pl.BlockSpec((parts, length // parts, HD), lambda h: (0, 0, h)),
        out_shape=jax.ShapeDtypeStruct((parts, length // parts, width), BF16),
        compiler_params=params(),
    )(queries, state, local, route_col, head_gain)


def slot_columns(ids, experts, local_experts):
    tokens = ids.shape[0]
    owners = experts // local_experts
    lanes = lax.broadcasted_iota(jnp.int32, (tokens, experts), 1)
    chosen = [(ids[:, j:j + 1] == lanes).astype(F32) for j in range(2)]
    t = lax.broadcasted_iota(jnp.int32, (tokens, tokens), 0)
    s = lax.broadcasted_iota(jnp.int32, (tokens, tokens), 1)
    earlier = contract(
        (t > s).astype(F32).astype(BF16), (chosen[0] + chosen[1]).astype(BF16), ((1,), (0,))
    )
    slots = []
    for j in range(2):
        rank = jnp.sum(earlier * chosen[j], axis=1, keepdims=True).astype(jnp.int32)
        expert = ids[:, j:j + 1]
        owner = expert // local_experts
        local = expert % local_experts
        slots.append(
            ((local // PAIR) * owners + owner) * GROUP_ROWS + (local % PAIR) * CAP + rank
        )
    return slots


def pack_kernel(chunks, local_experts, residual_ref, piece_ref, gain_ref, ids_ref, *refs):
    stream_ref, out_refs = refs[0], refs[1:1 + chunks]
    parts, rows, _ = piece_ref.shape
    owners, groups, _, width = out_refs[0].shape
    normed = jnp.concatenate([piece_ref[p] for p in range(parts)], axis=1)
    stream = (residual_ref[...].astype(F32) + normed.astype(F32)).astype(BF16)
    stream_ref[...] = stream
    wide = stream.astype(F32)
    scale = lax.rsqrt(jnp.mean(wide * wide, axis=-1, keepdims=True) + EPS)
    ffn_in = (wide * scale * gain_ref[...]).astype(BF16)
    experts = owners * local_experts
    slot0, slot1 = slot_columns(ids_ref[...], experts, local_experts)
    span = owners * GROUP_ROWS
    for c in range(chunks):
        for g in range(groups):
            base = (c * groups + g) * span
            lanes = lax.broadcasted_iota(jnp.int32, (rows, span), 1) + base
            spread = jnp.where((slot0 == lanes) | (slot1 == lanes), 1.0, 0.0).astype(BF16)
            packed = contract(spread, ffn_in, ((0,), (0,))).astype(BF16)
            out_refs[c][:, g] = packed.reshape(owners, GROUP_ROWS, width)


def pack(residual, pieces, gain, ids, chunks, owners, local_experts):
    tokens, width = residual.shape
    groups = local_experts // PAIR // chunks
    parcel = jax.ShapeDtypeStruct((owners, groups, GROUP_ROWS, width), BF16)
    out = pl.pallas_call(
        functools.partial(pack_kernel, chunks, local_experts),
        name="pack",
        out_shape=[jax.ShapeDtypeStruct((tokens, width), BF16)] + [parcel] * chunks,
        compiler_params=params(),
    )(residual, pieces, gain, ids)
    return out[0], out[1:]


def expert_kernel(x_ref, gate_ref, up_ref, down_ref, out_ref, acc_ref):
    e = pl.program_id(1)
    f = pl.program_id(2)
    owners, rows, width = x_ref.shape
    x = x_ref[...].reshape(owners * rows, width)
    gate = contract(x, gate_ref[...], ((1,), (0,)))
    upward = contract(x, up_ref[...], ((1,), (0,)))
    row = lax.broadcasted_iota(jnp.int32, gate.shape, 0)
    mine = (row // CAP) % PAIR == e
    hidden = gate / (1.0 + jnp.exp(-gate)) * upward
    hidden = jnp.where(mine, hidden, 0.0).astype(BF16)
    part = contract(hidden, down_ref[...], ((1,), (0,)))
    first = (e == 0) & (f == 0)

    @pl.when(first)
    def _():
        acc_ref[...] = part

    @pl.when(jnp.logical_not(first))
    def _():
        acc_ref[...] = acc_ref[...] + part

    @pl.when((e == pl.num_programs(1) - 1) & (f == pl.num_programs(2) - 1))
    def _():
        out_ref[...] = acc_ref[...].astype(BF16).reshape(owners, rows, width)


def serve_experts(received, w_gate, w_up, w_down, chunk):
    owners, groups, rows, width = received.shape
    hidden = w_gate.shape[2]
    split = 2
    step = hidden // split
    first = chunk * groups * PAIR
    token_spec = pl.BlockSpec((owners, None, rows, width), lambda g, e, f: (0, g, 0, 0))
    in_spec = pl.BlockSpec((None, width, step), lambda g, e, f: (first + g * PAIR + e, 0, f))
    return pl.pallas_call(
        expert_kernel,
        name=f"experts_{chunk}",
        grid=(groups, PAIR, split),
        in_specs=[
            token_spec,
            in_spec,
            in_spec,
            pl.BlockSpec((None, step, width), lambda g, e, f: (first + g * PAIR + e, f, 0)),
        ],
        out_specs=token_spec,
        out_shape=jax.ShapeDtypeStruct(received.shape, BF16),
        scratch_shapes=[pltpu.VMEM((owners * rows, width), F32)],
        compiler_params=params(),
    )(received, w_gate, w_up, w_down)


def combine_kernel(chunks, local_experts, stream_ref, ids_ref, gates_ref, *refs):
    back_refs, out_ref, first_ref, second_ref = refs[:chunks], refs[chunks], refs[-2], refs[-1]
    tokens = stream_ref.shape[0]
    owners, groups, rows, _ = back_refs[0].shape
    span = owners * rows

    @pl.when(pl.program_id(0) == 0)
    def _():
        slot0, slot1 = slot_columns(ids_ref[...], owners * local_experts, local_experts)
        lanes = lax.broadcasted_iota(jnp.int32, first_ref.shape, 1)
        first_ref[...] = jnp.where(slot0 == lanes, 1.0, 0.0).astype(BF16)
        second_ref[...] = jnp.where(slot1 == lanes, 1.0, 0.0).astype(BF16)

    back = jnp.concatenate(
        [
            back_refs[c][:, g].reshape(span, back_refs[c].shape[3])
            for c in range(chunks)
            for g in range(groups)
        ],
        axis=0,
    )
    gates = gates_ref[...]
    total = stream_ref[...].astype(F32)
    total = total + gates[:, 0:1] * contract(first_ref[...], back, ((1,), (0,)))
    total = total + gates[:, 1:2] * contract(second_ref[...], back, ((1,), (0,)))
    out_ref[...] = total.astype(BF16)


def combine(stream, ids, gates, backs, local_experts):
    tokens, width = stream.shape
    owners, groups, rows, _ = backs[0].shape
    chunks = len(backs)
    slots = owners * groups * rows * chunks
    step = min(512, width)
    back_spec = pl.BlockSpec((owners, groups, rows, step), lambda d: (0, 0, 0, d))
    return pl.pallas_call(
        functools.partial(combine_kernel, chunks, local_experts),
        name="combine",
        grid=(width // step,),
        in_specs=[
            pl.BlockSpec((tokens, step), lambda d: (0, d)),
            pl.BlockSpec(ids.shape, lambda d: (0, 0)),
            pl.BlockSpec(gates.shape, lambda d: (0, 0)),
        ]
        + [back_spec] * chunks,
        out_specs=pl.BlockSpec((tokens, step), lambda d: (0, d)),
        out_shape=jax.ShapeDtypeStruct((tokens, width), BF16),
        scratch_shapes=[pltpu.VMEM((tokens, slots), BF16)] * 2,
        compiler_params=params(),
    )(stream, ids, gates, *backs)


def body(
    queries,
    keys,
    values,
    mem_route,
    head_gain,
    residual_in,
    ffn_gain,
    expert_ids,
    expert_gates,
    w_gate,
    w_up,
    w_down,
):
    length = queries.shape[0]
    ctx_count = lax.axis_size("ctx")
    head_count = lax.axis_size("head")
    owners = ctx_count * head_count
    local_experts = w_gate.shape[0]
    pairs = local_experts // PAIR
    chunks = 2 if pairs % 2 == 0 else 1
    route_row = mem_route.reshape(1, length)
    route_col = mem_route.reshape(length, 1)

    states = block_states(keys, values, route_row)
    pieces = lax.all_to_all(states, "ctx", split_axis=0, concat_axis=0, tiled=True)
    before = exclusive_prefix(pieces.reshape(ctx_count, -1, HD))
    carried = lax.all_to_all(
        before.reshape(states.shape), "ctx", split_axis=0, concat_axis=0, tiled=True
    )
    local = local_attention(queries, keys, values, route_row, route_col)
    normed = mix_and_norm(queries, carried, local, route_col, head_gain[None], head_count)
    by_token = lax.all_to_all(normed, "head", split_axis=0, concat_axis=0, tiled=True)

    stream, parcels = pack(
        residual_in, by_token, ffn_gain[None], expert_ids, chunks, owners, local_experts
    )
    backs = []
    for c in range(chunks):
        received = lax.all_to_all(
            parcels[c], ("ctx", "head"), split_axis=0, concat_axis=0, tiled=True
        )
        served = serve_experts(received, w_gate, w_up, w_down, c)
        backs.append(
            lax.all_to_all(served, ("ctx", "head"), split_axis=0, concat_axis=0, tiled=True)
        )
    return combine(stream, expert_ids, expert_gates, backs, local_experts)


def solution(mesh):
    placed = (
        P("ctx", "head"),
        P("ctx", "head"),
        P("ctx", "head"),
        P("ctx"),
        P("head"),
        P(("ctx", "head"), None),
        P(),
        P(("ctx", "head"), None),
        P(("ctx", "head"), None),
        P(("ctx", "head"), None, None),
        P(("ctx", "head"), None, None),
        P(("ctx", "head"), None, None),
    )
    return jax.shard_map(
        body, mesh=mesh, in_specs=placed, out_specs=P(("ctx", "head"), None), check_vma=False
    )
```

profile of v0, /device:TPU:0, one launch (start us, length us, event | category | flops | bytes accessed | tf_op | source)
XLA Modules:
  0.0 296.5 jit_solution(16588606396443531755)
XLA Ops:
  0.0 4.4 %block_states.1 = bf16[2048,128]{1,0:T(8,128)(2,1)} custom-call(bf16[1024,512]{1,0:T(8,128)(2,1)} %key_ref.3, bf16[1024,512]{1,0:T(8,128)(2,1)} %value_ref.3, s32[1,1024]{1,0:T(1,128)} %bitcast.8), custom_call_target="tpu_custom_call" | custom-call | tf_op jit(solution)/shard_map/block_states/pallas_call | solution.py:40
  4.4 22.1 %all_to_all.42.piece_ref = bf16[8,256,128]{2,1,0:T(8,128)(2,1)} all-to-all(bf16[8,256,128]{2,1,0:T(8,128)(2,1)} %bitcast.7), channel_id=1, replica_groups=mesh['ctx'=8,'head'=4] {'ctx'}, dimensions={0} | all-to-all | bytes 1048576 | tf_op jit(solution)/shard_map/all_to_all | solution.py:338
  26.5 1.9 exclusive_prefix.1
  28.4 3.6 %all-to-all-start.1 = ((bf16[8,256,128]{2,1,0:T(8,128)(2,1)}), bf16[8,256,128]{2,1,0:T(8,128)(2,1)S(1)}, u32[]{:S(2)}, u32[]{:S(2)}) async-start(bf16[8,256,128]{2,1,0:T(8,128)(2,1)} %exclusive_prefix.1), calls=%async_computation.1 | async-start | bytes 1048576 | tf_op jit(solution)/shard_map/all_to_all | solution.py:340
  32.0 1.0 copy.16.route_col_ref
  33.0 7.2 %local_attention.1.local_ref = f32[1024,512]{1,0:T(8,128)} custom-call(bf16[1024,512]{1,0:T(8,128)(2,1)} %query_ref.3, bf16[1024,512]{1,0:T(8,128)(2,1)} %key_ref.3, bf16[1024,512]{1,0:T(8,128)(2,1)} %value_ref.3, s32[1,1024]{1,0:T(1,128)} %bitcast.9, s32[1024,1]{1,0:T(8,128)} %copy.16.route_col_ref), custom_call_target="tpu_custom_call" | custom-call | tf_op jit(solution)/shard_map/local_attention/pallas_call | solution.py:99
  40.2 5.9 %all-to-all-done.1 = bf16[8,256,128]{2,1,0:T(8,128)(2,1)S(1)} async-done(((bf16[8,256,128]{2,1,0:T(8,128)(2,1)}), bf16[8,256,128]{2,1,0:T(8,128)(2,1)S(1)}, u32[]{:S(2)}, u32[]{:S(2)}) %all-to-all-start.1) | async-done | bytes 524320 | tf_op jit(solution)/shard_map/all_to_all | solution.py:340
  47.0 5.6 %mix_and_norm.1 = bf16[4,256,512]{2,1,0:T(8,128)(2,1)} custom-call(bf16[1024,512]{1,0:T(8,128)(2,1)} %query_ref.3, bf16[2048,128]{1,0:T(8,128)(2,1)} %bitcast.6, f32[1024,512]{1,0:T(8,128)} %local_attention.1.local_ref, s32[1024,1]{1,0:T(8,128)} %copy.16.route_col_ref, f32[1,512]{1,0:T(1,128)} %bitcast.12), custom_call_target="tpu_custom_call" | custom-call | tf_op jit(solution)/shard_map/mix_and_norm/pallas_call | solution.py:135
  52.6 3.6 %all-to-all-start.2 = ((bf16[4,256,512]{2,1,0:T(8,128)(2,1)}), bf16[4,256,512]{2,1,0:T(8,128)(2,1)S(1)}, u32[]{:S(2)}, u32[]{:S(2)}) async-start(bf16[4,256,512]{2,1,0:T(8,128)(2,1)} %mix_and_norm.1), calls=%async_computation.2 | async-start | bytes 2097152 | tf_op jit(solution)/shard_map/all_to_all | solution.py:345
  57.1 13.6 %all-to-all-done.2.piece_ref = bf16[4,256,512]{2,1,0:T(8,128)(2,1)S(1)} async-done(((bf16[4,256,512]{2,1,0:T(8,128)(2,1)}), bf16[4,256,512]{2,1,0:T(8,128)(2,1)S(1)}, u32[]{:S(2)}, u32[]{:S(2)}) %all-to-all-start.2) | async-done | bytes 1048608 | tf_op jit(solution)/shard_map/all_to_all | solution.py:345
  70.7 1.0 copy-done.2
  71.7 5.3 %pack.1 = (bf16[256,2048]{1,0:T(8,128)(2,1)}, bf16[32,2,8,2048]{3,2,1,0:T(8,128)(2,1)}, bf16[32,2,8,2048]{3,2,1,0:T(8,128)(2,1)}) custom-call(bf16[256,2048]{1,0:T(8,128)(2,1)} %residual_ref.1, bf16[4,256,512]{2,1,0:T(8,128)(2,1)} %copy-done.2, f32[1,2048]{1,0:T(1,128)} %bitcast.11, s32[256,2]{1,0:T(8,128)} %copy.18.ids_ref), custom_call_target="tpu_custom_call" | custom-call | tf_op jit(solution)/shard_map/pack/pallas_call | solution.py:200
  77.0 52.1 %all_to_all.43.x_ref = bf16[32,2,8,2048]{3,2,1,0:T(8,128)(2,1)} all-to-all(bf16[32,2,8,2048]{3,2,1,0:T(8,128)(2,1)} %get-tuple-element.9), channel_id=1, replica_groups=mesh['ctx'=8,'head'=4] {'ctx','head'}, dimensions={0} | all-to-all | bytes 4194304 | tf_op jit(solution)/shard_map/all_to_all | solution.py:352
  129.1 3.6 %all-to-all-start.5 = ((bf16[32,2,8,2048]{3,2,1,0:T(8,128)(2,1)}), bf16[32,2,8,2048]{3,2,1,0:T(8,128)(2,1)S(1)}, u32[]{:S(2)}, u32[]{:S(2)}) async-start(bf16[32,2,8,2048]{3,2,1,0:T(8,128)(2,1)} %get-tuple-element.10), calls=%async_computation.5 | async-start | bytes 4194304 | tf_op jit(solution)/shard_map/all_to_all | solution.py:352
  132.7 16.1 %experts_0.1 = bf16[32,2,8,2048]{3,2,1,0:T(8,128)(2,1)} custom-call(bf16[32,2,8,2048]{3,2,1,0:T(8,128)(2,1)} %all_to_all.43.x_ref, bf16[8,2048,512]{2,1,0:T(8,128)(2,1)} %gate_ref.3, bf16[8,2048,512]{2,1,0:T(8,128)(2,1)} %up_ref.3, bf16[8,512,2048]{2,1,0:T(8,128)(2,1)} %down_ref.3), custom_call_target="tpu_custom_call" | custom-call | tf_op jit(solution)/shard_map/experts_0/pallas_call | solution.py:244
  148.8 32.6 %all-to-all-done.5.x_ref = bf16[32,2,8,2048]{3,2,1,0:T(8,128)(2,1)S(1)} async-done(((bf16[32,2,8,2048]{3,2,1,0:T(8,128)(2,1)}), bf16[32,2,8,2048]{3,2,1,0:T(8,128)(2,1)S(1)}, u32[]{:S(2)}, u32[]{:S(2)}) %all-to-all-start.5) | async-done | bytes 2097184 | tf_op jit(solution)/shard_map/all_to_all | solution.py:352
  181.4 1.3 copy-done.1
  182.8 4.1 %all-to-all-start.4 = ((bf16[32,2,8,2048]{3,2,1,0:T(8,128)(2,1)}), bf16[32,2,8,2048]{3,2,1,0:T(8,128)(2,1)S(1)}, u32[]{:S(2)}, u32[]{:S(2)}) async-start(bf16[32,2,8,2048]{3,2,1,0:T(8,128)(2,1)} %experts_0.1), calls=%async_computation.4 | async-start | bytes 4194304 | tf_op jit(solution)/shard_map/all_to_all | solution.py:357
  186.9 16.1 %experts_1.1 = bf16[32,2,8,2048]{3,2,1,0:T(8,128)(2,1)} custom-call(bf16[32,2,8,2048]{3,2,1,0:T(8,128)(2,1)} %copy-done.1, bf16[8,2048,512]{2,1,0:T(8,128)(2,1)} %gate_ref.3, bf16[8,2048,512]{2,1,0:T(8,128)(2,1)} %up_ref.3, bf16[8,512,2048]{2,1,0:T(8,128)(2,1)} %down_ref.3), custom_call_target="tpu_custom_call" | custom-call | tf_op jit(solution)/shard_map/experts_1/pallas_call | solution.py:244
  203.0 32.6 %all-to-all-done.4.refs_0_ = bf16[32,2,8,2048]{3,2,1,0:T(8,128)(2,1)S(1)} async-done(((bf16[32,2,8,2048]{3,2,1,0:T(8,128)(2,1)}), bf16[32,2,8,2048]{3,2,1,0:T(8,128)(2,1)S(1)}, u32[]{:S(2)}, u32[]{:S(2)}) %all-to-all-start.4) | async-done | bytes 2097184 | tf_op jit(solution)/shard_map/all_to_all | solution.py:357
  235.6 1.3 copy-done
  236.9 4.2 %all-to-all-start.6 = ((bf16[32,2,8,2048]{3,2,1,0:T(8,128)(2,1)}), bf16[32,2,8,2048]{3,2,1,0:T(8,128)(2,1)}, u32[]{:S(2)}, u32[]{:S(2)}) async-start(bf16[32,2,8,2048]{3,2,1,0:T(8,128)(2,1)} %experts_1.1), calls=%async_computation.6 | async-start | bytes 4194304 | tf_op jit(solution)/shard_map/all_to_all | solution.py:357
  241.9 47.9 %all-to-all-done.6.refs_1_ = bf16[32,2,8,2048]{3,2,1,0:T(8,128)(2,1)} async-done(((bf16[32,2,8,2048]{3,2,1,0:T(8,128)(2,1)}), bf16[32,2,8,2048]{3,2,1,0:T(8,128)(2,1)}, u32[]{:S(2)}, u32[]{:S(2)}) %all-to-all-start.6) | async-done | bytes 2097184 | tf_op jit(solution)/shard_map/all_to_all | solution.py:357
  289.9 6.6 %combine.1 = bf16[256,2048]{1,0:T(8,128)(2,1)} custom-call(bf16[256,2048]{1,0:T(8,128)(2,1)} %get-tuple-element.8.stream_ref, s32[256,2]{1,0:T(8,128)} %copy.18.ids_ref, f32[256,2]{1,0:T(8,128)} %copy.20.gates_ref, bf16[32,2,8,2048]{3,2,1,0:T(8,128)(2,1)} %copy-done, bf16[32,2,8,2048]{3,2,1,0:T(8,128)(2,1)} %all-to-all-done.6.refs_1_), custom_call_target="tpu_custom_call" | custom-call | tf_op jit(solution)/shard_map/combine/pallas_call | solution.py:296
  (13 shorter events, 2.4 us)
Async XLA Ops:
  4.4 27.6 %copy-start.4 = (s32[1024]{0:T(1024)S(1)}, s32[1024]{0:T(1024)}, u32[]{:S(2)}) copy-start(s32[1024]{0:T(1024)} %param.15) | copy-start | bytes 12292
  28.4 17.8 %all-to-all-start.1 = ((bf16[8,256,128]{2,1,0:T(8,128)(2,1)}), bf16[8,256,128]{2,1,0:T(8,128)(2,1)S(1)}, u32[]{:S(2)}, u32[]{:S(2)}) async-start(bf16[8,256,128]{2,1,0:T(8,128)(2,1)} %exclusive_prefix.1), calls=%async_computation.1 | async-start | bytes 1048576 | tf_op jit(solution)/shard_map/all_to_all | solution.py:340
  46.2 0.8 copy-start.3
  52.6 3.7 %copy-start.5 = (s32[256,2]{0,1:T(2,128)S(1)}, s32[256,2]{0,1:T(2,128)}, u32[]{:S(2)}) copy-start(s32[256,2]{0,1:T(2,128)} %param.19) | copy-start | bytes 6148
  52.6 18.1 %all-to-all-start.2 = ((bf16[4,256,512]{2,1,0:T(8,128)(2,1)}), bf16[4,256,512]{2,1,0:T(8,128)(2,1)S(1)}, u32[]{:S(2)}, u32[]{:S(2)}) async-start(bf16[4,256,512]{2,1,0:T(8,128)(2,1)} %mix_and_norm.1), calls=%async_computation.2 | async-start | bytes 2097152 | tf_op jit(solution)/shard_map/all_to_all | solution.py:345
  70.7 1.0 copy-start.2
  129.1 52.3 %all-to-all-start.5 = ((bf16[32,2,8,2048]{3,2,1,0:T(8,128)(2,1)}), bf16[32,2,8,2048]{3,2,1,0:T(8,128)(2,1)S(1)}, u32[]{:S(2)}, u32[]{:S(2)}) async-start(bf16[32,2,8,2048]{3,2,1,0:T(8,128)(2,1)} %get-tuple-element.10), calls=%async_computation.5 | async-start | bytes 4194304 | tf_op jit(solution)/shard_map/all_to_all | solution.py:352
  181.4 1.3 copy-start.1
  182.8 52.8 %all-to-all-start.4 = ((bf16[32,2,8,2048]{3,2,1,0:T(8,128)(2,1)}), bf16[32,2,8,2048]{3,2,1,0:T(8,128)(2,1)S(1)}, u32[]{:S(2)}, u32[]{:S(2)}) async-start(bf16[32,2,8,2048]{3,2,1,0:T(8,128)(2,1)} %experts_0.1), calls=%async_computation.4 | async-start | bytes 4194304 | tf_op jit(solution)/shard_map/all_to_all | solution.py:357
  203.0 38.2 %copy-start.6 = (f32[256,2]{0,1:T(2,128)S(1)}, f32[256,2]{0,1:T(2,128)}, u32[]{:S(2)}) copy-start(f32[256,2]{0,1:T(2,128)} %param.20) | copy-start | bytes 6148
  235.6 1.3 copy-start
  236.9 52.9 %all-to-all-start.6 = ((bf16[32,2,8,2048]{3,2,1,0:T(8,128)(2,1)}), bf16[32,2,8,2048]{3,2,1,0:T(8,128)(2,1)}, u32[]{:S(2)}, u32[]{:S(2)}) async-start(bf16[32,2,8,2048]{3,2,1,0:T(8,128)(2,1)} %experts_1.1), calls=%async_computation.6 | async-start | bytes 4194304 | tf_op jit(solution)/shard_map/all_to_all | solution.py:357
where the time goes:
time: 298 us; the launch traced here: 296 us
  waiting for transfers between devices  133 us (45%)
  blocking collectives  74.2 us (25%)
  Pallas kernels  63.3 us (21%)
  starting transfers between devices  19.1 us (6%)
  local copies, waits for them, and re-layouts  7.09 us (2%)
    all_to_all x2, waiting for transfers between devices, body(): lax.all_to_all(served, ('ctx', 'head'), split_axis=0, concat_axis=0, tile...  80.5 us
    all_to_all x1, blocking collectives, body(): lax.all_to_all(parcels[c], ('ctx', 'head'), split_axis=0, concat_axis=0,...  52.1 us
    all_to_all x1, waiting for transfers between devices, body(): lax.all_to_all(parcels[c], ('ctx', 'head'), split_axis=0, concat_axis=0,...  32.6 us
    pallas_call x2, Pallas kernels, serve_experts(): pl.pallas_call(expert_kernel, name=f'experts_{chunk}', grid=(groups, PAIR...  32.2 us
    all_to_all x1, blocking collectives, body(): lax.all_to_all(states, 'ctx', split_axis=0, concat_axis=0, tiled=True)  22.1 us
    all_to_all x1, waiting for transfers between devices, body(): lax.all_to_all(normed, 'head', split_axis=0, concat_axis=0, tiled=True)  13.6 us
    all_to_all x2, starting transfers between devices, body(): lax.all_to_all(served, ('ctx', 'head'), split_axis=0, concat_axis=0, tile...  8.31 us
    pallas_call x1, Pallas kernels, local_attention(): pl.pallas_call(functools.partial(local_kernel, rows), name='local_attenti...  7.19 us
  transfers between devices with their start and end apart: 5, of which 5 were waited for; matrix products, arithmetic and copies ran while one was open for 1% of the time, Pallas kernels for 13%

commit v1 on v0

--- a/solution.py
+++ b/solution.py
@@ -6,6 +6,7 @@
 from jax.experimental import pallas as pl
 from jax.experimental.pallas import tpu as pltpu
 from jax.sharding import PartitionSpec as P
+
 
 HD = 128
 M = 4
@@ -25,46 +26,64 @@
     return lax.dot_general(a, b, (dims, ((), ())), preferred_element_type=F32)
 
 
-def state_kernel(key_ref, value_ref, route_ref, out_ref):
+def state_kernel(tail, key_ref, value_ref, route_ref, meta_ref, out_ref):
+    parts, rows, _ = out_ref.shape
+    rows -= tail
+    head = pl.program_id(0)
     keys_t = key_ref[...].T
     values = value_ref[...]
     route = route_ref[...]
+    states = []
     for m in range(M):
         mask = (route == m).astype(F32).astype(BF16)
-        out_ref[pl.ds(m * HD, HD), :] = contract(keys_t * mask, values, ((1,), (0,))).astype(BF16)
-
-
-def block_states(keys, values, route_row):
+        states.append(contract(keys_t * mask, values, ((1,), (0,))).astype(BF16))
+    flat = jnp.concatenate(states, axis=0)
+    share = M * HD // rows
+    for i in range(share):
+        out_ref[head * share + i, :rows, :] = flat[i * rows:(i + 1) * rows]
+
+    @pl.when(head == 0)
+    def _():
+        for p in range(parts):
+            out_ref[p, rows:, :] = meta_ref[p].astype(BF16)
+
+
+def block_states(keys, values, route_row, meta, parts):
     length, width = keys.shape
     heads = width // HD
-    return pl.pallas_call(
-        state_kernel,
+    rows = heads * M * HD // parts
+    tail = meta.shape[1]
+    return pl.pallas_call(
+        functools.partial(state_kernel, tail),
         name="block_states",
         grid=(heads,),
         in_specs=[
             pl.BlockSpec((length, HD), lambda h: (0, h)),
             pl.BlockSpec((length, HD), lambda h: (0, h)),
             pl.BlockSpec((1, length), lambda h: (0, 0)),
+            pl.BlockSpec(meta.shape, lambda h: (0, 0, 0)),
         ],
-        out_specs=pl.BlockSpec((M * HD, HD), lambda h: (h, 0)),
-        out_shape=jax.ShapeDtypeStruct((heads * M * HD, HD), BF16),
-        compiler_params=params(),
-    )(keys, values, route_row)
+        out_specs=pl.BlockSpec((parts, rows + tail, HD), lambda h: (0, 0, 0)),
+        out_shape=jax.ShapeDtypeStruct((parts, rows + tail, HD), BF16),
+        compiler_params=params(),
+    )(keys, values, route_row, meta)
 
 
 def prefix_kernel(ranks, piece_ref, out_ref):
-    total = jnp.zeros(piece_ref.shape[1:], F32)
+    rows = out_ref.shape[1]
+    total = jnp.zeros(out_ref.shape[1:], F32)
     for r in range(ranks):
         out_ref[r] = total.astype(BF16)
         if r + 1 < ranks:
-            total = total + piece_ref[r].astype(F32)
-
-
-def exclusive_prefix(pieces):
-    return pl.pallas_call(
-        functools.partial(prefix_kernel, pieces.shape[0]),
+            total = total + piece_ref[r, :rows, :].astype(F32)
+
+
+def exclusive_prefix(pieces, tail):
+    ranks, rows, width = pieces.shape
+    return pl.pallas_call(
+        functools.partial(prefix_kernel, ranks),
         name="exclusive_prefix",
-        out_shape=jax.ShapeDtypeStruct(pieces.shape, BF16),
+        out_shape=jax.ShapeDtypeStruct((ranks, rows - tail, width), BF16),
         compiler_params=params(),
     )(pieces)
 
@@ -114,8 +133,10 @@
     )(queries, keys, values, route_row, route_col)
 
 
-def mix_kernel(query_ref, state_ref, local_ref, route_col_ref, gain_ref, out_ref):
+def mix_kernel(query_ref, state_ref, local_ref, route_col_ref, gain_ref, meta_ref, out_ref):
     parts, rows, _ = out_ref.shape
+    blocks = meta_ref.shape[0]
+    rows -= blocks
     query = query_ref[...]
     column = route_col_ref[...]
     wide = jnp.concatenate(
@@ -125,11 +146,14 @@
     scale = lax.rsqrt(jnp.mean(mixed * mixed, axis=-1, keepdims=True) + EPS)
     normed = (mixed * scale * gain_ref[...]).astype(BF16)
     for p in range(parts):
-        out_ref[p] = normed[p * rows:(p + 1) * rows]
-
-
-def mix_and_norm(queries, state, local, route_col, head_gain, parts):
+        out_ref[p, :rows, :] = normed[p * rows:(p + 1) * rows]
+        tail = [meta_ref[c, p:p + 1, :].astype(F32) for c in range(blocks)]
+        out_ref[p, rows:, :] = jnp.concatenate(tail, axis=0).astype(BF16)
+
+
+def mix_and_norm(queries, state, local, route_col, head_gain, meta, parts):
     length, width = queries.shape
+    rows = length // parts + meta.shape[0]
     heads = width // HD
     wide = pl.BlockSpec((length, HD), lambda h: (0, h))
     return pl.pallas_call(
@@ -142,11 +166,12 @@
             wide,
             pl.BlockSpec((length, 1), lambda h: (0, 0)),
             pl.BlockSpec((1, HD), lambda h: (0, h)),
+            pl.BlockSpec(meta.shape, lambda h: (0, 0, 0)),
         ],
-        out_specs=pl.BlockSpec((parts, length // parts, HD), lambda h: (0, 0, h)),
-        out_shape=jax.ShapeDtypeStruct((parts, length // parts, width), BF16),
-        compiler_params=params(),
-    )(queries, state, local, route_col, head_gain)
+        out_specs=pl.BlockSpec((parts, rows, HD), lambda h: (0, 0, h)),
+        out_shape=jax.ShapeDtypeStruct((parts, rows, width), BF16),
+        compiler_params=params(),
+    )(queries, state, local, route_col, head_gain, meta)
 
 
 def slot_columns(ids, experts, local_experts):
@@ -171,11 +196,11 @@
     return slots
 
 
-def pack_kernel(chunks, local_experts, residual_ref, piece_ref, gain_ref, ids_ref, *refs):
+def pack_dense_kernel(chunks, local_experts, residual_ref, piece_ref, gain_ref, ids_ref, *refs):
     stream_ref, out_refs = refs[0], refs[1:1 + chunks]
-    parts, rows, _ = piece_ref.shape
+    parts, rows = piece_ref.shape[0], residual_ref.shape[0]
     owners, groups, _, width = out_refs[0].shape
-    normed = jnp.concatenate([piece_ref[p] for p in range(parts)], axis=1)
+    normed = jnp.concatenate([piece_ref[p, :rows, :] for p in range(parts)], axis=1)
     stream = (residual_ref[...].astype(F32) + normed.astype(F32)).astype(BF16)
     stream_ref[...] = stream
     wide = stream.astype(F32)
@@ -193,20 +218,20 @@
             out_refs[c][:, g] = packed.reshape(owners, GROUP_ROWS, width)
 
 
-def pack(residual, pieces, gain, ids, chunks, owners, local_experts):
+def pack_dense(residual, pieces, gain, ids, chunks, owners, local_experts):
     tokens, width = residual.shape
     groups = local_experts // PAIR // chunks
     parcel = jax.ShapeDtypeStruct((owners, groups, GROUP_ROWS, width), BF16)
     out = pl.pallas_call(
-        functools.partial(pack_kernel, chunks, local_experts),
-        name="pack",
+        functools.partial(pack_dense_kernel, chunks, local_experts),
+        name="pack_dense",
         out_shape=[jax.ShapeDtypeStruct((tokens, width), BF16)] + [parcel] * chunks,
         compiler_params=params(),
     )(residual, pieces, gain, ids)
     return out[0], out[1:]
 
 
-def expert_kernel(x_ref, gate_ref, up_ref, down_ref, out_ref, acc_ref):
+def expert_dense_kernel(x_ref, gate_ref, up_ref, down_ref, out_ref, acc_ref):
     e = pl.program_id(1)
     f = pl.program_id(2)
     owners, rows, width = x_ref.shape
@@ -233,7 +258,7 @@
         out_ref[...] = acc_ref[...].astype(BF16).reshape(owners, rows, width)
 
 
-def serve_experts(received, w_gate, w_up, w_down, chunk):
+def serve_dense(received, w_gate, w_up, w_down, chunk):
     owners, groups, rows, width = received.shape
     hidden = w_gate.shape[2]
     split = 2
@@ -242,8 +267,7 @@
     token_spec = pl.BlockSpec((owners, None, rows, width), lambda g, e, f: (0, g, 0, 0))
     in_spec = pl.BlockSpec((None, width, step), lambda g, e, f: (first + g * PAIR + e, 0, f))
     return pl.pallas_call(
-        expert_kernel,
-        name=f"experts_{chunk}",
+        expert_dense_kernel,
         grid=(groups, PAIR, split),
         in_specs=[
             token_spec,
@@ -258,9 +282,8 @@
     )(received, w_gate, w_up, w_down)
 
 
-def combine_kernel(chunks, local_experts, stream_ref, ids_ref, gates_ref, *refs):
+def combine_dense_kernel(chunks, local_experts, stream_ref, ids_ref, gates_ref, *refs):
     back_refs, out_ref, first_ref, second_ref = refs[:chunks], refs[chunks], refs[-2], refs[-1]
-    tokens = stream_ref.shape[0]
     owners, groups, rows, _ = back_refs[0].shape
     span = owners * rows
 
@@ -286,7 +309,7 @@
     out_ref[...] = total.astype(BF16)
 
 
-def combine(stream, ids, gates, backs, local_experts):
+def combine_dense(stream, ids, gates, backs, local_experts):
     tokens, width = stream.shape
     owners, groups, rows, _ = backs[0].shape
     chunks = len(backs)
@@ -294,8 +317,8 @@
     step = min(512, width)
     back_spec = pl.BlockSpec((owners, groups, rows, step), lambda d: (0, 0, 0, d))
     return pl.pallas_call(
-        functools.partial(combine_kernel, chunks, local_experts),
-        name="combine",
+        functools.partial(combine_dense_kernel, chunks, local_experts),
+        name="combine_dense",
         grid=(width // step,),
         in_specs=[
             pl.BlockSpec((tokens, step), lambda d: (0, d)),
@@ -308,6 +331,354 @@
         scratch_shapes=[pltpu.VMEM((tokens, slots), BF16)] * 2,
         compiler_params=params(),
     )(stream, ids, gates, *backs)
+
+
+def route_kernel(local_experts, plan, ids_ref, code_ref, meta_ref):
+    tokens = ids_ref.shape[0]
+    owners = meta_ref.shape[0]
+    experts = owners * local_experts
+    ids = ids_ref[...]
+    lanes = lax.broadcasted_iota(jnp.int32, (tokens, experts), 1)
+    chosen = [(ids[:, j:j + 1] == lanes).astype(F32) for j in range(2)]
+    both = (chosen[0] + chosen[1]).astype(BF16)
+    t = lax.broadcasted_iota(jnp.int32, (tokens, tokens), 0)
+    s = lax.broadcasted_iota(jnp.int32, (tokens, tokens), 1)
+    earlier = contract((t > s).astype(F32).astype(BF16), both, ((1,), (0,)))
+    counts = contract(jnp.ones((8, tokens), BF16), both, ((1,), (0,)))
+    row = lax.broadcasted_iota(jnp.int32, (experts, experts), 0)
+    col = lax.broadcasted_iota(jnp.int32, (experts, experts), 1)
+    mates = row // local_experts == col // local_experts
+    below = jnp.where(mates & (row < col), 1.0, 0.0).astype(BF16)
+    ahead = jnp.where(mates & (row % local_experts < plan.ahead), 1.0, 0.0).astype(BF16)
+    offsets = contract(counts.astype(BF16), below, ((1,), (0,)))[0:1]
+    aheads = contract(counts.astype(BF16), ahead, ((1,), (0,)))[0:1]
+    slot_lane = lax.broadcasted_iota(jnp.int32, code_ref.shape, 1)
+    code = jnp.zeros(code_ref.shape, jnp.int32)
+    owner_lane = lax.broadcasted_iota(jnp.int32, (tokens, owners), 1)
+    local_lane = lax.broadcasted_iota(jnp.int32, (tokens, meta_ref.shape[1]), 1)
+    parcel_counts = 0.0
+    for j in range(2):
+        expert = ids[:, j:j + 1]
+        owner = expert // local_experts
+        local = expert % local_experts
+        place = jnp.sum((earlier + offsets) * chosen[j], axis=1, keepdims=True).astype(jnp.int32)
+        front = jnp.sum(aheads * chosen[j], axis=1, keepdims=True).astype(jnp.int32)
+        back = jnp.where(
+            (local < plan.ahead) & (place < plan.back[0]),
+            place,
+            plan.back[0] + place - jnp.minimum(front, plan.back[0]),
+        )
+        for lane, value in ((j, owner), (2 + j, place), (4 + j, back)):
+            code = jnp.where(slot_lane == lane, value, code)
+        parcel_counts = parcel_counts + contract(
+            (owner == owner_lane).astype(F32).astype(BF16),
+            (local == local_lane).astype(F32).astype(BF16),
+            ((0,), (0,)),
+        )
+    code_ref[...] = code
+    total = jnp.sum(parcel_counts, axis=1, keepdims=True)
+    lane = lax.broadcasted_iota(jnp.int32, meta_ref.shape, 1)
+    front = jnp.sum(jnp.where(lane < plan.ahead, parcel_counts, 0.0), axis=1, keepdims=True)
+    over = (total > sum(plan.out[:2])) | (
+        total - jnp.minimum(front, plan.back[0]) > plan.back[1]
+    )
+    flag = jnp.max(jnp.where(over, 1.0, 0.0), axis=0, keepdims=True)
+    meta_ref[...] = jnp.where(lane == local_experts, flag, parcel_counts)
+
+
+def route(ids, owners, local_experts, plan):
+    return pl.pallas_call(
+        functools.partial(route_kernel, local_experts, plan),
+        name="route",
+        out_shape=[
+            jax.ShapeDtypeStruct((ids.shape[0], 128), jnp.int32),
+            jax.ShapeDtypeStruct((owners, 128), F32),
+        ],
+        compiler_params=params(),
+    )(ids)
+
+
+class Plan:
+    def __init__(self, local_experts):
+        dense = local_experts * CAP
+        self.ahead = local_experts // 2
+        first = self.ahead * CAP
+        self.out = (first, first // 2, dense - first - first // 2)
+        self.back = (first // 2, first, dense - first - first // 2)
+
+
+def in_round(place, bounds, k, owner):
+    low = sum(bounds[:k])
+    inside = (place >= low) & (place < low + bounds[k])
+    return jnp.where(inside, owner * bounds[k] + place - low, -1)
+
+
+def one_hot(column, width):
+    lanes = lax.broadcasted_iota(jnp.int32, (column.shape[0], width), 1)
+    return jnp.where(column == lanes, 1.0, 0.0).astype(BF16)
+
+
+def pack_kernel(
+    plan, local_experts, residual_ref, piece_ref, gain_ref, code_ref, stream_ref, meta_ref, flag_ref, *out_refs
+):
+    parts, rows = piece_ref.shape[0], residual_ref.shape[0]
+    normed = jnp.concatenate([piece_ref[p, :rows, :] for p in range(parts)], axis=1)
+    tails = [piece_ref[p, rows:, :meta_ref.shape[2]].astype(F32) for p in range(parts)]
+    over = 0.0
+    for p, tail in enumerate(tails):
+        meta_ref[p] = tail.astype(jnp.int32)
+        lane = lax.broadcasted_iota(jnp.int32, tail.shape, 1)
+        over = jnp.maximum(over, jnp.max(jnp.where(lane == local_experts, tail, 0.0)))
+    flag = (over > 0.5).astype(jnp.int32)
+    flag_ref[0] = flag
+    stream = (residual_ref[...].astype(F32) + normed.astype(F32)).astype(BF16)
+    stream_ref[...] = stream
+    wide = stream.astype(F32)
+    scale = lax.rsqrt(jnp.mean(wide * wide, axis=-1, keepdims=True) + EPS)
+    ffn_in = (wide * scale * gain_ref[...]).astype(BF16)
+    code = code_ref[...]
+
+    def fill(k):
+        owners, rows, width = out_refs[k].shape
+        spread = sum(
+            one_hot(
+                in_round(code[:, 2 + j:3 + j], plan.out, k, code[:, j:j + 1]), owners * rows
+            )
+            for j in range(2)
+        )
+        packed = contract(spread, ffn_in, ((0,), (0,))).astype(BF16)
+        out_refs[k][...] = packed.reshape(owners, rows, width)
+
+    fill(0)
+    fill(1)
+
+    @pl.when(flag > 0)
+    def _():
+        fill(2)
+
+
+VMEM = pl.BlockSpec(memory_space=pltpu.VMEM)
+SMEM = pl.BlockSpec(memory_space=pltpu.SMEM)
+
+
+def pack(residual, pieces, gain, code, local_experts, plan):
+    tokens, width = residual.shape
+    parts, rows, _ = pieces.shape
+    blocks = rows - tokens
+    owners = parts * blocks
+    out = pl.pallas_call(
+        functools.partial(pack_kernel, plan, local_experts),
+        name="pack",
+        in_specs=[VMEM] * 4,
+        out_specs=[VMEM, VMEM, SMEM] + [VMEM] * 3,
+        out_shape=[
+            jax.ShapeDtypeStruct((tokens, width), BF16),
+            jax.ShapeDtypeStruct((parts, blocks, 128), jnp.int32),
+            jax.ShapeDtypeStruct((1,), jnp.int32),
+        ]
+        + [jax.ShapeDtypeStruct((owners, rows, width), BF16) for rows in plan.out],
+        compiler_params=params(),
+    )(residual, pieces, gain, code)
+    meta = jnp.swapaxes(out[1], 0, 1).reshape(owners, 128)
+    return out[0], meta, out[2], out[3:]
+
+
+def batch_columns(meta, expert, local_experts, plan):
+    owners = meta.shape[0]
+    counts = jnp.where(
+        lax.broadcasted_iota(jnp.int32, meta.shape, 1) < local_experts, meta, 0
+    ).astype(F32)
+    lanes = counts.shape[1]
+    row = lax.broadcasted_iota(jnp.int32, (lanes, lanes), 0)
+    col = lax.broadcasted_iota(jnp.int32, (lanes, lanes), 1)
+    below = jnp.where(row < col, 1.0, 0.0).astype(BF16)
+    offsets = contract(counts.astype(BF16), below, ((1,), (0,)))
+    batch = owners * CAP
+    source_row = lax.broadcasted_iota(jnp.int32, (batch, owners), 0) // CAP
+    source_col = lax.broadcasted_iota(jnp.int32, (batch, owners), 1)
+    expand = jnp.where(source_row == source_col, 1.0, 0.0).astype(BF16)
+    lane = lax.broadcasted_iota(jnp.int32, (batch, lanes), 1)
+
+    def column(values, picked):
+        wide = contract(expand, values.astype(BF16), ((1,), (0,)))
+        return jnp.sum(jnp.where(picked, wide, 0.0), axis=1, keepdims=True).astype(jnp.int32)
+
+    count = column(counts, lane == expert)
+    offset = column(offsets, lane == expert)
+    front = column(counts, lane < plan.ahead)
+    index = lax.broadcasted_iota(jnp.int32, (batch, 1), 0)
+    rank = index % CAP
+    valid = rank < count
+    place = offset + rank
+    back = jnp.where(
+        (expert < plan.ahead) & (place < plan.back[0]),
+        place,
+        plan.back[0] + place - jnp.minimum(front, plan.back[0]),
+    )
+    return index // CAP, jnp.where(valid, place, -1), jnp.where(valid, back, -1)
+
+
+def expert_kernel(
+    first, taken, given, has_base, local_experts, plan, flag_ref, meta_ref, *refs
+):
+    x_refs, refs = refs[:len(taken)], refs[len(taken):]
+    gate_ref, up_ref, down_ref = refs[:3]
+    base_ref = refs[3] if has_base else None
+    refs = refs[3 + has_base:]
+    out_refs, (batch_ref, acc_ref, done_ref) = refs[:len(given)], refs[len(given):]
+    e = pl.program_id(0)
+    f = pl.program_id(1)
+    last_f = pl.num_programs(1) - 1
+    batch = batch_ref.shape[0]
+    meta = meta_ref[...]
+
+    @pl.when(f == 0)
+    def _():
+        source, place, _ = batch_columns(meta, first + e, local_experts, plan)
+
+        def rows_of(i, k):
+            owners, rows, width = x_refs[i].shape
+            spread = one_hot(in_round(place, plan.out, k, source), owners * rows)
+            return contract(spread, x_refs[i][...].reshape(owners * rows, width), ((1,), (0,)))
+
+        total = 0.0
+        for i, k in enumerate(taken):
+            if k < 2:
+                total = total + rows_of(i, k)
+        batch_ref[...] = total.astype(BF16)
+        for i, k in enumerate(taken):
+            if k == 2:
+
+                @pl.when(flag_ref[0] > 0)
+                def _():
+                    batch_ref[...] = batch_ref[...] + rows_of(i, k).astype(BF16)
+
+    x = batch_ref[...]
+    gate = contract(x, gate_ref[...], ((1,), (0,)))
+    upward = contract(x, up_ref[...], ((1,), (0,)))
+    hidden = (gate / (1.0 + jnp.exp(-gate)) * upward).astype(BF16)
+    part = contract(hidden, down_ref[...], ((1,), (0,)))
+
+    @pl.when(f == 0)
+    def _():
+        acc_ref[...] = part
+
+    @pl.when((f > 0) & (f < last_f))
+    def _():
+        acc_ref[...] = acc_ref[...] + part
+
+    @pl.when(f == last_f)
+    def _():
+        done_ref[e] = (acc_ref[...] + part).astype(BF16)
+
+    @pl.when((e == pl.num_programs(0) - 1) & (f == last_f))
+    def _():
+        count = done_ref.shape[0]
+        columns = [batch_columns(meta, first + i, local_experts, plan) for i in range(count)]
+        source = jnp.concatenate([c[0] for c in columns], axis=0)
+        back = jnp.concatenate([c[2] for c in columns], axis=0)
+        done = done_ref[...].reshape(count * batch, done_ref.shape[2])
+
+        def put(i, k):
+            owners, rows, width = out_refs[i].shape
+            spread = one_hot(in_round(back, plan.back, k, source), owners * rows)
+            rows_out = contract(spread, done, ((0,), (0,)))
+            if has_base and k == 1:
+                rows_out = rows_out + base_ref[...].reshape(owners * rows, width).astype(F32)
+            out_refs[i][...] = rows_out.astype(BF16).reshape(owners, rows, width)
+
+        for i, k in enumerate(given):
+            if k < 2:
+                put(i, k)
+            else:
+
+                @pl.when(flag_ref[0] > 0)
+                def _():
+                    put(i, k)
+
+
+def serve_experts(flag, meta, received, weights, base, first, taken, given, plan):
+    w_gate, w_up, w_down = weights
+    local_experts, width, hidden = w_gate.shape
+    owners = meta.shape[0]
+    count = plan.ahead
+    split = 2
+    step = hidden // split
+
+    def whole(x):
+        return pl.BlockSpec(x.shape, lambda e, f: (0,) * len(x.shape))
+
+    in_spec = pl.BlockSpec((None, width, step), lambda e, f: (first + e, 0, f))
+    extra = [] if base is None else [base]
+    outs = [jax.ShapeDtypeStruct((owners, plan.back[k], width), BF16) for k in given]
+    batch = owners * CAP
+    return pl.pallas_call(
+        functools.partial(
+            expert_kernel, first, taken, given, base is not None, local_experts, plan
+        ),
+        grid=(count, split),
+        in_specs=[SMEM, whole(meta)]
+        + [whole(x) for x in received]
+        + [
+            in_spec,
+            in_spec,
+            pl.BlockSpec((None, step, width), lambda e, f: (first + e, f, 0)),
+        ]
+        + [whole(x) for x in extra],
+        out_specs=[whole(x) for x in outs],
+        out_shape=outs,
+        scratch_shapes=[
+            pltpu.VMEM((batch, width), BF16),
+            pltpu.VMEM((batch, width), F32),
+            pltpu.VMEM((count, batch, width), BF16),
+        ],
+        compiler_params=params(),
+    )(flag, meta, *received, w_gate, w_up, w_down, *extra)
+
+
+def combine_kernel(plan, flag_ref, stream_ref, code_ref, gates_ref, *refs):
+    back_refs, out_ref, acc_ref = refs[:3], refs[3], refs[4]
+    code = code_ref[...]
+    gates = gates_ref[...]
+
+    def part(k):
+        owners, rows, width = back_refs[k].shape
+        flat = back_refs[k][...].reshape(owners * rows, width)
+        total = 0.0
+        for j in range(2):
+            spread = one_hot(
+                in_round(code[:, 4 + j:5 + j], plan.back, k, code[:, j:j + 1]), owners * rows
+            )
+            total = total + gates[:, j:j + 1] * contract(spread, flat, ((1,), (0,)))
+        return total
+
+    acc_ref[...] = stream_ref[...].astype(F32) + part(0) + part(1)
+
+    @pl.when(flag_ref[0] > 0)
+    def _():
+        acc_ref[...] = acc_ref[...] + part(2)
+
+    out_ref[...] = acc_ref[...].astype(BF16)
+
+
+def combine(flag, stream, code, gates, backs, plan):
+    return pl.pallas_call(
+        functools.partial(combine_kernel, plan),
+        name="combine",
+        in_specs=[SMEM] + [VMEM] * (3 + len(backs)),
+        out_specs=VMEM,
+        out_shape=jax.ShapeDtypeStruct(stream.shape, BF16),
+        scratch_shapes=[pltpu.VMEM(stream.shape, F32)],
+        compiler_params=params(),
+    )(flag, stream, code, gates, *backs)
+
+
+def everywhere(x):
+    return lax.all_to_all(x, ("ctx", "head"), split_axis=0, concat_axis=0, tiled=True)
+
+
+def everywhere_if(flag, x):
+    return lax.cond(flag[0] > 0, everywhere, lambda y: y, x)
 
 
 def body(
@@ -329,22 +700,53 @@
     head_count = lax.axis_size("head")
     owners = ctx_count * head_count
     local_experts = w_gate.shape[0]
+    compact = local_experts * CAP % (4 * GROUP_ROWS) == 0
+    if compact:
+        plan = Plan(local_experts)
+        code, meta_out = route(expert_ids, owners, local_experts, plan)
+        meta = everywhere(meta_out.reshape(owners, 1, -1)).reshape(owners, -1)
+        flag = jnp.max(meta[:, local_experts])[None]
+    route_row = mem_route.reshape(1, length)
+    route_col = mem_route.reshape(length, 1)
+
+    compact = local_experts * CAP % (4 * GROUP_ROWS) == 0
+    if compact:
+        plan = Plan(local_experts)
+        code, counts = route(expert_ids, owners, local_experts, plan)
+        tail = jnp.pad(counts.reshape(ctx_count, head_count, HD), ((0, 0), (0, -head_count % 8), (0, 0)))
+    else:
+        tail = jnp.zeros((ctx_count, head_count, HD), F32)
+    tail_rows = tail.shape[1]
+    states = block_states(keys, values, route_row, tail, ctx_count)
+    pieces = lax.all_to_all(states, "ctx", split_axis=0, concat_axis=0, tiled=True)
+    before = exclusive_prefix(pieces, tail_rows)
+    carried = lax.all_to_all(before, "ctx", split_axis=0, concat_axis=0, tiled=True).reshape(-1, HD)
+    local = local_attention(queries, keys, values, route_row, route_col)
+    normed = mix_and_norm(
+        queries, carried, local, route_col, head_gain[None], pieces[:, -tail_rows:], head_count
+    )
+    by_token = lax.all_to_all(normed, "head", split_axis=0, concat_axis=0, tiled=True)
+
+    if compact:
+        weights = (w_gate, w_up, w_down)
+        stream, meta, flag, parcels = pack(
+            residual_in, by_token, ffn_gain[None], code, local_experts, plan
+        )
+        received = [everywhere(parcels[0]), everywhere(parcels[1])]
+        back_0, base = serve_experts(flag, meta, received[:1], weights, None, 0, (0,), (0, 1), plan)
+        received.append(everywhere_if(flag, parcels[2]))
+        back_0 = everywhere(back_0)
+        back_1, back_2 = serve_experts(
+            flag, meta, received, weights, base, plan.ahead, (0, 1, 2), (1, 2), plan
+        )
+        back_2 = everywhere_if(flag, back_2)
+        back_1 = everywhere(back_1)
+        backs = [back_0, back_1, back_2]
+        return combine(flag, stream, code, expert_gates, backs, plan)
+
     pairs = local_experts // PAIR
     chunks = 2 if pairs % 2 == 0 else 1
-    route_row = mem_route.reshape(1, length)
-    route_col = mem_route.reshape(length, 1)
-
-    states = block_states(keys, values, route_row)
-    pieces = lax.all_to_all(states, "ctx", split_axis=0, concat_axis=0, tiled=True)
-    before = exclusive_prefix(pieces.reshape(ctx_count, -1, HD))
-    carried = lax.all_to_all(
-        before.reshape(states.shape), "ctx", split_axis=0, concat_axis=0, tiled=True
-    )
-    local = local_attention(queries, keys, values, route_row, route_col)
-    normed = mix_and_norm(queries, carried, local, route_col, head_gain[None], head_count)
-    by_token = lax.all_to_all(normed, "head", split_axis=0, concat_axis=0, tiled=True)
-
-    stream, parcels = pack(
+    stream, parcels = pack_dense(
         residual_in, by_token, ffn_gain[None], expert_ids, chunks, owners, local_experts
     )
     backs = []
@@ -352,11 +754,11 @@
         received = lax.all_to_all(
             parcels[c], ("ctx", "head"), split_axis=0, concat_axis=0, tiled=True
         )
-        served = serve_experts(received, w_gate, w_up, w_down, c)
+        served = serve_dense(received, w_gate, w_up, w_down, c)
         backs.append(
             lax.all_to_all(served, ("ctx", "head"), split_axis=0, concat_axis=0, tiled=True)
         )
-    return combine(stream, expert_ids, expert_gates, backs, local_experts)
+    return combine_dense(stream, expert_ids, expert_gates, backs, local_experts)
 
 
 def solution(mesh):

time: 298 us -> 280 us (0.940)
  waiting for transfers between devices: 133 us -> 57.3 us
  blocking collectives: 74.2 us -> 124 us
  Pallas kernels: 63.3 us -> 74.6 us
  starting transfers between devices: 19.1 us -> 10.9 us
  local copies, waits for them, and re-layouts: 7.09 us -> 10.9 us
    all_to_all x5 -> x3, waiting for transfers between devices: 133 us -> 57.3 us  [the longest x2 53 us: everywhere(): lax.all_to_all(x, ('ctx', 'head'), split_axis=0, concat_axis=0, tiled=True)]
    all_to_all x1 -> x3, blocking collectives: 52.1 us -> 101 us  [the longest x2 81.9 us: everywhere(): lax.all_to_all(x, ('ctx', 'head'), split_axis=0, concat_axis=0, tiled=True)]
    pallas_call x6 -> x7, Pallas kernels: 50.5 us -> 61.8 us  [the longest x2 41.3 us: serve_experts(): pl.pallas_call(functools.partial(expert_kernel, first, taken, given, base...]
    all_to_all x5 -> x3, starting transfers between devices: 19.1 us -> 10.9 us  [the longest x2 7.39 us: everywhere(): lax.all_to_all(x, ('ctx', 'head'), split_axis=0, concat_axis=0, tiled=True)]
  transfers between devices with their start and end apart: 5 -> 3, of which waited for: 5 -> 3; matrix products, arithmetic and copies ran while one was open for 1% -> 1% of each run, Pallas kernels for 13% -> 10%
where the time goes in v1:
time: 280 us; the launch traced here: 279 us
  blocking collectives  124 us (44%)
  Pallas kernels  74.6 us (27%)
  waiting for transfers between devices  57.3 us (20%)
  local copies, waits for them, and re-layouts  10.9 us (4%)
  starting transfers between devices  10.9 us (4%)
    all_to_all x2, blocking collectives, everywhere(): lax.all_to_all(x, ('ctx', 'head'), split_axis=0, concat_axis=0, tiled=True)  81.9 us
    all_to_all x2, waiting for transfers between devices, everywhere(): lax.all_to_all(x, ('ctx', 'head'), split_axis=0, concat_axis=0, tiled=True)  53 us
    pallas_call x2, Pallas kernels, serve_experts(): pl.pallas_call(functools.partial(expert_kernel, first, taken, given, base...  41.3 us
    all_to_all x1, blocking collectives, body(): lax.all_to_all(states, 'ctx', split_axis=0, concat_axis=0, tiled=True)  23.2 us
    all_to_all x1, blocking collectives, body(): lax.all_to_all(normed, 'head', split_axis=0, concat_axis=0, tiled=True)  19.1 us
    all_to_all x2, starting transfers between devices, everywhere(): lax.all_to_all(x, ('ctx', 'head'), split_axis=0, concat_axis=0, tiled=True)  7.39 us
    pallas_call x1, Pallas kernels, local_attention(): pl.pallas_call(functools.partial(local_kernel, rows), name='local_attenti...  7.19 us
    unnamed x16, local copies, waits for them, and re-layouts  6.61 us
  transfers between devices with their start and end apart: 3, of which 3 were waited for; matrix products, arithmetic and copies ran while one was open for 1% of the time, Pallas kernels for 10%

profile of v1, /device:TPU:0, one launch (start us, length us, event | category | flops | bytes accessed | tf_op | source)
XLA Modules:
  0.0 278.5 jit_solution(3996011068805865316)
XLA Ops:
  0.0 1.5 copy.16.ids_ref
  1.5 2.6 route.1
  4.1 1.3 pad.4.meta_ref
  5.4 4.4 %block_states.1 = bf16[8,264,128]{2,1,0:T(8,128)(2,1)} custom-call(bf16[1024,512]{1,0:T(8,128)(2,1)} %key_ref.3, bf16[1024,512]{1,0:T(8,128)(2,1)} %value_ref.3, s32[1,1024]{1,0:T(1,128)} %bitcast.12, f32[8,8,128]{2,1,0:T(8,128)} %pad.4.meta_ref), custom_call_target="tpu_custom_call" | custom-call | tf_op jit(solution)/shard_map/block_states/pallas_call | solution.py:56
  9.8 23.2 %all_to_all.45.piece_ref = bf16[8,264,128]{2,1,0:T(8,128)(2,1)} all-to-all(bf16[8,264,128]{2,1,0:T(8,128)(2,1)} %block_states.1), channel_id=1, replica_groups=mesh['ctx'=8,'head'=4] {'ctx'}, dimensions={0} | all-to-all | bytes 1081344 | tf_op jit(solution)/shard_map/all_to_all | solution.py:721
  33.0 1.9 exclusive_prefix.1
  35.0 3.5 %all-to-all-start.3 = ((bf16[8,256,128]{2,1,0:T(8,128)(2,1)}), bf16[8,256,128]{2,1,0:T(8,128)(2,1)S(1)}, u32[]{:S(2)}, u32[]{:S(2)}) async-start(bf16[8,256,128]{2,1,0:T(8,128)(2,1)} %exclusive_prefix.1), calls=%async_computation.3 | async-start | bytes 1048576 | tf_op jit(solution)/shard_map/all_to_all | solution.py:723
  39.5 7.2 %local_attention.1.local_ref = f32[1024,512]{1,0:T(8,128)} custom-call(bf16[1024,512]{1,0:T(8,128)(2,1)} %query_ref.3, bf16[1024,512]{1,0:T(8,128)(2,1)} %key_ref.3, bf16[1024,512]{1,0:T(8,128)(2,1)} %value_ref.3, s32[1,1024]{1,0:T(1,128)} %bitcast.13, s32[1024,1]{1,0:T(8,128)} %copy.17.route_col_ref), custom_call_target="tpu_custom_call" | custom-call | tf_op jit(solution)/shard_map/local_attention/pallas_call | solution.py:118
  46.7 1.3 slice.4.meta_ref
  48.0 4.3 %all-to-all-done.3 = bf16[8,256,128]{2,1,0:T(8,128)(2,1)S(1)} async-done(((bf16[8,256,128]{2,1,0:T(8,128)(2,1)}), bf16[8,256,128]{2,1,0:T(8,128)(2,1)S(1)}, u32[]{:S(2)}, u32[]{:S(2)}) %all-to-all-start.3) | async-done | bytes 524320 | tf_op jit(solution)/shard_map/all_to_all | solution.py:723
  53.1 5.6 %mix_and_norm.1 = bf16[4,264,512]{2,1,0:T(8,128)(2,1)} custom-call(bf16[1024,512]{1,0:T(8,128)(2,1)} %query_ref.3, bf16[2048,128]{1,0:T(8,128)(2,1)} %bitcast.9, f32[1024,512]{1,0:T(8,128)} %local_attention.1.local_ref, s32[1024,1]{1,0:T(8,128)} %copy.17.route_col_ref, f32[1,512]{1,0:T(1,128)} %bitcast.18, bf16[8,8,128]{2,1,0:T(8,128)(2,1)} %slice.4.meta_ref), custom_call_target="tpu_custom_call" | custom-call | tf_op jit(solution)/shard_map/mix_and_norm/pallas_call | solution.py:159
  58.7 19.1 %all_to_all.46.piece_ref = bf16[4,264,512]{2,1,0:T(8,128)(2,1)} all-to-all(bf16[4,264,512]{2,1,0:T(8,128)(2,1)} %mix_and_norm.1), channel_id=1, replica_groups=mesh['ctx'=8,'head'=4] {'head'}, dimensions={0} | all-to-all | bytes 2162688 | tf_op jit(solution)/shard_map/all_to_all | solution.py:728
  77.8 5.2 %pack.1 = (bf16[256,2048]{1,0:T(8,128)(2,1)}, s32[4,8,128]{2,1,0:T(8,128)}, s32[1]{0:T(128)}, bf16[32,16,2048]{2,1,0:T(8,128)(2,1)}, bf16[32,8,2048]{2,1,0:T(8,128)(2,1)}, /*index=5*/bf16[32,8,2048]{2,1,0:T(8,128)(2,1)S(1)}) custom-call(bf16[256,2048]{1,0:T(8,128)(2,1)} %residual_ref.1, bf16[4,264,512]{2,1,0:T(8,128)(2,1)} %all_to_all.46.piece_ref, ...), custom_call_target="tpu_custom_call" | custom-call | tf_op jit(solution)/shard_map/pack/pallas_call | solution.py:469
  83.7 52.1 %all_to_all.47.refs_0_ = bf16[32,16,2048]{2,1,0:T(8,128)(2,1)} all-to-all(bf16[32,16,2048]{2,1,0:T(8,128)(2,1)} %get-tuple-element.32), channel_id=1, replica_groups=mesh['ctx'=8,'head'=4] {'ctx','head'}, dimensions={0} | all-to-all | bytes 4194304 | tf_op jit(solution)/shard_map/all_to_all | solution.py:677
  135.9 3.8 %all-to-all-start.7 = ((bf16[32,8,2048]{2,1,0:T(8,128)(2,1)}), bf16[32,8,2048]{2,1,0:T(8,128)(2,1)S(1)}, u32[]{:S(2)}, u32[]{:S(2)}) async-start(bf16[32,8,2048]{2,1,0:T(8,128)(2,1)} %get-tuple-element.34), calls=%async_computation.7 | async-start | bytes 2097152 | tf_op jit(solution)/shard_map/all_to_all | solution.py:677
  140.2 20.3 %shard_map.118 = (bf16[32,8,2048]{2,1,0:T(8,128)(2,1)}, bf16[32,16,2048]{2,1,0:T(8,128)(2,1)}) custom-call(s32[1]{0:T(128)} %get-tuple-element.29.flag_ref, s32[32,128]{1,0:T(8,128)} %bitcast.10, bf16[32,16,2048]{2,1,0:T(8,128)(2,1)} %all_to_all.47.refs_0_, bf16[8,2048,512]{2,1,0:T(8,128)(2,1)} %refs_3_.3, bf16[8,2048,512]{2,1,0:T(8,128)(2,1)} %refs_4_.1, ...), custom_call_target="tpu_custom_call" | custom-call | tf_op jit(solution)/shard_map/pallas_call | solution.py:615
  160.6 5.1 %all-to-all-done.7.refs_1_ = bf16[32,8,2048]{2,1,0:T(8,128)(2,1)S(1)} async-done(((bf16[32,8,2048]{2,1,0:T(8,128)(2,1)}), bf16[32,8,2048]{2,1,0:T(8,128)(2,1)S(1)}, u32[]{:S(2)}, u32[]{:S(2)}) %all-to-all-start.7) | async-done | bytes 1048608 | tf_op jit(solution)/shard_map/all_to_all | solution.py:677
  166.6 21.0 %shard_map.119 = (bf16[32,16,2048]{2,1,0:T(8,128)(2,1)}, bf16[32,8,2048]{2,1,0:T(8,128)(2,1)S(1)}) custom-call(s32[1]{0:T(128)} %get-tuple-element.29.flag_ref, s32[32,128]{1,0:T(8,128)} %bitcast.11, bf16[32,16,2048]{2,1,0:T(8,128)(2,1)} %all_to_all.47.refs_0_, bf16[32,8,2048]{2,1,0:T(8,128)(2,1)} %copy-done.1, ...), custom_call_target="tpu_custom_call" | custom-call | tf_op jit(solution)/shard_map/pallas_call | solution.py:615
  187.6 1.2 copy-done.3
  188.8 29.7 %all_to_all.48.refs_0_ = bf16[32,8,2048]{2,1,0:T(8,128)(2,1)} all-to-all(bf16[32,8,2048]{2,1,0:T(8,128)(2,1)S(1)} %copy-done.3), channel_id=1, replica_groups=mesh['ctx'=8,'head'=4] {'ctx','head'}, dimensions={0} | all-to-all | bytes 2097152 | tf_op jit(solution)/shard_map/all_to_all | solution.py:677
  218.6 3.6 %all-to-all-start.8 = ((bf16[32,16,2048]{2,1,0:T(8,128)(2,1)}), bf16[32,16,2048]{2,1,0:T(8,128)(2,1)S(1)}, u32[]{:S(2)}, u32[]{:S(2)}) async-start(bf16[32,16,2048]{2,1,0:T(8,128)(2,1)} %get-tuple-element.37), calls=%async_computation.8 | async-start | bytes 4194304 | tf_op jit(solution)/shard_map/all_to_all | solution.py:677
  223.0 47.9 %all-to-all-done.8.refs_1_ = bf16[32,16,2048]{2,1,0:T(8,128)(2,1)S(1)} async-done(((bf16[32,16,2048]{2,1,0:T(8,128)(2,1)}), bf16[32,16,2048]{2,1,0:T(8,128)(2,1)S(1)}, u32[]{:S(2)}, u32[]{:S(2)}) %all-to-all-start.8) | async-done | bytes 2097184 | tf_op jit(solution)/shard_map/all_to_all | solution.py:677
  270.9 1.3 copy-done
  272.3 6.3 %combine.1 = bf16[256,2048]{1,0:T(8,128)(2,1)} custom-call(s32[1]{0:T(128)} %get-tuple-element.29.flag_ref, bf16[256,2048]{1,0:T(8,128)(2,1)} %get-tuple-element.30.stream_ref, s32[256,128]{1,0:T(8,128)} %get-tuple-element.28.code_ref, f32[256,2]{1,0:T(8,128)} %copy.20.gates_ref, bf16[32,8,2048]{2,1,0:T(8,128)(2,1)} %all_to_all.48.refs_0_, ...), custom_call_target="tpu_custom_call" | custom-call | tf_op jit(solution)/shard_map/combine/pallas_call | solution.py:665
  (17 shorter events, 4.2 us)
Async XLA Ops:
  9.8 28.6 %copy-start.4 = (s32[1024]{0:T(1024)S(1)}, s32[1024]{0:T(1024)}, u32[]{:S(2)}) copy-start(s32[1024]{0:T(1024)} %param.19) | copy-start | bytes 12292
  35.0 17.4 %all-to-all-start.3 = ((bf16[8,256,128]{2,1,0:T(8,128)(2,1)}), bf16[8,256,128]{2,1,0:T(8,128)(2,1)S(1)}, u32[]{:S(2)}, u32[]{:S(2)}) async-start(bf16[8,256,128]{2,1,0:T(8,128)(2,1)} %exclusive_prefix.1), calls=%async_computation.3 | async-start | bytes 1048576 | tf_op jit(solution)/shard_map/all_to_all | solution.py:723
  52.3 0.8 copy-start.2
  135.9 3.8 %copy-start.5 = (s32[4,8,128]{2,1,0:T(8,128)S(1)}, s32[4,8,128]{2,1,0:T(8,128)}, u32[]{:S(2)}) copy-start(s32[4,8,128]{2,1,0:T(8,128)} %get-tuple-element.31) | copy-start | bytes 49156
  135.9 29.8 %all-to-all-start.7 = ((bf16[32,8,2048]{2,1,0:T(8,128)(2,1)}), bf16[32,8,2048]{2,1,0:T(8,128)(2,1)S(1)}, u32[]{:S(2)}, u32[]{:S(2)}) async-start(bf16[32,8,2048]{2,1,0:T(8,128)(2,1)} %get-tuple-element.34), calls=%async_computation.7 | async-start | bytes 2097152 | tf_op jit(solution)/shard_map/all_to_all | solution.py:677
  165.7 1.0 copy-start.1
  187.6 1.2 copy-start.3
  218.6 3.6 %copy-start.6 = (f32[256,2]{0,1:T(2,128)S(1)}, f32[256,2]{0,1:T(2,128)}, u32[]{:S(2)}) copy-start(f32[256,2]{0,1:T(2,128)} %param.24) | copy-start | bytes 6148
  218.6 52.4 %all-to-all-start.8 = ((bf16[32,16,2048]{2,1,0:T(8,128)(2,1)}), bf16[32,16,2048]{2,1,0:T(8,128)(2,1)S(1)}, u32[]{:S(2)}, u32[]{:S(2)}) async-start(bf16[32,16,2048]{2,1,0:T(8,128)(2,1)} %get-tuple-element.37), calls=%async_computation.8 | async-start | bytes 4194304 | tf_op jit(solution)/shard_map/all_to_all | solution.py:677
  270.9 1.3 copy-start

commit v2 on v0

--- a/solution.py
+++ b/solution.py
@@ -6,6 +6,7 @@
 from jax.experimental import pallas as pl
 from jax.experimental.pallas import tpu as pltpu
 from jax.sharding import PartitionSpec as P
+
 
 HD = 128
 M = 4
@@ -171,7 +172,7 @@
     return slots
 
 
-def pack_kernel(chunks, local_experts, residual_ref, piece_ref, gain_ref, ids_ref, *refs):
+def pack_dense_kernel(chunks, local_experts, residual_ref, piece_ref, gain_ref, ids_ref, *refs):
     stream_ref, out_refs = refs[0], refs[1:1 + chunks]
     parts, rows, _ = piece_ref.shape
     owners, groups, _, width = out_refs[0].shape
@@ -193,20 +194,20 @@
             out_refs[c][:, g] = packed.reshape(owners, GROUP_ROWS, width)
 
 
-def pack(residual, pieces, gain, ids, chunks, owners, local_experts):
+def pack_dense(residual, pieces, gain, ids, chunks, owners, local_experts):
     tokens, width = residual.shape
     groups = local_experts // PAIR // chunks
     parcel = jax.ShapeDtypeStruct((owners, groups, GROUP_ROWS, width), BF16)
     out = pl.pallas_call(
-        functools.partial(pack_kernel, chunks, local_experts),
-        name="pack",
+        functools.partial(pack_dense_kernel, chunks, local_experts),
+        name="pack_dense",
         out_shape=[jax.ShapeDtypeStruct((tokens, width), BF16)] + [parcel] * chunks,
         compiler_params=params(),
     )(residual, pieces, gain, ids)
     return out[0], out[1:]
 
 
-def expert_kernel(x_ref, gate_ref, up_ref, down_ref, out_ref, acc_ref):
+def expert_dense_kernel(x_ref, gate_ref, up_ref, down_ref, out_ref, acc_ref):
     e = pl.program_id(1)
     f = pl.program_id(2)
     owners, rows, width = x_ref.shape
@@ -233,7 +234,7 @@
         out_ref[...] = acc_ref[...].astype(BF16).reshape(owners, rows, width)
 
 
-def serve_experts(received, w_gate, w_up, w_down, chunk):
+def serve_dense(received, w_gate, w_up, w_down, chunk):
     owners, groups, rows, width = received.shape
     hidden = w_gate.shape[2]
     split = 2
@@ -242,8 +243,7 @@
     token_spec = pl.BlockSpec((owners, None, rows, width), lambda g, e, f: (0, g, 0, 0))
     in_spec = pl.BlockSpec((None, width, step), lambda g, e, f: (first + g * PAIR + e, 0, f))
     return pl.pallas_call(
-        expert_kernel,
-        name=f"experts_{chunk}",
+        expert_dense_kernel,
         grid=(groups, PAIR, split),
         in_specs=[
             token_spec,
@@ -258,9 +258,8 @@
     )(received, w_gate, w_up, w_down)
 
 
-def combine_kernel(chunks, local_experts, stream_ref, ids_ref, gates_ref, *refs):
+def combine_dense_kernel(chunks, local_experts, stream_ref, ids_ref, gates_ref, *refs):
     back_refs, out_ref, first_ref, second_ref = refs[:chunks], refs[chunks], refs[-2], refs[-1]
-    tokens = stream_ref.shape[0]
     owners, groups, rows, _ = back_refs[0].shape
     span = owners * rows
 
@@ -286,7 +285,7 @@
     out_ref[...] = total.astype(BF16)
 
 
-def combine(stream, ids, gates, backs, local_experts):
+def combine_dense(stream, ids, gates, backs, local_experts):
     tokens, width = stream.shape
     owners, groups, rows, _ = backs[0].shape
     chunks = len(backs)
@@ -294,8 +293,8 @@
     step = min(512, width)
     back_spec = pl.BlockSpec((owners, groups, rows, step), lambda d: (0, 0, 0, d))
     return pl.pallas_call(
-        functools.partial(combine_kernel, chunks, local_experts),
-        name="combine",
+        functools.partial(combine_dense_kernel, chunks, local_experts),
+        name="combine_dense",
         grid=(width // step,),
         in_specs=[
             pl.BlockSpec((tokens, step), lambda d: (0, d)),
@@ -310,7 +309,536 @@
     )(stream, ids, gates, *backs)
 
 
-def body(
+class Plan:
+    def __init__(self, local_experts):
+        dense = local_experts * CAP
+        self.ahead = local_experts // 2
+        first = self.ahead * CAP
+        self.out = (first, first // 2, dense - first - first // 2)
+        self.back = (first // 2, first, dense - first - first // 2)
+
+
+def in_round(place, bounds, k, owner):
+    low = sum(bounds[:k])
+    inside = (place >= low) & (place < low + bounds[k])
+    return jnp.where(inside, owner * bounds[k] + place - low, -1)
+
+
+def one_hot(column, width):
+    lanes = lax.broadcasted_iota(jnp.int32, (column.shape[0], width), 1)
+    return jnp.where(column == lanes, 1.0, 0.0).astype(BF16)
+
+
+VMEM = pl.BlockSpec(memory_space=pltpu.VMEM)
+SMEM = pl.BlockSpec(memory_space=pltpu.SMEM)
+
+
+def route_kernel(local_experts, plan, parts, head_ref, *refs):
+    id_refs, (code_ref, meta_ref), spread_refs = refs[:parts], refs[parts:parts + 2], refs[parts + 2:]
+    tokens = id_refs[0].shape[1]
+    contexts = meta_ref.shape[0]
+    owners = contexts * parts
+    experts = owners * local_experts
+    head = head_ref[0]
+    t = lax.broadcasted_iota(jnp.int32, (tokens, tokens), 0)
+    s = lax.broadcasted_iota(jnp.int32, (tokens, tokens), 1)
+    earlier_mask = (t > s).astype(F32).astype(BF16)
+    row = lax.broadcasted_iota(jnp.int32, (experts, experts), 0)
+    col = lax.broadcasted_iota(jnp.int32, (experts, experts), 1)
+    mates = row // local_experts == col // local_experts
+    below = jnp.where(mates & (row < col), 1.0, 0.0).astype(BF16)
+    ahead = jnp.where(mates & (row % local_experts < plan.ahead), 1.0, 0.0).astype(BF16)
+    lanes = lax.broadcasted_iota(jnp.int32, (tokens, experts), 1)
+    owner_lane = lax.broadcasted_iota(jnp.int32, (tokens, owners), 1)
+    local_lane = lax.broadcasted_iota(jnp.int32, (tokens, HD), 1)
+    owner_row = lax.broadcasted_iota(jnp.int32, (contexts, owners), 1)
+    context_row = lax.broadcasted_iota(jnp.int32, (contexts, owners), 0)
+    mine = jnp.where(owner_row == context_row * parts + head, 1.0, 0.0).astype(BF16)
+    lane = lax.broadcasted_iota(jnp.int32, (owners, HD), 1)
+    pair_rows = [ref[...].astype(F32) for ref in id_refs]
+    id_rows = jnp.concatenate(pair_rows + [jnp.zeros((-2 * parts % 8, tokens), F32)] * (2 * parts % 8 > 0), axis=0)
+    id_cols = id_rows.T
+    flags = 0.0
+    metas = []
+    for b in range(parts):
+        ids = [id_cols[:, 2 * b + j:2 * b + j + 1].astype(jnp.int32) for j in range(2)]
+        chosen = [(i == lanes).astype(F32) for i in ids]
+        both = (chosen[0] + chosen[1]).astype(BF16)
+        counts = contract(jnp.ones((8, tokens), BF16), both, ((1,), (0,))).astype(BF16)
+        position = contract(earlier_mask, both, ((1,), (0,))) + contract(counts, below, ((1,), (0,)))[0:1]
+        places = [jnp.sum(position * c, axis=1, keepdims=True) for c in chosen]
+        wide = jnp.concatenate(places + [jnp.zeros((tokens, HD - 2), F32)], axis=1)
+        place_rows = wide.T[0:8]
+        parcel_counts = 0.0
+        for j in range(2):
+            parcel_counts = parcel_counts + contract(
+                (ids[j] // local_experts == owner_lane).astype(F32).astype(BF16),
+                (ids[j] % local_experts == local_lane).astype(F32).astype(BF16),
+                ((0,), (0,)),
+            )
+        if b == 0:
+            aheads = contract(counts, ahead, ((1,), (0,)))[0:1]
+            slot_lane = lax.broadcasted_iota(jnp.int32, code_ref.shape, 1)
+            code = jnp.zeros(code_ref.shape, jnp.int32)
+            for j in range(2):
+                place = places[j].astype(jnp.int32)
+                front = jnp.sum(aheads * chosen[j], axis=1, keepdims=True).astype(jnp.int32)
+                back = jnp.where(
+                    (ids[j] % local_experts < plan.ahead) & (place < plan.back[0]),
+                    place,
+                    plan.back[0] + place - jnp.minimum(front, plan.back[0]),
+                )
+                code = jnp.where(slot_lane == j, ids[j] // local_experts, code)
+                code = jnp.where(slot_lane == 4 + j, back, code)
+            code_ref[...] = code
+        for k, spread_ref in enumerate(spread_refs):
+            slots = spread_ref.shape[1]
+            slot = lax.broadcasted_iota(jnp.int32, (slots, tokens), 0)
+            hit = None
+            for j in range(2):
+                owner = id_rows[2 * b + j:2 * b + j + 1].astype(jnp.int32) // local_experts
+                index = in_round(place_rows[j:j + 1].astype(jnp.int32), plan.out, k, owner)
+                hit = (slot == index) if hit is None else hit | (slot == index)
+            spread_ref[b] = jnp.where(hit, 1.0, 0.0).astype(BF16)
+        total = jnp.sum(parcel_counts, axis=1, keepdims=True)
+        front = jnp.sum(jnp.where(lane < plan.ahead, parcel_counts, 0.0), axis=1, keepdims=True)
+        over = (total > sum(plan.out[:2])) | (
+            total - jnp.minimum(front, plan.back[0]) > plan.back[1]
+        )
+        flags = jnp.maximum(flags, jnp.max(jnp.where(over, 1.0, 0.0), axis=0, keepdims=True))
+        metas.append(contract(mine, parcel_counts.astype(BF16), ((1,), (0,))))
+    meta_lane = lax.broadcasted_iota(jnp.int32, (contexts, HD), 1)
+    meta_ref[...] = jnp.zeros(meta_ref.shape, F32)
+    for b in range(parts):
+        marked = jnp.where(meta_lane == local_experts, flags, metas[b])
+        for c in range(contexts):
+            meta_ref[c, b:b + 1, :] = marked[c:c + 1]
+
+
+def route(head, ids, contexts, local_experts, plan):
+    parts = len(ids)
+    tokens = ids[0].shape[1]
+    owners = contexts * parts
+    return pl.pallas_call(
+        functools.partial(route_kernel, local_experts, plan, parts),
+        name="route",
+        in_specs=[SMEM] + [VMEM] * parts,
+        out_specs=[VMEM] * 5,
+        out_shape=[
+            jax.ShapeDtypeStruct((tokens, HD), jnp.int32),
+            jax.ShapeDtypeStruct((contexts, parts + -parts % 8, HD), F32),
+        ]
+        + [jax.ShapeDtypeStruct((parts, owners * rows, tokens), BF16) for rows in plan.out],
+        compiler_params=params(),
+    )(head, *ids)
+
+
+def prefix_with_counts_kernel(piece_ref, meta_ref, out_ref):
+    ranks, rows, _ = piece_ref.shape
+    total = jnp.zeros(piece_ref.shape[1:], F32)
+    for r in range(ranks):
+        out_ref[r, :rows, :] = total.astype(BF16)
+        out_ref[r, rows:, :] = meta_ref[r].astype(BF16)
+        if r + 1 < ranks:
+            total = total + piece_ref[r].astype(F32)
+
+
+def prefix_with_counts(pieces, meta):
+    ranks, rows, width = pieces.shape
+    return pl.pallas_call(
+        prefix_with_counts_kernel,
+        name="prefix_with_counts",
+        in_specs=[VMEM] * 2,
+        out_specs=VMEM,
+        out_shape=jax.ShapeDtypeStruct((ranks, rows + meta.shape[1], width), BF16),
+        compiler_params=params(),
+    )(pieces, meta)
+
+
+def columns_kernel(parts, head_ref, whole_ref, *out_refs):
+    step = whole_ref.shape[1] // parts
+    for s in range(parts):
+        start = pl.multiple_of((head_ref[0] + s) % parts * step, step)
+        out_refs[s][...] = whole_ref[:, pl.ds(start, step)]
+
+
+def columns_by_turn(head, whole, parts):
+    tokens, width = whole.shape
+    return pl.pallas_call(
+        functools.partial(columns_kernel, parts),
+        name="columns_by_turn",
+        in_specs=[SMEM, VMEM],
+        out_specs=[VMEM] * parts,
+        out_shape=[jax.ShapeDtypeStruct((tokens, width // parts), BF16)] * parts,
+        compiler_params=params(),
+    )(head, whole)
+
+
+def mix_pack_kernel(
+    parts, local_experts, plan, head_ref, query_ref, state_ref, tail_ref, local_ref, route_col_ref, gain_ref, *refs
+):
+    residual_refs, spread_refs = refs[:parts], refs[parts:parts + 3]
+    refs = refs[parts + 3:]
+    meta_ref, flag_ref, parcel_refs, stream_refs = refs[0], refs[1], refs[2:5], refs[5:5 + parts]
+    normed_ref = refs[-1]
+    head = head_ref[0]
+    share, rows, _ = state_ref.shape
+    contexts, tail, _ = tail_ref.shape
+    rows -= tail
+    query = query_ref[...]
+    column = route_col_ref[...]
+    wide = jnp.concatenate(
+        [query * jnp.where(column == m, 2.0, 1.0).astype(BF16) for m in range(M)], axis=1
+    )
+    state = jnp.concatenate([state_ref[i, :rows, :] for i in range(share)], axis=0)
+    mixed = contract(wide, state, ((1,), (0,))) + local_ref[...]
+    scale = lax.rsqrt(jnp.mean(mixed * mixed, axis=-1, keepdims=True) + EPS)
+    normed_ref[...] = (mixed * scale * gain_ref[...]).astype(BF16)
+
+    counts = tail_ref[...].astype(F32)
+    owners = contexts * parts
+    lane = lax.broadcasted_iota(jnp.int32, counts.shape, 2)
+    over = jnp.max(jnp.where(lane == local_experts, counts, 0.0))
+    flag = (over > 0.5).astype(jnp.int32)
+    flag_ref[0] = flag
+
+    @pl.when(pl.program_id(0) == 0)
+    def _():
+        source = lax.broadcasted_iota(jnp.int32, (owners, contexts * tail), 0)
+        given = lax.broadcasted_iota(jnp.int32, (owners, contexts * tail), 1)
+        turn = (head - source % parts + parts) % parts
+        order = jnp.where(given == source // parts * tail + turn, 1.0, 0.0).astype(BF16)
+        flat = counts.reshape(contexts * tail, counts.shape[2]).astype(BF16)
+        meta_ref[...] = contract(order, flat, ((1,), (0,))).astype(jnp.int32)
+
+    tokens = residual_refs[0].shape[0]
+    for s in range(parts):
+        start = pl.multiple_of((head - s + parts) % parts * tokens, tokens)
+        normed = normed_ref[pl.ds(start, tokens), :]
+        stream = (residual_refs[s][...].astype(F32) + normed.astype(F32)).astype(BF16)
+        stream_refs[s][...] = stream
+
+    def fill(k):
+        each = plan.out[k]
+        for s in range(parts):
+            packed = contract(spread_refs[k][s], stream_refs[s][...], ((1,), (0,))).astype(BF16)
+            parcel_refs[k][:, s * each:(s + 1) * each, :] = packed.reshape(owners, each, HD)
+
+    fill(0)
+    fill(1)
+
+    @pl.when(flag > 0)
+    def _():
+        fill(2)
+
+
+def mix_and_pack(head, queries, carried, tail, local, route_col, head_gain, residuals, spreads, local_experts, plan):
+    length, width = queries.shape
+    heads = width // HD
+    contexts, rows, _ = carried.shape
+    share = contexts // heads
+    parts = len(residuals)
+    tokens = length // parts
+    owners = contexts * parts
+    wide = pl.BlockSpec((length, HD), lambda h: (0, h))
+    narrow = pl.BlockSpec((tokens, HD), lambda h: (0, h))
+
+    def whole(x):
+        return pl.BlockSpec(x.shape, lambda h: (0,) * len(x.shape))
+
+    parcels = [jax.ShapeDtypeStruct((owners, parts * r, width), BF16) for r in plan.out]
+    meta = jax.ShapeDtypeStruct((owners, HD), jnp.int32)
+    out = pl.pallas_call(
+        functools.partial(mix_pack_kernel, parts, local_experts, plan),
+        name="mix_and_pack",
+        grid=(heads,),
+        in_specs=[
+            SMEM,
+            wide,
+            pl.BlockSpec((share, rows, HD), lambda h: (h, 0, 0)),
+            pl.BlockSpec((contexts, tail, HD), lambda h: (0, (rows - tail) // tail, 0)),
+            wide,
+            pl.BlockSpec((length, 1), lambda h: (0, 0)),
+            pl.BlockSpec((1, HD), lambda h: (0, h)),
+        ]
+        + [narrow] * parts
+        + [whole(x) for x in spreads],
+        out_specs=[whole(meta), SMEM]
+        + [pl.BlockSpec((owners, x.shape[1], HD), lambda h: (0, 0, h)) for x in parcels]
+        + [narrow] * parts,
+        out_shape=[meta, jax.ShapeDtypeStruct((1,), jnp.int32)]
+        + parcels
+        + [jax.ShapeDtypeStruct((tokens, width), BF16)] * parts,
+        scratch_shapes=[pltpu.VMEM((length, HD), BF16)],
+        compiler_params=params(),
+    )(head, queries, carried, carried, local, route_col, head_gain, *residuals, *spreads)
+    return out[0], out[1], out[2:5], out[5:]
+
+
+def gated(gates, spreads, back):
+    total = 0.0
+    for j, spread in enumerate(spreads):
+        total = total + gates[:, j:j + 1] * contract(spread, back, ((1,), (0,)))
+    return total
+
+
+def choices(code, plan, k, owners):
+    return [
+        one_hot(in_round(code[:, 4 + j:5 + j], plan.back, k, code[:, j:j + 1]), owners * plan.back[k])
+        for j in range(2)
+    ]
+
+
+def combine_ahead_kernel(plan, parts, head_ref, code_ref, gates_ref, back_ref, *refs):
+    stream_refs, (acc_ref, pick_ref) = refs[:parts], refs[parts:]
+    code = code_ref[...]
+    owners, rows, width = back_ref.shape
+    flat = back_ref[...].reshape(owners * rows, width)
+    acc_ref[...] = gated(gates_ref[...], choices(code, plan, 0, owners), flat)
+    step = width // parts
+    for s in range(parts):
+        start = pl.multiple_of((head_ref[0] + s) % parts * step, step)
+        acc_ref[:, pl.ds(start, step)] = acc_ref[:, pl.ds(start, step)] + stream_refs[s][...].astype(F32)
+    for j, spread in enumerate(choices(code, plan, 1, owners)):
+        pick_ref[j] = spread
+
+
+def combine_ahead(head, code, gates, back, streams, plan):
+    owners, _, width = back.shape
+    tokens = code.shape[0]
+    return pl.pallas_call(
+        functools.partial(combine_ahead_kernel, plan, len(streams)),
+        name="combine_ahead",
+        in_specs=[SMEM] + [VMEM] * (3 + len(streams)),
+        out_specs=[VMEM] * 2,
+        out_shape=[
+            jax.ShapeDtypeStruct((tokens, width), F32),
+            jax.ShapeDtypeStruct((2, tokens, owners * plan.back[1]), BF16),
+        ],
+        compiler_params=params(),
+    )(head, code, gates, back, *streams)
+
+
+def combine_kernel(plan, flag_ref, code_ref, gates_ref, acc_ref, pick_ref, back_ref, late_ref, out_ref):
+    code = code_ref[...]
+    gates = gates_ref[...]
+    owners, rows, step = back_ref.shape
+    flat = back_ref[...].reshape(owners * rows, step)
+    total = acc_ref[...] + gated(gates, [pick_ref[0], pick_ref[1]], flat)
+    out_ref[...] = total.astype(BF16)
+
+    @pl.when(flag_ref[0] > 0)
+    def _():
+        late = late_ref[...].reshape(owners * plan.back[2], step)
+        more = gated(gates, choices(code, plan, 2, owners), late)
+        out_ref[...] = (total + more).astype(BF16)
+
+
+def combine(flag, code, gates, acc, picks, back, late, plan):
+    tokens, width = acc.shape
+    owners = back.shape[0]
+    step = min(512, width)
+
+    def whole(x):
+        return pl.BlockSpec(x.shape, lambda d: (0,) * len(x.shape))
+
+    narrow = pl.BlockSpec((tokens, step), lambda d: (0, d))
+    return pl.pallas_call(
+        functools.partial(combine_kernel, plan),
+        name="combine",
+        grid=(width // step,),
+        in_specs=[
+            SMEM,
+            whole(code),
+            whole(gates),
+            narrow,
+            whole(picks),
+            pl.BlockSpec((owners, plan.back[1], step), lambda d: (0, 0, d)),
+            pl.BlockSpec((owners, plan.back[2], step), lambda d: (0, 0, d)),
+        ],
+        out_specs=narrow,
+        out_shape=jax.ShapeDtypeStruct((tokens, width), BF16),
+        compiler_params=params(),
+    )(flag, code, gates, acc, picks, back, late)
+
+
+def batch_columns(meta, expert, local_experts, plan):
+    owners = meta.shape[0]
+    counts = jnp.where(
+        lax.broadcasted_iota(jnp.int32, meta.shape, 1) < local_experts, meta, 0
+    ).astype(F32)
+    lanes = counts.shape[1]
+    row = lax.broadcasted_iota(jnp.int32, (lanes, lanes), 0)
+    col = lax.broadcasted_iota(jnp.int32, (lanes, lanes), 1)
+    below = jnp.where(row < col, 1.0, 0.0).astype(BF16)
+    offsets = contract(counts.astype(BF16), below, ((1,), (0,)))
+    batch = owners * CAP
+    source_row = lax.broadcasted_iota(jnp.int32, (batch, owners), 0) // CAP
+    source_col = lax.broadcasted_iota(jnp.int32, (batch, owners), 1)
+    expand = jnp.where(source_row == source_col, 1.0, 0.0).astype(BF16)
+    lane = lax.broadcasted_iota(jnp.int32, (batch, lanes), 1)
+
+    def column(values, picked):
+        wide = contract(expand, values.astype(BF16), ((1,), (0,)))
+        return jnp.sum(jnp.where(picked, wide, 0.0), axis=1, keepdims=True).astype(jnp.int32)
+
+    count = column(counts, lane == expert)
+    offset = column(offsets, lane == expert)
+    front = column(counts, lane < plan.ahead)
+    index = lax.broadcasted_iota(jnp.int32, (batch, 1), 0)
+    rank = index % CAP
+    valid = rank < count
+    place = offset + rank
+    back = jnp.where(
+        (expert < plan.ahead) & (place < plan.back[0]),
+        place,
+        plan.back[0] + place - jnp.minimum(front, plan.back[0]),
+    )
+    return index // CAP, jnp.where(valid, place, -1), jnp.where(valid, back, -1)
+
+
+def expert_kernel(
+    first, taken, given, has_base, local_experts, parts, plan, flag_ref, meta_ref, gain_ref, *refs
+):
+    x_refs, refs = refs[:len(taken)], refs[len(taken):]
+    gate_ref, up_ref, down_ref = refs[:3]
+    base_ref = refs[3] if has_base else None
+    refs = refs[3 + has_base:]
+    out_refs, (batch_ref, acc_ref, done_ref) = refs[:len(given)], refs[len(given):]
+    e = pl.program_id(0)
+    f = pl.program_id(1)
+    last_f = pl.num_programs(1) - 1
+    batch = batch_ref.shape[0]
+    meta = meta_ref[...]
+
+    @pl.when(f == 0)
+    def _():
+        source, place, _ = batch_columns(meta, first + e, local_experts, plan)
+
+        context = source // parts
+        block = source % parts
+
+        def rows_of(i, k):
+            owners, rows, step = x_refs[i].shape
+            pieces = x_refs[i][...].reshape(owners // parts, parts, rows, step)
+            found = []
+            for h in range(parts):
+                turn = (h - block + parts) % parts
+                spread = one_hot(
+                    in_round(place, plan.out, k, context * parts + turn), owners * plan.out[k]
+                )
+                flat = pieces[:, h].reshape(owners // parts * rows, step)
+                found.append(contract(spread, flat, ((1,), (0,))))
+            return jnp.concatenate(found, axis=1)
+
+        total = 0.0
+        for i, k in enumerate(taken):
+            if k < 2:
+                total = total + rows_of(i, k)
+        acc_ref[...] = total
+        for i, k in enumerate(taken):
+            if k == 2:
+
+                @pl.when(flag_ref[0] > 0)
+                def _():
+                    acc_ref[...] = acc_ref[...] + rows_of(i, k)
+
+        stream = acc_ref[...]
+        scale = lax.rsqrt(jnp.mean(stream * stream, axis=-1, keepdims=True) + EPS)
+        batch_ref[...] = (stream * scale * gain_ref[...]).astype(BF16)
+
+    x = batch_ref[...]
+    gate = contract(x, gate_ref[...], ((1,), (0,)))
+    upward = contract(x, up_ref[...], ((1,), (0,)))
+    hidden = (gate / (1.0 + jnp.exp(-gate)) * upward).astype(BF16)
+    part = contract(hidden, down_ref[...], ((1,), (0,)))
+
+    @pl.when(f == 0)
+    def _():
+        acc_ref[...] = part
+
+    @pl.when((f > 0) & (f < last_f))
+    def _():
+        acc_ref[...] = acc_ref[...] + part
+
+    @pl.when(f == last_f)
+    def _():
+        done_ref[e] = (acc_ref[...] + part).astype(BF16)
+
+    @pl.when((e == pl.num_programs(0) - 1) & (f == last_f))
+    def _():
+        count = done_ref.shape[0]
+        columns = [batch_columns(meta, first + i, local_experts, plan) for i in range(count)]
+        source = jnp.concatenate([c[0] for c in columns], axis=0)
+        back = jnp.concatenate([c[2] for c in columns], axis=0)
+        done = done_ref[...].reshape(count * batch, done_ref.shape[2])
+
+        def put(i, k):
+            owners, rows, width = out_refs[i].shape
+            spread = one_hot(in_round(back, plan.back, k, source), owners * rows)
+            rows_out = contract(spread, done, ((0,), (0,)))
+            if has_base and k == 1:
+                rows_out = rows_out + base_ref[...].reshape(owners * rows, width).astype(F32)
+            out_refs[i][...] = rows_out.astype(BF16).reshape(owners, rows, width)
+
+        for i, k in enumerate(given):
+            if k < 2:
+                put(i, k)
+            else:
+
+                @pl.when(flag_ref[0] > 0)
+                def _():
+                    put(i, k)
+
+
+def serve_experts(flag, meta, gain, parts, received, weights, base, first, taken, given, plan):
+    w_gate, w_up, w_down = weights
+    local_experts, width, hidden = w_gate.shape
+    owners = meta.shape[0]
+    count = plan.ahead
+    split = 2
+    step = hidden // split
+
+    def whole(x):
+        return pl.BlockSpec(x.shape, lambda e, f: (0,) * len(x.shape))
+
+    in_spec = pl.BlockSpec((None, width, step), lambda e, f: (first + e, 0, f))
+    extra = [] if base is None else [base]
+    outs = [jax.ShapeDtypeStruct((owners, plan.back[k], width), BF16) for k in given]
+    batch = owners * CAP
+    return pl.pallas_call(
+        functools.partial(
+            expert_kernel, first, taken, given, base is not None, local_experts, parts, plan
+        ),
+        grid=(count, split),
+        in_specs=[SMEM, whole(meta), whole(gain)]
+        + [whole(x) for x in received]
+        + [
+            in_spec,
+            in_spec,
+            pl.BlockSpec((None, step, width), lambda e, f: (first + e, f, 0)),
+        ]
+        + [whole(x) for x in extra],
+        out_specs=[whole(x) for x in outs],
+        out_shape=outs,
+        scratch_shapes=[
+            pltpu.VMEM((batch, width), BF16),
+            pltpu.VMEM((batch, width), F32),
+            pltpu.VMEM((count, batch, width), BF16),
+        ],
+        compiler_params=params(),
+    )(flag, meta, gain, *received, w_gate, w_up, w_down, *extra)
+
+
+def everywhere(x):
+    return lax.all_to_all(x, ("ctx", "head"), split_axis=0, concat_axis=0, tiled=True)
+
+
+def everywhere_if(flag, x):
+    return lax.cond(flag[0] > 0, everywhere, lambda y: y, x)
+
+
+def body_dense(
     queries,
     keys,
     values,
@@ -344,7 +872,7 @@
     normed = mix_and_norm(queries, carried, local, route_col, head_gain[None], head_count)
     by_token = lax.all_to_all(normed, "head", split_axis=0, concat_axis=0, tiled=True)
 
-    stream, parcels = pack(
+    stream, parcels = pack_dense(
         residual_in, by_token, ffn_gain[None], expert_ids, chunks, owners, local_experts
     )
     backs = []
@@ -352,11 +880,87 @@
         received = lax.all_to_all(
             parcels[c], ("ctx", "head"), split_axis=0, concat_axis=0, tiled=True
         )
-        served = serve_experts(received, w_gate, w_up, w_down, c)
+        served = serve_dense(received, w_gate, w_up, w_down, c)
         backs.append(
             lax.all_to_all(served, ("ctx", "head"), split_axis=0, concat_axis=0, tiled=True)
         )
-    return combine(stream, expert_ids, expert_gates, backs, local_experts)
+    return combine_dense(stream, expert_ids, expert_gates, backs, local_experts)
+
+
+def body_compact(
+    queries,
+    keys,
+    values,
+    mem_route,
+    head_gain,
+    residual_in,
+    ffn_gain,
+    expert_ids,
+    expert_gates,
+    w_gate,
+    w_up,
+    w_down,
+):
+    length = queries.shape[0]
+    contexts = lax.axis_size("ctx")
+    parts = lax.axis_size("head")
+    local_experts = w_gate.shape[0]
+    plan = Plan(local_experts)
+    route_row = mem_route.reshape(1, length)
+    route_col = mem_route.reshape(length, 1)
+    head = lax.axis_index("head").astype(jnp.int32)[None]
+
+    def turned(pieces, step):
+        return [pieces[0]] + [
+            lax.ppermute(pieces[s], "head", [(h, (h + step * s) % parts) for h in range(parts)])
+            for s in range(1, parts)
+        ]
+
+    ids = turned([expert_ids.T] * parts, 1)
+    states = block_states(keys, values, route_row)
+    pieces = lax.all_to_all(states, "ctx", split_axis=0, concat_axis=0, tiled=True)
+    code, counts, *spreads = route(head, ids, contexts, local_experts, plan)
+    before = prefix_with_counts(pieces.reshape(contexts, -1, HD), counts)
+    carried = lax.all_to_all(before, "ctx", split_axis=0, concat_axis=0, tiled=True)
+    cut = columns_by_turn(head, residual_in, parts)
+    residuals = turned(cut, 1)
+    local = local_attention(queries, keys, values, route_row, route_col)
+    meta, flag, parcels, streams = mix_and_pack(
+        head,
+        queries,
+        carried,
+        counts.shape[1],
+        local,
+        route_col,
+        head_gain[None],
+        residuals,
+        spreads,
+        local_experts,
+        plan,
+    )
+    weights = (w_gate, w_up, w_down)
+    gain = ffn_gain[None]
+    received = [everywhere(parcels[0])]
+    received.append(everywhere(parcels[1]))
+    streams = turned(streams, -1)
+    back_0, base = serve_experts(
+        flag, meta, gain, parts, received[:1], weights, None, 0, (0,), (0, 1), plan
+    )
+    received.append(everywhere_if(flag, parcels[2]))
+    back_0 = everywhere(back_0)
+    back_1, back_2 = serve_experts(
+        flag, meta, gain, parts, received, weights, base, plan.ahead, (0, 1, 2), (1, 2), plan
+    )
+    back_2 = everywhere_if(flag, back_2)
+    back_1 = everywhere(back_1)
+    acc, picks = combine_ahead(head, code, expert_gates, back_0, streams, plan)
+    return combine(flag, code, expert_gates, acc, picks, back_1, back_2, plan)
+
+
+def body(*args):
+    local_experts = args[-1].shape[0]
+    compact = local_experts * CAP % (4 * GROUP_ROWS) == 0
+    return body_compact(*args) if compact else body_dense(*args)
 
 
 def solution(mesh):

time: 298 us -> 259 us (0.87)
  waiting for transfers between devices: 133 us -> 53 us
  Pallas kernels: 63.3 us -> 84.9 us
  blocking collectives: 74.2 us -> 84.8 us
  starting transfers between devices: 19.1 us -> 26.5 us
    all_to_all x5 -> x4, waiting for transfers between devices: 133 us -> 18.4 us  [the longest x2 15.6 us: everywhere(): lax.all_to_all(x, ('ctx', 'head'), split_axis=0, concat_axis=0, tiled=True)]
    ppermute x0 -> x9, waiting for transfers between devices: none -> 34.6 us  [turned(): lax.ppermute(pieces[s], 'head', [(h, (h + step * s) % parts) for h in ran...]
    pallas_call x6 -> x8, Pallas kernels: 51.7 us -> 73.3 us  [the longest x2 43.4 us: serve_experts(): pl.pallas_call(functools.partial(expert_kernel, first, taken, given, base...]
    all_to_all x2, blocking collectives: 74.2 us -> 84.8 us  [everywhere(): lax.all_to_all(x, ('ctx', 'head'), split_axis=0, concat_axis=0, tiled=True)]
    ppermute x0 -> x9, starting transfers between devices: none -> 8.01 us  [turned(): lax.ppermute(pieces[s], 'head', [(h, (h + step * s) % parts) for h in ran...]
    all_to_all x5 -> x4, starting transfers between devices: 19.1 us -> 18.5 us  [the longest x2 7.46 us: everywhere(): lax.all_to_all(x, ('ctx', 'head'), split_axis=0, concat_axis=0, tiled=True)]
    unnamed x16 -> x31, local copies, waits for them, and re-layouts: 6.05 us -> 6.59 us
  transfers between devices with their start and end apart: 5 -> 13, of which waited for: 5 -> 9; matrix products, arithmetic and copies ran while one was open for 1% -> 1% of each run, Pallas kernels for 13% -> 16%
where the time goes in v2:
time: 259 us; the launch traced here: 258 us
  Pallas kernels  84.9 us (33%)
  blocking collectives  84.8 us (33%)
  waiting for transfers between devices  53 us (20%)
  starting transfers between devices  26.5 us (10%)
  local copies, waits for them, and re-layouts  7.66 us (3%)
    all_to_all x2, blocking collectives, everywhere(): lax.all_to_all(x, ('ctx', 'head'), split_axis=0, concat_axis=0, tiled=True)  84.8 us
    pallas_call x2, Pallas kernels, serve_experts(): pl.pallas_call(functools.partial(expert_kernel, first, taken, given, base...  43.4 us
    ppermute x9, waiting for transfers between devices, turned(): lax.ppermute(pieces[s], 'head', [(h, (h + step * s) % parts) for h in ran...  34.6 us
    all_to_all x2, waiting for transfers between devices, everywhere(): lax.all_to_all(x, ('ctx', 'head'), split_axis=0, concat_axis=0, tiled=True)  15.6 us
    pallas_call x1, Pallas kernels, mix_and_pack(): pl.pallas_call(functools.partial(mix_pack_kernel, parts, local_experts, p...  9.03 us
    ppermute x9, starting transfers between devices, turned(): lax.ppermute(pieces[s], 'head', [(h, (h + step * s) % parts) for h in ran...  8.01 us
    all_to_all x2, starting transfers between devices, everywhere(): lax.all_to_all(x, ('ctx', 'head'), split_axis=0, concat_axis=0, tiled=True)  7.46 us
    all_to_all x1, starting transfers between devices, body_compact(): lax.all_to_all(states, 'ctx', split_axis=0, concat_axis=0, tiled=True)  7.44 us
  transfers between devices with their start and end apart: 13, of which 9 were waited for; matrix products, arithmetic and copies ran while one was open for 1% of the time, Pallas kernels for 16%

profile of v2, /device:TPU:0, one launch (start us, length us, event | category | flops | bytes accessed | tf_op | source)
XLA Modules:
  0.0 257.8 jit_solution(13097331885848781361)
XLA Ops:
  0.0 4.4 %block_states.1 = bf16[2048,128]{1,0:T(8,128)(2,1)} custom-call(bf16[1024,512]{1,0:T(8,128)(2,1)} %key_ref.3, bf16[1024,512]{1,0:T(8,128)(2,1)} %value_ref.3, s32[1,1024]{1,0:T(1,128)} %bitcast.9), custom_call_target="tpu_custom_call" | custom-call | tf_op jit(solution)/shard_map/block_states/pallas_call | solution.py:41
  4.4 7.4 %all-to-all-start.2 = ((bf16[8,256,128]{2,1,0:T(8,128)(2,1)}), bf16[8,256,128]{2,1,0:T(8,128)(2,1)S(1)}, u32[]{:S(2)}, u32[]{:S(2)}) async-start(bf16[8,256,128]{2,1,0:T(8,128)(2,1)} %bitcast.8), calls=%async_computation.2 | async-start | bytes 1048576 | tf_op jit(solution)/shard_map/all_to_all | solution.py:921
  11.9 1.6 collective-permute-start.1
  16.7 6.8 %route.1 = (s32[256,128]{1,0:T(8,128)}, f32[8,8,128]{2,1,0:T(8,128)}, bf16[4,512,256]{2,1,0:T(8,128)(2,1)}, bf16[4,256,256]{2,1,0:T(8,128)(2,1)}, bf16[4,256,256]{2,1,0:T(8,128)(2,1)}) custom-call(s32[1]{0:T(128)} %bitcast.head_ref, s32[2,256]{1,0:T(2,128)} %bitcast.15, s32[2,256]{1,0:T(2,128)} %copy-done.12, s32[2,256]{1,0:T(2,128)} %copy-done.13, ...), custom_call_target="tpu_custom_call" | custom-call | tf_op jit(solution)/shard_map/route/pallas_call | solution.py:422
  23.5 2.8 %all-to-all-done.2.piece_ref = bf16[8,256,128]{2,1,0:T(8,128)(2,1)S(1)} async-done(((bf16[8,256,128]{2,1,0:T(8,128)(2,1)}), bf16[8,256,128]{2,1,0:T(8,128)(2,1)S(1)}, u32[]{:S(2)}, u32[]{:S(2)}) %all-to-all-start.2) | async-done | bytes 524320 | tf_op jit(solution)/shard_map/all_to_all | solution.py:921
  27.1 1.9 prefix_with_counts.1
  29.0 3.6 %all-to-all-start.3 = ((bf16[8,264,128]{2,1,0:T(8,128)(2,1)}), bf16[8,264,128]{2,1,0:T(8,128)(2,1)S(1)}, u32[]{:S(2)}, u32[]{:S(2)}) async-start(bf16[8,264,128]{2,1,0:T(8,128)(2,1)} %prefix_with_counts.1), calls=%async_computation.3 | async-start | bytes 1081344 | tf_op jit(solution)/shard_map/all_to_all | solution.py:924
  32.7 2.3 columns_by_turn.1
  39.0 7.2 %local_attention.1.local_ref = f32[1024,512]{1,0:T(8,128)} custom-call(bf16[1024,512]{1,0:T(8,128)(2,1)} %query_ref.3, bf16[1024,512]{1,0:T(8,128)(2,1)} %key_ref.3, bf16[1024,512]{1,0:T(8,128)(2,1)} %value_ref.3, s32[1,1024]{1,0:T(1,128)} %bitcast.10, s32[1024,1]{1,0:T(8,128)} %copy.15.route_col_ref), custom_call_target="tpu_custom_call" | custom-call | tf_op jit(solution)/shard_map/local_attention/pallas_call | solution.py:100
  46.3 2.3 collective-permute-done.5.refs_3_
  49.5 9.0 %mix_and_pack.1 = (s32[32,128]{1,0:T(8,128)}, s32[1]{0:T(128)}, bf16[32,64,512]{2,1,0:T(8,128)(2,1)}, bf16[32,32,512]{2,1,0:T(8,128)(2,1)}, bf16[32,32,512]{2,1,...) custom-call(s32[1]{0:T(128)} %bitcast.head_ref, ...), custom_call_target="tpu_custom_call" | custom-call | tf_op jit(solution)/shard_map/mix_and_pack/pallas_call | solution.py:551
  59.2 55.1 %all_to_all.44.refs_0_ = bf16[32,64,512]{2,1,0:T(8,128)(2,1)} all-to-all(bf16[32,64,512]{2,1,0:T(8,128)(2,1)} %get-tuple-element.50), channel_id=1, replica_groups=mesh['ctx'=8,'head'=4] {'ctx','head'}, dimensions={0} | all-to-all | bytes 4194304 | tf_op jit(solution)/shard_map/all_to_all | solution.py:834
  114.3 3.8 %all-to-all-start.6 = ((bf16[32,32,512]{2,1,0:T(8,128)(2,1)}), bf16[32,32,512]{2,1,0:T(8,128)(2,1)S(1)}, u32[]{:S(2)}, u32[]{:S(2)}) async-start(bf16[32,32,512]{2,1,0:T(8,128)(2,1)} %get-tuple-element.58), calls=%async_computation.6 | async-start | bytes 2097152 | tf_op jit(solution)/shard_map/all_to_all | solution.py:834
  118.2 21.3 %shard_map.118 = (bf16[32,8,2048]{2,1,0:T(8,128)(2,1)}, bf16[32,16,2048]{2,1,0:T(8,128)(2,1)}) custom-call(s32[1]{0:T(128)} %get-tuple-element.47.flag_ref, s32[32,128]{1,0:T(8,128)} %get-tuple-element.49.meta_ref, f32[1,2048]{1,0:T(1,128)} %bitcast.12, bf16[32,64,512]{2,1,0:T(8,128)(2,1)} %all_to_all.44.refs_0_, bf16[8,2048,512]{2,1,0:T(8,128)(2,1)} %refs_3_.3, ...), custom_call_target="tpu_custom_call" | custom-call | tf_op jit(solution)/shard_map/pallas_call | solution.py:809
  139.4 4.7 %all-to-all-done.6.refs_1_ = bf16[32,32,512]{2,1,0:T(8,128)(2,1)S(1)} async-done(((bf16[32,32,512]{2,1,0:T(8,128)(2,1)}), bf16[32,32,512]{2,1,0:T(8,128)(2,1)S(1)}, u32[]{:S(2)}, u32[]{:S(2)}) %all-to-all-start.6) | async-done | bytes 1048608 | tf_op jit(solution)/shard_map/all_to_all | solution.py:834
  145.1 22.1 %shard_map.119 = (bf16[32,16,2048]{2,1,0:T(8,128)(2,1)}, bf16[32,8,2048]{2,1,0:T(8,128)(2,1)S(1)}) custom-call(s32[1]{0:T(128)} %get-tuple-element.47.flag_ref, s32[32,128]{1,0:T(8,128)} %get-tuple-element.49.meta_ref, f32[1,2048]{1,0:T(1,128)} %bitcast.13, bf16[32,64,512]{2,1,0:T(8,128)(2,1)} %all_to_all.44.refs_0_, bf16[32,32,512]{2,1,0:T(8,128)(2,1)} %copy-done.2, ...), custom_call_target="tpu_custom_call" | custom-call | tf_op jit(solution)/shard_map/pallas_call | solution.py:809
  168.5 29.7 %all_to_all.45.back_ref = bf16[32,8,2048]{2,1,0:T(8,128)(2,1)} all-to-all(bf16[32,8,2048]{2,1,0:T(8,128)(2,1)S(1)} %copy-done.4), channel_id=1, replica_groups=mesh['ctx'=8,'head'=4] {'ctx','head'}, dimensions={0} | all-to-all | bytes 2097152 | tf_op jit(solution)/shard_map/all_to_all | solution.py:834
  198.2 3.6 %all-to-all-start.7 = ((bf16[32,16,2048]{2,1,0:T(8,128)(2,1)}), bf16[32,16,2048]{2,1,0:T(8,128)(2,1)S(1)}, u32[]{:S(2)}, u32[]{:S(2)}) async-start(bf16[32,16,2048]{2,1,0:T(8,128)(2,1)} %get-tuple-element.61), calls=%async_computation.7 | async-start | bytes 4194304 | tf_op jit(solution)/shard_map/all_to_all | solution.py:834
  201.8 1.5 collective-permute-start.6
  204.7 21.3 %collective-permute-done.6.refs_1_ = bf16[256,512]{1,0:T(8,128)(2,1)S(1)} collective-permute-done((bf16[256,512]{1,0:T(8,128)(2,1)}, bf16[256,512]{1,0:T(8,128)(2,1)S(1)}, u32[]{:S(2)}, u32[]{:S(2)}) %collective-permute-start.6) | collective-permute-done | bytes 262176 | tf_op jit(solution)/shard_map/ppermute | solution.py:915
  226.0 9.6 %collective-permute-done.7.refs_2_ = bf16[256,512]{1,0:T(8,128)(2,1)} collective-permute-done((bf16[256,512]{1,0:T(8,128)(2,1)}, bf16[256,512]{1,0:T(8,128)(2,1)}, u32[]{:S(2)}, u32[]{:S(2)}) %collective-permute-start.7) | collective-permute-done | bytes 262176 | tf_op jit(solution)/shard_map/ppermute | solution.py:915
  235.7 4.1 %combine_ahead.1 = (f32[256,2048]{1,0:T(8,128)}, bf16[2,256,512]{2,1,0:T(8,128)(2,1)}) custom-call(s32[1]{0:T(128)} %bitcast.head_ref, s32[256,128]{1,0:T(8,128)} %get-tuple-element.48.code_ref, f32[256,2]{1,0:T(8,128)} %copy.18.gates_ref, bf16[32,8,2048]{2,1,0:T(8,128)(2,1)} %all_to_all.45.back_ref, bf16[256,512]{1,0:T(8,128)(2,1)} %get-tuple-element.52.refs_0_, ...), custom_call_target="tpu_custom_call" | custom-call | tf_op jit(solution)/shard_map/combine_ahead/pallas_call | solution.py:609
  239.8 10.9 %all-to-all-done.7.back_ref = bf16[32,16,2048]{2,1,0:T(8,128)(2,1)S(1)} async-done(((bf16[32,16,2048]{2,1,0:T(8,128)(2,1)}), bf16[32,16,2048]{2,1,0:T(8,128)(2,1)S(1)}, u32[]{:S(2)}, u32[]{:S(2)}) %all-to-all-start.7) | async-done | bytes 2097184 | tf_op jit(solution)/shard_map/all_to_all | solution.py:834
  252.0 5.7 %combine.1 = bf16[256,2048]{1,0:T(8,128)(2,1)} custom-call(s32[1]{0:T(128)} %get-tuple-element.47.flag_ref, s32[256,128]{1,0:T(8,128)} %get-tuple-element.48.code_ref, f32[256,2]{1,0:T(8,128)} %copy.18.gates_ref, f32[256,2048]{1,0:T(8,128)} %get-tuple-element.56.acc_ref, bf16[2,256,512]{2,1,0:T(8,128)(2,1)} %get-tuple-element.57.pick_ref, ...), custom_call_target="tpu_custom_call" | custom-call | tf_op jit(solution)/shard_map/combine/pallas_call | solution.py:646
  (48 shorter events, 13.9 us)
Async XLA Ops:
  0.0 11.8 %copy-start.11 = (s32[256,2]{0,1:T(2,128)S(1)}, s32[256,2]{0,1:T(2,128)}, u32[]{:S(2)}) copy-start(s32[256,2]{0,1:T(2,128)} %param.23) | copy-start | bytes 6148
  4.4 33.6 %copy-start.9 = (s32[1024]{0:T(1024)S(1)}, s32[1024]{0:T(1024)}, u32[]{:S(2)}) copy-start(s32[1024]{0:T(1024)} %param.19) | copy-start | bytes 12292
  4.4 21.9 %all-to-all-start.2 = ((bf16[8,256,128]{2,1,0:T(8,128)(2,1)}), bf16[8,256,128]{2,1,0:T(8,128)(2,1)S(1)}, u32[]{:S(2)}, u32[]{:S(2)}) async-start(bf16[8,256,128]{2,1,0:T(8,128)(2,1)} %bitcast.8), calls=%async_computation.2 | async-start | bytes 1048576 | tf_op jit(solution)/shard_map/all_to_all | solution.py:921
  11.8 3.1 %collective-permute-start = (s32[2,256]{1,0:T(2,128)S(1)}, s32[2,256]{1,0:T(2,128)S(1)}, u32[]{:S(2)}, u32[]{:S(2)}) collective-permute-start(s32[2,256]{1,0:T(2,128)S(1)} %bitcast.16), channel_id=1, source_target_pairs={{0,1},{1,2},{2,3},{3,0},{4,5},{5,6},{6,7},{7,4},{8,9},{9,10},{10,1... | collective-permute-start | bytes 6152 | tf_op jit(solution)/shard_map/ppermute | solution.py:915
  11.9 3.7 %collective-permute-start.1 = (s32[2,256]{1,0:T(2,128)S(1)}, s32[2,256]{1,0:T(2,128)S(1)}, u32[]{:S(2)}, u32[]{:S(2)}) collective-permute-start(s32[2,256]{1,0:T(2,128)S(1)} %bitcast.17), channel_id=1, source_target_pairs={{0,2},{1,3},{2,0},{3,1},{4,6},{5,7},{6,4},{7,5},{8,10},{9,11},{10,... | collective-permute-start | bytes 6152 | tf_op jit(solution)/shard_map/ppermute | solution.py:915
  13.5 2.7 %collective-permute-start.2 = (s32[2,256]{1,0:T(2,128)S(1)}, s32[2,256]{1,0:T(2,128)S(1)}, u32[]{:S(2)}, u32[]{:S(2)}) collective-permute-start(s32[2,256]{1,0:T(2,128)S(1)} %bitcast.18), channel_id=1, source_target_pairs={{0,3},{1,0},{2,1},{3,2},{4,7},{5,4},{6,5},{7,6},{8,11},{9,8},{10,9... | collective-permute-start | bytes 6152 | tf_op jit(solution)/shard_map/ppermute | solution.py:915
  14.9 1.3 copy-start.12
  29.0 19.5 %all-to-all-start.3 = ((bf16[8,264,128]{2,1,0:T(8,128)(2,1)}), bf16[8,264,128]{2,1,0:T(8,128)(2,1)S(1)}, u32[]{:S(2)}, u32[]{:S(2)}) async-start(bf16[8,264,128]{2,1,0:T(8,128)(2,1)} %prefix_with_counts.1), calls=%async_computation.3 | async-start | bytes 1081344 | tf_op jit(solution)/shard_map/all_to_all | solution.py:924
  35.0 11.2 %collective-permute-start.3 = (bf16[256,512]{1,0:T(8,128)(2,1)}, bf16[256,512]{1,0:T(8,128)(2,1)S(1)}, u32[]{:S(2)}, u32[]{:S(2)}) collective-permute-start(bf16[256,512]{1,0:T(8,128)(2,1)} %get-tuple-element.41), channel_id=1, source_target_pairs={{0,1},{1,2},{2,3},{3,0},{4,5},{5,6},{6,7},{7,4},{8,9},{9,10},{10,1... | collective-permute-start | bytes 786440 | tf_op jit(solution)/shard_map/ppermute | solution.py:915
  35.1 11.1 %collective-permute-start.4 = (bf16[256,512]{1,0:T(8,128)(2,1)}, bf16[256,512]{1,0:T(8,128)(2,1)S(1)}, u32[]{:S(2)}, u32[]{:S(2)}) collective-permute-start(bf16[256,512]{1,0:T(8,128)(2,1)} %get-tuple-element.42), channel_id=1, source_target_pairs={{0,2},{1,3},{2,0},{3,1},{4,6},{5,7},{6,4},{7,5},{8,10},{9,11},{10,... | collective-permute-start | bytes 786440 | tf_op jit(solution)/shard_map/ppermute | solution.py:915
  36.6 12.0 %collective-permute-start.5 = (bf16[256,512]{1,0:T(8,128)(2,1)}, bf16[256,512]{1,0:T(8,128)(2,1)S(1)}, u32[]{:S(2)}, u32[]{:S(2)}) collective-permute-start(bf16[256,512]{1,0:T(8,128)(2,1)} %get-tuple-element.43), channel_id=1, source_target_pairs={{0,3},{1,0},{2,1},{3,2},{4,7},{5,4},{6,5},{7,6},{8,11},{9,8},{10,9... | collective-permute-start | bytes 786440 | tf_op jit(solution)/shard_map/ppermute | solution.py:915
  46.2 2.3 copy-start.5
  46.3 2.3 copy-start.6
  48.6 0.9 copy-start.1
  114.3 29.9 %all-to-all-start.6 = ((bf16[32,32,512]{2,1,0:T(8,128)(2,1)}), bf16[32,32,512]{2,1,0:T(8,128)(2,1)S(1)}, u32[]{:S(2)}, u32[]{:S(2)}) async-start(bf16[32,32,512]{2,1,0:T(8,128)(2,1)} %get-tuple-element.58), calls=%async_computation.6 | async-start | bytes 2097152 | tf_op jit(solution)/shard_map/all_to_all | solution.py:834
  144.2 1.0 copy-start.2
  167.3 1.2 copy-start.4
  198.2 5.7 %copy-start.10 = (f32[256,2]{0,1:T(2,128)S(1)}, f32[256,2]{0,1:T(2,128)}, u32[]{:S(2)}) copy-start(f32[256,2]{0,1:T(2,128)} %param.24) | copy-start | bytes 6148
  198.2 52.5 %all-to-all-start.7 = ((bf16[32,16,2048]{2,1,0:T(8,128)(2,1)}), bf16[32,16,2048]{2,1,0:T(8,128)(2,1)S(1)}, u32[]{:S(2)}, u32[]{:S(2)}) async-start(bf16[32,16,2048]{2,1,0:T(8,128)(2,1)} %get-tuple-element.61), calls=%async_computation.7 | async-start | bytes 4194304 | tf_op jit(solution)/shard_map/all_to_all | solution.py:834
  201.8 24.2 %collective-permute-start.6 = (bf16[256,512]{1,0:T(8,128)(2,1)}, bf16[256,512]{1,0:T(8,128)(2,1)S(1)}, u32[]{:S(2)}, u32[]{:S(2)}) collective-permute-start(bf16[256,512]{1,0:T(8,128)(2,1)} %get-tuple-element.53), channel_id=1, source_target_pairs={{0,3},{1,0},{2,1},{3,2},{4,7},{5,4},{6,5},{7,6},{8,11},{9,8},{10,9... | collective-permute-start | bytes 786440 | tf_op jit(solution)/shard_map/ppermute | solution.py:915
  203.4 32.3 %collective-permute-start.7 = (bf16[256,512]{1,0:T(8,128)(2,1)}, bf16[256,512]{1,0:T(8,128)(2,1)}, u32[]{:S(2)}, u32[]{:S(2)}) collective-permute-start(bf16[256,512]{1,0:T(8,128)(2,1)} %get-tuple-element.54), channel_id=1, source_target_pairs={{0,2},{1,3},{2,0},{3,1},{4,6},{5,7},{6,4},{7,5},{8,10},{9,11},{10,... | collective-permute-start | bytes 786440 | tf_op jit(solution)/shard_map/ppermute | solution.py:915
  203.8 31.9 %collective-permute-start.8 = (bf16[256,512]{1,0:T(8,128)(2,1)}, bf16[256,512]{1,0:T(8,128)(2,1)}, u32[]{:S(2)}, u32[]{:S(2)}) collective-permute-start(bf16[256,512]{1,0:T(8,128)(2,1)} %get-tuple-element.55), channel_id=1, source_target_pairs={{0,1},{1,2},{2,3},{3,0},{4,5},{5,6},{6,7},{7,4},{8,9},{9,10},{10,1... | collective-permute-start | bytes 786440 | tf_op jit(solution)/shard_map/ppermute | solution.py:915
  226.0 9.6 %copy-start.8 = (bf16[256,512]{1,0:T(8,128)(2,1)}, bf16[256,512]{1,0:T(8,128)(2,1)S(1)}, u32[]{:S(2)}) copy-start(bf16[256,512]{1,0:T(8,128)(2,1)S(1)} %collective-permute-done.6.refs_1_) | copy-start | bytes 786436
  250.7 1.4 copy-start
  (4 other events, 2.7 us)

commit v3 on v2

--- a/solution.py
+++ b/solution.py
@@ -18,8 +18,16 @@
 BF16 = jnp.bfloat16
 
 
-def params(**more):
-    return pltpu.CompilerParams(vmem_limit_bytes=60 * 1024 * 1024, **more)
+def params(mebibytes=60):
+    return pltpu.CompilerParams(vmem_limit_bytes=mebibytes * 1024 * 1024)
+
+
+def in_hbm(x):
+    return pltpu.with_memory_space_constraint(x, pltpu.HBM)
+
+
+def in_vmem(x):
+    return pltpu.with_memory_space_constraint(x, pltpu.VMEM)
 
 
 def contract(a, b, dims):
@@ -48,9 +56,9 @@
             pl.BlockSpec((1, length), lambda h: (0, 0)),
         ],
         out_specs=pl.BlockSpec((M * HD, HD), lambda h: (h, 0)),
-        out_shape=jax.ShapeDtypeStruct((heads * M * HD, HD), BF16),
-        compiler_params=params(),
-    )(keys, values, route_row)
+        out_shape=pltpu.HBM((heads * M * HD, HD), BF16),
+        compiler_params=params(16),
+    )(in_hbm(keys), in_hbm(values), in_hbm(route_row))
 
 
 def prefix_kernel(ranks, piece_ref, out_ref):
@@ -111,8 +119,8 @@
         out_specs=wide,
         out_shape=jax.ShapeDtypeStruct((length, width), F32),
         scratch_shapes=[pltpu.VMEM((length, length), F32)],
-        compiler_params=params(),
-    )(queries, keys, values, route_row, route_col)
+        compiler_params=params(32),
+    )(in_hbm(queries), in_hbm(keys), in_hbm(values), route_row, route_col)
 
 
 def mix_kernel(query_ref, state_ref, local_ref, route_col_ref, gain_ref, out_ref):
@@ -425,11 +433,11 @@
         in_specs=[SMEM] + [VMEM] * parts,
         out_specs=[VMEM] * 5,
         out_shape=[
-            jax.ShapeDtypeStruct((tokens, HD), jnp.int32),
+            pltpu.HBM((tokens, HD), jnp.int32),
             jax.ShapeDtypeStruct((contexts, parts + -parts % 8, HD), F32),
         ]
-        + [jax.ShapeDtypeStruct((parts, owners * rows, tokens), BF16) for rows in plan.out],
-        compiler_params=params(),
+        + [pltpu.HBM((parts, owners * rows, tokens), BF16) for rows in plan.out],
+        compiler_params=params(24),
     )(head, *ids)
 
 
@@ -450,8 +458,8 @@
         name="prefix_with_counts",
         in_specs=[VMEM] * 2,
         out_specs=VMEM,
-        out_shape=jax.ShapeDtypeStruct((ranks, rows + meta.shape[1], width), BF16),
-        compiler_params=params(),
+        out_shape=pltpu.HBM((ranks, rows + meta.shape[1], width), BF16),
+        compiler_params=params(12),
     )(pieces, meta)
 
 
@@ -469,41 +477,43 @@
         name="columns_by_turn",
         in_specs=[SMEM, VMEM],
         out_specs=[VMEM] * parts,
-        out_shape=[jax.ShapeDtypeStruct((tokens, width // parts), BF16)] * parts,
-        compiler_params=params(),
+        out_shape=[pltpu.HBM((tokens, width // parts), BF16)] * parts,
+        compiler_params=params(12),
     )(head, whole)
 
 
 def mix_pack_kernel(
     parts, local_experts, plan, head_ref, query_ref, state_ref, tail_ref, local_ref, route_col_ref, gain_ref, *refs
 ):
-    residual_refs, spread_refs = refs[:parts], refs[parts:parts + 3]
-    refs = refs[parts + 3:]
-    meta_ref, flag_ref, parcel_refs, stream_refs = refs[0], refs[1], refs[2:5], refs[5:5 + parts]
+    residual_refs, spread_ref = refs[:parts], refs[parts]
+    refs = refs[parts + 1:]
+    meta_ref, flag_ref, parcel_ref, stream_refs = refs[0], refs[1], refs[2], refs[3:3 + parts]
     normed_ref = refs[-1]
     head = head_ref[0]
-    share, rows, _ = state_ref.shape
+    pieces, rows, _ = state_ref.shape
     contexts, tail, _ = tail_ref.shape
     rows -= tail
-    query = query_ref[...]
+    width = query_ref.shape[1]
+    together = width // HD
+    share = pieces // together
     column = route_col_ref[...]
-    wide = jnp.concatenate(
-        [query * jnp.where(column == m, 2.0, 1.0).astype(BF16) for m in range(M)], axis=1
-    )
-    state = jnp.concatenate([state_ref[i, :rows, :] for i in range(share)], axis=0)
-    mixed = contract(wide, state, ((1,), (0,))) + local_ref[...]
-    scale = lax.rsqrt(jnp.mean(mixed * mixed, axis=-1, keepdims=True) + EPS)
-    normed_ref[...] = (mixed * scale * gain_ref[...]).astype(BF16)
-
-    counts = tail_ref[...].astype(F32)
-    owners = contexts * parts
-    lane = lax.broadcasted_iota(jnp.int32, counts.shape, 2)
-    over = jnp.max(jnp.where(lane == local_experts, counts, 0.0))
-    flag = (over > 0.5).astype(jnp.int32)
-    flag_ref[0] = flag
+    doubled = [jnp.where(column == m, 2.0, 1.0).astype(BF16) for m in range(M)]
+    for g in range(together):
+        span = slice(g * HD, (g + 1) * HD)
+        query = query_ref[:, span]
+        wide = jnp.concatenate([query * weight for weight in doubled], axis=1)
+        state = jnp.concatenate([state_ref[g * share + i, :rows, :] for i in range(share)], axis=0)
+        mixed = contract(wide, state, ((1,), (0,))) + local_ref[:, span]
+        scale = lax.rsqrt(jnp.mean(mixed * mixed, axis=-1, keepdims=True) + EPS)
+        normed_ref[:, span] = (mixed * scale * gain_ref[:, span]).astype(BF16)
 
     @pl.when(pl.program_id(0) == 0)
     def _():
+        counts = tail_ref[...].astype(F32)
+        owners = contexts * parts
+        lane = lax.broadcasted_iota(jnp.int32, counts.shape, 2)
+        over = jnp.max(jnp.where(lane == local_experts, counts, 0.0))
+        flag_ref[0] = (over > 0.5).astype(jnp.int32)
         source = lax.broadcasted_iota(jnp.int32, (owners, contexts * tail), 0)
         given = lax.broadcasted_iota(jnp.int32, (owners, contexts * tail), 1)
         turn = (head - source % parts + parts) % parts
@@ -517,41 +527,37 @@
         normed = normed_ref[pl.ds(start, tokens), :]
         stream = (residual_refs[s][...].astype(F32) + normed.astype(F32)).astype(BF16)
         stream_refs[s][...] = stream
-
-    def fill(k):
-        each = plan.out[k]
-        for s in range(parts):
-            packed = contract(spread_refs[k][s], stream_refs[s][...], ((1,), (0,))).astype(BF16)
-            parcel_refs[k][:, s * each:(s + 1) * each, :] = packed.reshape(owners, each, HD)
-
-    fill(0)
-    fill(1)
-
-    @pl.when(flag > 0)
-    def _():
-        fill(2)
-
-
-def mix_and_pack(head, queries, carried, tail, local, route_col, head_gain, residuals, spreads, local_experts, plan):
+        put_parcels(plan.out[0], s, spread_ref[s], stream, parcel_ref)
+
+
+def put_parcels(each, s, spread, stream, parcel_ref):
+    owners, _, width = parcel_ref.shape
+    packed = contract(spread, stream, ((1,), (0,))).astype(BF16)
+    parcel_ref[:, s * each:(s + 1) * each, :] = packed.reshape(owners, each, width)
+
+
+def mix_and_pack(head, queries, carried, tail, local, route_col, head_gain, residuals, spread, local_experts, plan):
     length, width = queries.shape
     heads = width // HD
+    together = 2 if heads % 2 == 0 else 1
+    step = together * HD
     contexts, rows, _ = carried.shape
-    share = contexts // heads
+    share = contexts * together // heads
     parts = len(residuals)
     tokens = length // parts
     owners = contexts * parts
-    wide = pl.BlockSpec((length, HD), lambda h: (0, h))
-    narrow = pl.BlockSpec((tokens, HD), lambda h: (0, h))
+    wide = pl.BlockSpec((length, step), lambda h: (0, h))
+    narrow = pl.BlockSpec((tokens, step), lambda h: (0, h))
 
     def whole(x):
         return pl.BlockSpec(x.shape, lambda h: (0,) * len(x.shape))
 
-    parcels = [jax.ShapeDtypeStruct((owners, parts * r, width), BF16) for r in plan.out]
-    meta = jax.ShapeDtypeStruct((owners, HD), jnp.int32)
+    each = parts * plan.out[0]
+    meta = pltpu.HBM((owners, HD), jnp.int32)
     out = pl.pallas_call(
         functools.partial(mix_pack_kernel, parts, local_experts, plan),
         name="mix_and_pack",
-        grid=(heads,),
+        grid=(heads // together,),
         in_specs=[
             SMEM,
             wide,
@@ -559,20 +565,63 @@
             pl.BlockSpec((contexts, tail, HD), lambda h: (0, (rows - tail) // tail, 0)),
             wide,
             pl.BlockSpec((length, 1), lambda h: (0, 0)),
-            pl.BlockSpec((1, HD), lambda h: (0, h)),
+            pl.BlockSpec((1, step), lambda h: (0, h)),
         ]
         + [narrow] * parts
-        + [whole(x) for x in spreads],
-        out_specs=[whole(meta), SMEM]
-        + [pl.BlockSpec((owners, x.shape[1], HD), lambda h: (0, 0, h)) for x in parcels]
+        + [whole(spread)],
+        out_specs=[whole(meta), SMEM, pl.BlockSpec((owners, each, step), lambda h: (0, 0, h))]
         + [narrow] * parts,
-        out_shape=[meta, jax.ShapeDtypeStruct((1,), jnp.int32)]
-        + parcels
-        + [jax.ShapeDtypeStruct((tokens, width), BF16)] * parts,
-        scratch_shapes=[pltpu.VMEM((length, HD), BF16)],
-        compiler_params=params(),
-    )(head, queries, carried, carried, local, route_col, head_gain, *residuals, *spreads)
-    return out[0], out[1], out[2:5], out[5:]
+        out_shape=[
+            meta,
+            jax.ShapeDtypeStruct((1,), jnp.int32),
+            pltpu.HBM((owners, each, width), BF16),
+        ]
+        + [pltpu.HBM((tokens, width), BF16)] * parts,
+        scratch_shapes=[pltpu.VMEM((length, step), BF16)],
+        compiler_params=params(32),
+    )(
+        head,
+        in_hbm(queries),
+        carried,
+        carried,
+        local,
+        route_col,
+        head_gain,
+        *map(in_hbm, residuals),
+        in_hbm(spread),
+    )
+    return out[0], out[1], out[2], out[3:]
+
+
+def pack_kernel(each, spread_ref, *refs):
+    for s, stream_ref in enumerate(refs[:-1]):
+        put_parcels(each, s, spread_ref[s], stream_ref[...], refs[-1])
+
+
+def pack(k, spread, streams, owners, plan):
+    each = plan.out[k]
+    shape = (owners, len(streams) * each, streams[0].shape[1])
+    return pl.pallas_call(
+        functools.partial(pack_kernel, each),
+        in_specs=[VMEM] * (1 + len(streams)),
+        out_specs=VMEM,
+        out_shape=pltpu.HBM(shape, BF16),
+        compiler_params=params(24),
+    )(in_hbm(spread), *map(in_hbm, streams))
+
+
+def unset_kernel(out_ref):
+    pass
+
+
+def unset(shape):
+    return pl.pallas_call(
+        unset_kernel,
+        name="unset",
+        out_specs=pl.BlockSpec(memory_space=pl.ANY),
+        out_shape=pltpu.HBM(shape, BF16),
+        compiler_params=params(4),
+    )()
 
 
 def gated(gates, spreads, back):
@@ -589,7 +638,7 @@
     ]
 
 
-def combine_ahead_kernel(plan, parts, head_ref, code_ref, gates_ref, back_ref, *refs):
+def combine_ahead_kernel(plan, parts, head_ref, flag_ref, code_ref, gates_ref, back_ref, late_ref, *refs):
     stream_refs, (acc_ref, pick_ref) = refs[:parts], refs[parts:]
     code = code_ref[...]
     owners, rows, width = back_ref.shape
@@ -602,41 +651,40 @@
     for j, spread in enumerate(choices(code, plan, 1, owners)):
         pick_ref[j] = spread
 
-
-def combine_ahead(head, code, gates, back, streams, plan):
+    @pl.when(flag_ref[0] > 0)
+    def _():
+        late = late_ref[...].reshape(owners * plan.back[2], width)
+        acc_ref[...] = acc_ref[...] + gated(gates_ref[...], choices(code, plan, 2, owners), late)
+
+
+def combine_ahead(head, flag, code, gates, back, late, streams, plan):
     owners, _, width = back.shape
     tokens = code.shape[0]
     return pl.pallas_call(
         functools.partial(combine_ahead_kernel, plan, len(streams)),
         name="combine_ahead",
-        in_specs=[SMEM] + [VMEM] * (3 + len(streams)),
+        in_specs=[SMEM] * 2 + [VMEM] * (4 + len(streams)),
         out_specs=[VMEM] * 2,
         out_shape=[
-            jax.ShapeDtypeStruct((tokens, width), F32),
-            jax.ShapeDtypeStruct((2, tokens, owners * plan.back[1]), BF16),
+            pltpu.HBM((tokens, width), F32),
+            pltpu.HBM((2, tokens, owners * plan.back[1]), BF16),
         ],
-        compiler_params=params(),
-    )(head, code, gates, back, *streams)
-
-
-def combine_kernel(plan, flag_ref, code_ref, gates_ref, acc_ref, pick_ref, back_ref, late_ref, out_ref):
-    code = code_ref[...]
-    gates = gates_ref[...]
+        compiler_params=params(28),
+    )(head, flag, code, gates, back, late, *streams)
+
+
+def combine_kernel(gates_ref, acc_ref, pick_ref, back_ref, out_ref):
     owners, rows, step = back_ref.shape
     flat = back_ref[...].reshape(owners * rows, step)
-    total = acc_ref[...] + gated(gates, [pick_ref[0], pick_ref[1]], flat)
+    total = acc_ref[...]
+    for j in range(2):
+        total = total + gates_ref[:, j:j + 1] * contract(pick_ref[j], flat, ((1,), (0,)))
     out_ref[...] = total.astype(BF16)
 
-    @pl.when(flag_ref[0] > 0)
-    def _():
-        late = late_ref[...].reshape(owners * plan.back[2], step)
-        more = gated(gates, choices(code, plan, 2, owners), late)
-        out_ref[...] = (total + more).astype(BF16)
-
-
-def combine(flag, code, gates, acc, picks, back, late, plan):
+
+def combine(gates, acc, picks, back):
     tokens, width = acc.shape
-    owners = back.shape[0]
+    owners, rows, _ = back.shape
     step = min(512, width)
 
     def whole(x):
@@ -644,22 +692,19 @@
 
     narrow = pl.BlockSpec((tokens, step), lambda d: (0, d))
     return pl.pallas_call(
-        functools.partial(combine_kernel, plan),
+        combine_kernel,
         name="combine",
         grid=(width // step,),
         in_specs=[
-            SMEM,
-            whole(code),
             whole(gates),
             narrow,
             whole(picks),
-            pl.BlockSpec((owners, plan.back[1], step), lambda d: (0, 0, d)),
-            pl.BlockSpec((owners, plan.back[2], step), lambda d: (0, 0, d)),
+            pl.BlockSpec((owners, rows, step), lambda d: (0, 0, d)),
         ],
         out_specs=narrow,
         out_shape=jax.ShapeDtypeStruct((tokens, width), BF16),
-        compiler_params=params(),
-    )(flag, code, gates, acc, picks, back, late)
+        compiler_params=params(20),
+    )(gates, in_hbm(acc), in_hbm(picks), in_vmem(back))
 
 
 def batch_columns(meta, expert, local_experts, plan):
@@ -803,8 +848,9 @@
         return pl.BlockSpec(x.shape, lambda e, f: (0,) * len(x.shape))
 
     in_spec = pl.BlockSpec((None, width, step), lambda e, f: (first + e, 0, f))
-    extra = [] if base is None else [base]
-    outs = [jax.ShapeDtypeStruct((owners, plan.back[k], width), BF16) for k in given]
+    extra = [] if base is None else [in_hbm(base)]
+    outs = [pltpu.HBM((owners, plan.back[k], width), BF16) for k in given]
+    received = [in_vmem(x) if k == 1 else in_hbm(x) for k, x in zip(taken, received)]
     batch = owners * CAP
     return pl.pallas_call(
         functools.partial(
@@ -826,7 +872,7 @@
             pltpu.VMEM((batch, width), F32),
             pltpu.VMEM((count, batch, width), BF16),
         ],
-        compiler_params=params(),
+        compiler_params=params(44),
     )(flag, meta, gain, *received, w_gate, w_up, w_down, *extra)
 
 
@@ -835,7 +881,7 @@
 
 
 def everywhere_if(flag, x):
-    return lax.cond(flag[0] > 0, everywhere, lambda y: y, x)
+    return lax.cond(flag[0] > 0, everywhere, lambda y: unset(y.shape), x)
 
 
 def body_dense(
@@ -925,7 +971,7 @@
     cut = columns_by_turn(head, residual_in, parts)
     residuals = turned(cut, 1)
     local = local_attention(queries, keys, values, route_row, route_col)
-    meta, flag, parcels, streams = mix_and_pack(
+    meta, flag, parcels, own_streams = mix_and_pack(
         head,
         queries,
         carried,
@@ -934,27 +980,38 @@
         route_col,
         head_gain[None],
         residuals,
-        spreads,
+        spreads[0],
         local_experts,
         plan,
     )
     weights = (w_gate, w_up, w_down)
     gain = ffn_gain[None]
-    received = [everywhere(parcels[0])]
-    received.append(everywhere(parcels[1]))
-    streams = turned(streams, -1)
+    received = [everywhere(parcels)]
+    parcels = pack(1, spreads[1], own_streams, contexts * parts, plan)
+    received.append(everywhere(parcels))
+    streams = turned(own_streams, -1)
     back_0, base = serve_experts(
         flag, meta, gain, parts, received[:1], weights, None, 0, (0,), (0, 1), plan
     )
-    received.append(everywhere_if(flag, parcels[2]))
+    received.append(
+        lax.cond(
+            flag[0] > 0,
+            lambda spread, pieces: everywhere(pack(2, spread, pieces, contexts * parts, plan)),
+            lambda spread, pieces: unset(
+                (contexts * parts, parts * plan.out[2], pieces[0].shape[1])
+            ),
+            spreads[2],
+            own_streams,
+        )
+    )
     back_0 = everywhere(back_0)
     back_1, back_2 = serve_experts(
         flag, meta, gain, parts, received, weights, base, plan.ahead, (0, 1, 2), (1, 2), plan
     )
     back_2 = everywhere_if(flag, back_2)
     back_1 = everywhere(back_1)
-    acc, picks = combine_ahead(head, code, expert_gates, back_0, streams, plan)
-    return combine(flag, code, expert_gates, acc, picks, back_1, back_2, plan)
+    acc, picks = combine_ahead(head, flag, code, expert_gates, back_0, back_2, streams, plan)
+    return combine(expert_gates, acc, picks, back_1)
 
 
 def body(*args):

time: 259 us -> 249 us (0.961)
  blocking collectives: 84.8 us -> 29.6 us
  waiting for transfers between devices: 53 us -> 102 us
  starting transfers between devices: 26.5 us -> 33 us
  local copies, waits for them, and re-layouts: 7.66 us -> 2.52 us
  Pallas kernels: 84.9 us -> 80 us
    all_to_all x2 -> x1, blocking collectives: 84.8 us -> 29.6 us  [everywhere(): lax.all_to_all(x, ('ctx', 'head'), split_axis=0, concat_axis=0, tiled=True)]
    all_to_all x2 -> x3, waiting for transfers between devices: 15.6 us -> 60 us  [everywhere(): lax.all_to_all(x, ('ctx', 'head'), split_axis=0, concat_axis=0, tiled=True)]
    all_to_all x2 -> x3, starting transfers between devices: 7.46 us -> 14 us  [everywhere(): lax.all_to_all(x, ('ctx', 'head'), split_axis=0, concat_axis=0, tiled=True)]
    unnamed x31 -> x23, local copies, waits for them, and re-layouts: 6.59 us -> 2.3 us
    pallas_call x1, Pallas kernels: 9.03 us -> 5.75 us  [mix_and_pack(): pl.pallas_call(functools.partial(mix_pack_kernel, parts, local_experts, p...]
    ppermute x9, waiting for transfers between devices: 34.6 us -> 37.2 us  [turned(): lax.ppermute(pieces[s], 'head', [(h, (h + step * s) % parts) for h in ran...]
    pallas_call x1 -> x4, Pallas kernels: 5.75 us -> 7.34 us  [the longest x1 4.58 us: combine(): pl.pallas_call(combine_kernel, name='combine', grid=(width // step,), in_...]
  transfers between devices with their start and end apart: 13 -> 14, of which waited for: 9 -> 11; matrix products, arithmetic and copies ran while one was open for 1% -> 0% of each run, Pallas kernels for 16% -> 17%
where the time goes in v3:
time: 249 us; the launch traced here: 248 us
  waiting for transfers between devices  102 us (41%)
  Pallas kernels  80 us (32%)
  starting transfers between devices  33 us (13%)
  blocking collectives  29.6 us (12%)
  local copies, waits for them, and re-layouts  2.52 us (1%)
    all_to_all x3, waiting for transfers between devices, everywhere(): lax.all_to_all(x, ('ctx', 'head'), split_axis=0, concat_axis=0, tiled=True)  60 us
    pallas_call x2, Pallas kernels, serve_experts(): pl.pallas_call(functools.partial(expert_kernel, first, taken, given, base...  43.7 us
    ppermute x9, waiting for transfers between devices, turned(): lax.ppermute(pieces[s], 'head', [(h, (h + step * s) % parts) for h in ran...  37.2 us
    all_to_all x1, blocking collectives, everywhere(): lax.all_to_all(x, ('ctx', 'head'), split_axis=0, concat_axis=0, tiled=True)  29.6 us
    all_to_all x3, starting transfers between devices, everywhere(): lax.all_to_all(x, ('ctx', 'head'), split_axis=0, concat_axis=0, tiled=True)  14 us
    ppermute x9, starting transfers between devices, turned(): lax.ppermute(pieces[s], 'head', [(h, (h + step * s) % parts) for h in ran...  8.02 us
    all_to_all x1, starting transfers between devices, body_compact(): lax.all_to_all(states, 'ctx', split_axis=0, concat_axis=0, tiled=True)  7.44 us
    pallas_call x1, Pallas kernels, route(): pl.pallas_call(functools.partial(route_kernel, local_experts, plan, parts...  6.12 us
  transfers between devices with their start and end apart: 14, of which 11 were waited for; matrix products, arithmetic and copies ran while one was open for 0% of the time, Pallas kernels for 17%

profile of v3, /device:TPU:0, one launch (start us, length us, event | category | flops | bytes accessed | tf_op | source)
XLA Modules:
  0.0 247.7 jit_solution(5594247836572468868)
XLA Ops:
  0.0 4.4 %block_states.1 = bf16[2048,128]{1,0:T(8,128)(2,1)} custom-call(bf16[1024,512]{1,0:T(8,128)(2,1)} %key_ref.3, bf16[1024,512]{1,0:T(8,128)(2,1)} %value_ref.3, s32[1,1024]{1,0:T(1,128)} %bitcast.8), custom_call_target="tpu_custom_call" | custom-call | tf_op jit(solution)/shard_map/block_states/pallas_call | solution.py:49
  4.4 7.4 %all-to-all-start.2 = ((bf16[8,256,128]{2,1,0:T(8,128)(2,1)}), bf16[8,256,128]{2,1,0:T(8,128)(2,1)S(1)}, u32[]{:S(2)}, u32[]{:S(2)}) async-start(bf16[8,256,128]{2,1,0:T(8,128)(2,1)} %bitcast.18), calls=%async_computation.2 | async-start | bytes 1048576 | tf_op jit(solution)/shard_map/all_to_all | solution.py:967
  11.9 1.6 collective-permute-start.1
  16.2 6.1 %route.1 = (s32[256,128]{1,0:T(8,128)}, f32[8,8,128]{2,1,0:T(8,128)S(1)}, bf16[4,512,256]{2,1,0:T(8,128)(2,1)}, bf16[4,256,256]{2,1,0:T(8,128)(2,1)}, bf16[4,256,256]{2,1,0:T(8,128)(2,1)}) custom-call(s32[1]{0:T(128)} %bitcast.head_ref, s32[2,256]{1,0:T(2,128)S(1)} %bitcast.17, s32[2,256]{1,0:T(2,128)S(1)} %collective-permute-done.refs_1_, ...), custom_call_target="tpu_custom_call" | custom-call | tf_op jit(solution)/shard_map/route/pallas_call | solution.py:430
  22.3 4.0 %all-to-all-done.2.piece_ref = bf16[8,256,128]{2,1,0:T(8,128)(2,1)S(1)} async-done(((bf16[8,256,128]{2,1,0:T(8,128)(2,1)}), bf16[8,256,128]{2,1,0:T(8,128)(2,1)S(1)}, u32[]{:S(2)}, u32[]{:S(2)}) %all-to-all-start.2) | async-done | bytes 524320 | tf_op jit(solution)/shard_map/all_to_all | solution.py:967
  27.2 3.6 %all-to-all-start.3 = ((bf16[8,264,128]{2,1,0:T(8,128)(2,1)}), bf16[8,264,128]{2,1,0:T(8,128)(2,1)S(1)}, u32[]{:S(2)}, u32[]{:S(2)}) async-start(bf16[8,264,128]{2,1,0:T(8,128)(2,1)} %prefix_with_counts.1), calls=%async_computation.3 | async-start | bytes 1081344 | tf_op jit(solution)/shard_map/all_to_all | solution.py:970
  35.1 6.0 %local_attention.1.local_ref = f32[1024,512]{1,0:T(8,128)S(1)} custom-call(bf16[1024,512]{1,0:T(8,128)(2,1)} %query_ref.3, bf16[1024,512]{1,0:T(8,128)(2,1)} %key_ref.3, bf16[1024,512]{1,0:T(8,128)(2,1)} %value_ref.3, s32[1,1024]{1,0:T(1,128)S(1)} %bitcast.10, s32[1024,1]{1,0:T(8,128)S(1)} %copy.15.route_col_ref), custom_call_target="tpu_custom_call" | custom-call | tf_op jit(solution)/shard_map/local_attention/pallas_call | solution.py:108
  41.4 4.1 %collective-permute-done.5.refs_3_ = bf16[256,512]{1,0:T(8,128)(2,1)} collective-permute-done((bf16[256,512]{1,0:T(8,128)(2,1)}, bf16[256,512]{1,0:T(8,128)(2,1)}, u32[]{:S(2)}, u32[]{:S(2)}) %collective-permute-start.5) | collective-permute-done | bytes 262176 | tf_op jit(solution)/shard_map/ppermute | solution.py:961
  45.9 5.7 %mix_and_pack.1 = (s32[32,128]{1,0:T(8,128)}, s32[1]{0:T(128)}, bf16[32,64,512]{2,1,0:T(8,128)(2,1)}, bf16[256,512]{1,0:T(8,128)(2,1)}, bf16[256,512]{1,0:T(8,12...) custom-call(s32[1]{0:T(128)} %bitcast.head_ref, bf16[1024,512]{1,0:T(8,128)(2,1)} %query_ref.3, ...), custom_call_target="tpu_custom_call" | custom-call | tf_op jit(solution)/shard_map/mix_and_pack/pallas_call | solution.py:557
  52.3 6.1 %all-to-all-start.4 = ((bf16[32,64,512]{2,1,0:T(8,128)(2,1)}), bf16[32,64,512]{2,1,0:T(8,128)(2,1)S(1)}, u32[]{:S(2)}, u32[]{:S(2)}) async-start(bf16[32,64,512]{2,1,0:T(8,128)(2,1)} %get-tuple-element.58), calls=%async_computation.4 | async-start | bytes 4194304 | tf_op jit(solution)/shard_map/all_to_all | solution.py:880
  58.4 2.8 %shard_map.119 = bf16[32,32,512]{2,1,0:T(8,128)(2,1)} custom-call(bf16[4,256,256]{2,1,0:T(8,128)(2,1)} %get-tuple-element.60.spread_ref, bf16[256,512]{1,0:T(8,128)(2,1)} %get-tuple-element.61.refs_0_, bf16[256,512]{1,0:T(8,128)(2,1)} %get-tuple-element.62.refs_1_, bf16[256,512]{1,0:T(8,128)(2,1)} %get-tuple-element.63.refs_2_, ...), custom_call_target="tpu_custom_call" | custom-call | tf_op jit(solution)/shard_map/pallas_call | solution.py:604
  61.1 46.0 %all-to-all-done.4.refs_0_ = bf16[32,64,512]{2,1,0:T(8,128)(2,1)S(1)} async-done(((bf16[32,64,512]{2,1,0:T(8,128)(2,1)}), bf16[32,64,512]{2,1,0:T(8,128)(2,1)S(1)}, u32[]{:S(2)}, u32[]{:S(2)}) %all-to-all-start.4) | async-done | bytes 2097184 | tf_op jit(solution)/shard_map/all_to_all | solution.py:880
  107.1 4.3 %all-to-all-start.6 = ((bf16[32,32,512]{2,1,0:T(8,128)(2,1)}), bf16[32,32,512]{2,1,0:T(8,128)(2,1)S(1)}, u32[]{:S(2)}, u32[]{:S(2)}) async-start(bf16[32,32,512]{2,1,0:T(8,128)(2,1)} %shard_map.119), calls=%async_computation.6 | async-start | bytes 2097152 | tf_op jit(solution)/shard_map/all_to_all | solution.py:880
  111.4 21.3 %shard_map.118 = (bf16[32,8,2048]{2,1,0:T(8,128)(2,1)}, bf16[32,16,2048]{2,1,0:T(8,128)(2,1)}) custom-call(s32[1]{0:T(128)} %get-tuple-element.55.flag_ref, s32[32,128]{1,0:T(8,128)S(1)} %copy-done.2, f32[1,2048]{1,0:T(1,128)S(1)} %bitcast.11, bf16[32,64,512]{2,1,0:T(8,128)(2,1)} %copy-done.7, bf16[8,2048,512]{2,1,0:T(8,128)(2,1)} %refs_3_.3, ...), custom_call_target="tpu_custom_call" | custom-call | tf_op jit(solution)/shard_map/pallas_call | solution.py:855
  132.7 4.7 %all-to-all-done.6.refs_1_ = bf16[32,32,512]{2,1,0:T(8,128)(2,1)S(1)} async-done(((bf16[32,32,512]{2,1,0:T(8,128)(2,1)}), bf16[32,32,512]{2,1,0:T(8,128)(2,1)S(1)}, u32[]{:S(2)}, u32[]{:S(2)}) %all-to-all-start.6) | async-done | bytes 1048608 | tf_op jit(solution)/shard_map/all_to_all | solution.py:880
  137.4 22.4 %shard_map.120 = (bf16[32,16,2048]{2,1,0:T(8,128)(2,1)}, bf16[32,8,2048]{2,1,0:T(8,128)(2,1)}) custom-call(s32[1]{0:T(128)} %get-tuple-element.55.flag_ref, s32[32,128]{1,0:T(8,128)S(1)} %copy-done.2, f32[1,2048]{1,0:T(1,128)S(1)} %bitcast.12, bf16[32,64,512]{2,1,0:T(8,128)(2,1)} %copy-done.7, bf16[32,32,512]{2,1,0:T(8,128)(2,1)S(1)} %all-to-all-done.6.refs_1_, ...), custom_call_target="tpu_custom_call" | custom-call | tf_op jit(solution)/shard_map/pallas_call | solution.py:855
  161.0 29.6 %all_to_all.44.back_ref = bf16[32,8,2048]{2,1,0:T(8,128)(2,1)S(1)} all-to-all(bf16[32,8,2048]{2,1,0:T(8,128)(2,1)S(1)} %copy-done.8), channel_id=1, replica_groups=mesh['ctx'=8,'head'=4] {'ctx','head'}, dimensions={0} | all-to-all | bytes 2097152 | tf_op jit(solution)/shard_map/all_to_all | solution.py:880
  190.6 3.6 %all-to-all-start.7 = ((bf16[32,16,2048]{2,1,0:T(8,128)(2,1)}), bf16[32,16,2048]{2,1,0:T(8,128)(2,1)S(1)}, u32[]{:S(2)}, u32[]{:S(2)}) async-start(bf16[32,16,2048]{2,1,0:T(8,128)(2,1)} %get-tuple-element.70), calls=%async_computation.7 | async-start | bytes 4194304 | tf_op jit(solution)/shard_map/all_to_all | solution.py:880
  194.3 1.5 collective-permute-start.6
  196.5 22.0 %collective-permute-done.6.refs_1_ = bf16[256,512]{1,0:T(8,128)(2,1)S(1)} collective-permute-done((bf16[256,512]{1,0:T(8,128)(2,1)}, bf16[256,512]{1,0:T(8,128)(2,1)S(1)}, u32[]{:S(2)}, u32[]{:S(2)}) %collective-permute-start.6) | collective-permute-done | bytes 262176 | tf_op jit(solution)/shard_map/ppermute | solution.py:961
  218.5 9.6 %collective-permute-done.7.refs_2_ = bf16[256,512]{1,0:T(8,128)(2,1)} collective-permute-done((bf16[256,512]{1,0:T(8,128)(2,1)}, bf16[256,512]{1,0:T(8,128)(2,1)}, u32[]{:S(2)}, u32[]{:S(2)}) %collective-permute-start.7) | collective-permute-done | bytes 262176 | tf_op jit(solution)/shard_map/ppermute | solution.py:961
  229.0 4.8 %combine_ahead.1 = (f32[256,2048]{1,0:T(8,128)}, bf16[2,256,512]{2,1,0:T(8,128)(2,1)}) custom-call(s32[1]{0:T(128)} %bitcast.head_ref, s32[1]{0:T(128)} %get-tuple-element.55.flag_ref, s32[256,128]{1,0:T(8,128)S(1)} %copy-done.1, f32[256,2]{1,0:T(8,128)S(1)} %copy.18.gates_ref, bf16[32,8,2048]{2,1,0:T(8,128)(2,1)S(1)} %all_to_all.44.back_ref, ...), custom_call_target="tpu_custom_call" | custom-call | tf_op jit(solution)/shard_map/combine_ahead/pallas_call | solution.py:663
  233.8 9.3 %all-to-all-done.7.back_ref = bf16[32,16,2048]{2,1,0:T(8,128)(2,1)S(1)} async-done(((bf16[32,16,2048]{2,1,0:T(8,128)(2,1)}), bf16[32,16,2048]{2,1,0:T(8,128)(2,1)S(1)}, u32[]{:S(2)}, u32[]{:S(2)}) %all-to-all-start.7) | async-done | bytes 2097184 | tf_op jit(solution)/shard_map/all_to_all | solution.py:880
  243.1 4.6 %combine.1 = bf16[256,2048]{1,0:T(8,128)(2,1)} custom-call(f32[256,2]{1,0:T(8,128)S(1)} %copy.18.gates_ref, f32[256,2048]{1,0:T(8,128)} %get-tuple-element.68.acc_ref, bf16[2,256,512]{2,1,0:T(8,128)(2,1)} %get-tuple-element.69.pick_ref, bf16[32,16,2048]{2,1,0:T(8,128)(2,1)S(1)} %all-to-all-done.7.back_ref), custom_call_target="tpu_custom_call" | custom-call | tf_op jit(solution)/shard_map/combine/pallas_call | solution.py:694
  (44 shorter events, 11.3 us)
Async XLA Ops:
  0.0 11.8 %copy-start.6 = (s32[256,2]{0,1:T(2,128)S(1)}, s32[256,2]{0,1:T(2,128)}, u32[]{:S(2)}) copy-start(s32[256,2]{0,1:T(2,128)} %param.23) | copy-start | bytes 6148
  4.4 26.5 %copy-start = (bf16[256,2048]{1,0:T(8,128)(2,1)S(1)}, bf16[256,2048]{1,0:T(8,128)(2,1)}, u32[]{:S(2)}) copy-start(bf16[256,2048]{1,0:T(8,128)(2,1)} %whole_ref.1) | copy-start | bytes 3145732
  4.4 30.5 %copy-start.3 = (s32[1024]{0:T(1024)S(1)}, s32[1024]{0:T(1024)}, u32[]{:S(2)}) copy-start(s32[1024]{0:T(1024)} %param.19) | copy-start | bytes 12292
  4.4 21.9 %all-to-all-start.2 = ((bf16[8,256,128]{2,1,0:T(8,128)(2,1)}), bf16[8,256,128]{2,1,0:T(8,128)(2,1)S(1)}, u32[]{:S(2)}, u32[]{:S(2)}) async-start(bf16[8,256,128]{2,1,0:T(8,128)(2,1)} %bitcast.18), calls=%async_computation.2 | async-start | bytes 1048576 | tf_op jit(solution)/shard_map/all_to_all | solution.py:967
  11.8 3.1 %collective-permute-start = (s32[2,256]{1,0:T(2,128)S(1)}, s32[2,256]{1,0:T(2,128)S(1)}, u32[]{:S(2)}, u32[]{:S(2)}) collective-permute-start(s32[2,256]{1,0:T(2,128)S(1)} %bitcast.14), channel_id=1, source_target_pairs={{0,1},{1,2},{2,3},{3,0},{4,5},{5,6},{6,7},{7,4},{8,9},{9,10},{10,1... | collective-permute-start | bytes 6152 | tf_op jit(solution)/shard_map/ppermute | solution.py:961
  11.9 3.7 %collective-permute-start.1 = (s32[2,256]{1,0:T(2,128)S(1)}, s32[2,256]{1,0:T(2,128)S(1)}, u32[]{:S(2)}, u32[]{:S(2)}) collective-permute-start(s32[2,256]{1,0:T(2,128)S(1)} %bitcast.15), channel_id=1, source_target_pairs={{0,2},{1,3},{2,0},{3,1},{4,6},{5,7},{6,4},{7,5},{8,10},{9,11},{10,... | collective-permute-start | bytes 6152 | tf_op jit(solution)/shard_map/ppermute | solution.py:961
  13.5 2.7 %collective-permute-start.2 = (s32[2,256]{1,0:T(2,128)S(1)}, s32[2,256]{1,0:T(2,128)S(1)}, u32[]{:S(2)}, u32[]{:S(2)}) collective-permute-start(s32[2,256]{1,0:T(2,128)S(1)} %bitcast.16), channel_id=1, source_target_pairs={{0,3},{1,0},{2,1},{3,2},{4,7},{5,4},{6,5},{7,6},{8,11},{9,8},{10,9... | collective-permute-start | bytes 6152 | tf_op jit(solution)/shard_map/ppermute | solution.py:961
  27.2 18.7 %all-to-all-start.3 = ((bf16[8,264,128]{2,1,0:T(8,128)(2,1)}), bf16[8,264,128]{2,1,0:T(8,128)(2,1)S(1)}, u32[]{:S(2)}, u32[]{:S(2)}) async-start(bf16[8,264,128]{2,1,0:T(8,128)(2,1)} %prefix_with_counts.1), calls=%async_computation.3 | async-start | bytes 1081344 | tf_op jit(solution)/shard_map/all_to_all | solution.py:970
  31.9 9.3 %collective-permute-start.3 = (bf16[256,512]{1,0:T(8,128)(2,1)}, bf16[256,512]{1,0:T(8,128)(2,1)S(1)}, u32[]{:S(2)}, u32[]{:S(2)}) collective-permute-start(bf16[256,512]{1,0:T(8,128)(2,1)} %get-tuple-element.51), channel_id=1, source_target_pairs={{0,1},{1,2},{2,3},{3,0},{4,5},{5,6},{6,7},{7,4},{8,9},{9,10},{10,1... | collective-permute-start | bytes 786440 | tf_op jit(solution)/shard_map/ppermute | solution.py:961
  31.9 9.5 %collective-permute-start.4 = (bf16[256,512]{1,0:T(8,128)(2,1)}, bf16[256,512]{1,0:T(8,128)(2,1)}, u32[]{:S(2)}, u32[]{:S(2)}) collective-permute-start(bf16[256,512]{1,0:T(8,128)(2,1)} %get-tuple-element.52), channel_id=1, source_target_pairs={{0,2},{1,3},{2,0},{3,1},{4,6},{5,7},{6,4},{7,5},{8,10},{9,11},{10,... | collective-permute-start | bytes 786440 | tf_op jit(solution)/shard_map/ppermute | solution.py:961
  33.4 12.1 %collective-permute-start.5 = (bf16[256,512]{1,0:T(8,128)(2,1)}, bf16[256,512]{1,0:T(8,128)(2,1)}, u32[]{:S(2)}, u32[]{:S(2)}) collective-permute-start(bf16[256,512]{1,0:T(8,128)(2,1)} %get-tuple-element.53), channel_id=1, source_target_pairs={{0,3},{1,0},{2,1},{3,2},{4,7},{5,4},{6,5},{7,6},{8,11},{9,8},{10,9... | collective-permute-start | bytes 786440 | tf_op jit(solution)/shard_map/ppermute | solution.py:961
  35.1 10.7 %copy-start.5 = (f32[512]{0:T(512)S(1)}, f32[512]{0:T(512)}, u32[]{:S(2)}) copy-start(f32[512]{0:T(512)} %param.20) | copy-start | bytes 6148
  41.2 4.7 %copy-start.9 = (bf16[256,512]{1,0:T(8,128)(2,1)}, bf16[256,512]{1,0:T(8,128)(2,1)S(1)}, u32[]{:S(2)}) copy-start(bf16[256,512]{1,0:T(8,128)(2,1)S(1)} %collective-permute-done.3.refs_1_) | copy-start | bytes 786436
  52.3 54.8 %all-to-all-start.4 = ((bf16[32,64,512]{2,1,0:T(8,128)(2,1)}), bf16[32,64,512]{2,1,0:T(8,128)(2,1)S(1)}, u32[]{:S(2)}, u32[]{:S(2)}) async-start(bf16[32,64,512]{2,1,0:T(8,128)(2,1)} %get-tuple-element.58), calls=%async_computation.4 | async-start | bytes 4194304 | tf_op jit(solution)/shard_map/all_to_all | solution.py:880
  58.4 53.0 %copy-start.2 = (s32[32,128]{1,0:T(8,128)S(1)}, s32[32,128]{1,0:T(8,128)}, u32[]{:S(2)}) copy-start(s32[32,128]{1,0:T(8,128)} %get-tuple-element.57.meta_ref) | copy-start | bytes 49156
  58.4 53.0 %copy-start.4 = (f32[2048]{0:T(1024)S(1)}, f32[2048]{0:T(1024)}, u32[]{:S(2)}) copy-start(f32[2048]{0:T(1024)} %param.22) | copy-start | bytes 24580
  107.1 4.3 %copy-start.7 = (bf16[32,64,512]{2,1,0:T(8,128)(2,1)}, bf16[32,64,512]{2,1,0:T(8,128)(2,1)S(1)}, u32[]{:S(2)}) copy-start(bf16[32,64,512]{2,1,0:T(8,128)(2,1)S(1)} %all-to-all-done.4.refs_0_) | copy-start | bytes 6291460
  107.1 30.3 %all-to-all-start.6 = ((bf16[32,32,512]{2,1,0:T(8,128)(2,1)}), bf16[32,32,512]{2,1,0:T(8,128)(2,1)S(1)}, u32[]{:S(2)}, u32[]{:S(2)}) async-start(bf16[32,32,512]{2,1,0:T(8,128)(2,1)} %shard_map.119), calls=%async_computation.6 | async-start | bytes 2097152 | tf_op jit(solution)/shard_map/all_to_all | solution.py:880
  159.8 1.2 copy-start.8
  190.6 5.7 %copy-start.10 = (f32[256,2]{0,1:T(2,128)S(1)}, f32[256,2]{0,1:T(2,128)}, u32[]{:S(2)}) copy-start(f32[256,2]{0,1:T(2,128)} %param.24) | copy-start | bytes 6148
  190.6 52.5 %all-to-all-start.7 = ((bf16[32,16,2048]{2,1,0:T(8,128)(2,1)}), bf16[32,16,2048]{2,1,0:T(8,128)(2,1)S(1)}, u32[]{:S(2)}, u32[]{:S(2)}) async-start(bf16[32,16,2048]{2,1,0:T(8,128)(2,1)} %get-tuple-element.70), calls=%async_computation.7 | async-start | bytes 4194304 | tf_op jit(solution)/shard_map/all_to_all | solution.py:880
  194.3 24.2 %collective-permute-start.6 = (bf16[256,512]{1,0:T(8,128)(2,1)}, bf16[256,512]{1,0:T(8,128)(2,1)S(1)}, u32[]{:S(2)}, u32[]{:S(2)}) collective-permute-start(bf16[256,512]{1,0:T(8,128)(2,1)} %get-tuple-element.62.refs_1_), channel_id=1, source_target_pairs={{0,3},{1,0},{2,1},{3,2},{4,7},{5,4},{6,5},{7,6},{8,11},{9,8},{10,9... | collective-permute-start | bytes 786440 | tf_op jit(solution)/shard_map/ppermute | solution.py:961
  195.8 32.3 %collective-permute-start.7 = (bf16[256,512]{1,0:T(8,128)(2,1)}, bf16[256,512]{1,0:T(8,128)(2,1)}, u32[]{:S(2)}, u32[]{:S(2)}) collective-permute-start(bf16[256,512]{1,0:T(8,128)(2,1)} %get-tuple-element.63.refs_2_), channel_id=1, source_target_pairs={{0,2},{1,3},{2,0},{3,1},{4,6},{5,7},{6,4},{7,5},{8,10},{9,11},{10,... | collective-permute-start | bytes 786440 | tf_op jit(solution)/shard_map/ppermute | solution.py:961
  196.2 31.9 %collective-permute-start.8 = (bf16[256,512]{1,0:T(8,128)(2,1)}, bf16[256,512]{1,0:T(8,128)(2,1)}, u32[]{:S(2)}, u32[]{:S(2)}) collective-permute-start(bf16[256,512]{1,0:T(8,128)(2,1)} %get-tuple-element.64.refs_3_), channel_id=1, source_target_pairs={{0,1},{1,2},{2,3},{3,0},{4,5},{5,6},{6,7},{7,4},{8,9},{9,10},{10,1... | collective-permute-start | bytes 786440 | tf_op jit(solution)/shard_map/ppermute | solution.py:961
  (1 other events, 0.9 us)

commit v4 on v3

--- a/solution.py
+++ b/solution.py
@@ -341,13 +341,70 @@
 SMEM = pl.BlockSpec(memory_space=pltpu.SMEM)
 
 
-def route_kernel(local_experts, plan, parts, head_ref, *refs):
-    id_refs, (code_ref, meta_ref), spread_refs = refs[:parts], refs[parts:parts + 2], refs[parts + 2:]
+def id_columns(id_refs):
+    parts = len(id_refs)
+    pad = -2 * parts % 8
+    rows = [ref[...].astype(F32) for ref in id_refs]
+    if pad:
+        rows.append(jnp.zeros((pad, id_refs[0].shape[1]), F32))
+    rows = jnp.concatenate(rows, axis=0)
+    return rows, rows.T
+
+
+def counts_kernel(local_experts, plan, parts, head_ref, *refs):
+    id_refs, meta_ref = refs[:parts], refs[parts]
     tokens = id_refs[0].shape[1]
     contexts = meta_ref.shape[0]
     owners = contexts * parts
-    experts = owners * local_experts
     head = head_ref[0]
+    owner_lane = lax.broadcasted_iota(jnp.int32, (tokens, owners), 1)
+    local_lane = lax.broadcasted_iota(jnp.int32, (tokens, HD), 1)
+    owner_row = lax.broadcasted_iota(jnp.int32, (contexts, owners), 1)
+    context_row = lax.broadcasted_iota(jnp.int32, (contexts, owners), 0)
+    mine = jnp.where(owner_row == context_row * parts + head, 1.0, 0.0).astype(BF16)
+    lane = lax.broadcasted_iota(jnp.int32, (owners, HD), 1)
+    _, id_cols = id_columns(id_refs)
+    flags = 0.0
+    metas = []
+    for b in range(parts):
+        counts = 0.0
+        for j in range(2):
+            ids = id_cols[:, 2 * b + j:2 * b + j + 1].astype(jnp.int32)
+            counts = counts + contract(
+                (ids // local_experts == owner_lane).astype(F32).astype(BF16),
+                (ids % local_experts == local_lane).astype(F32).astype(BF16),
+                ((0,), (0,)),
+            )
+        total = jnp.sum(counts, axis=1, keepdims=True)
+        front = jnp.sum(jnp.where(lane < plan.ahead, counts, 0.0), axis=1, keepdims=True)
+        over = (total > sum(plan.out[:2])) | (
+            total - jnp.minimum(front, plan.back[0]) > plan.back[1]
+        )
+        flags = jnp.maximum(flags, jnp.max(jnp.where(over, 1.0, 0.0), axis=0, keepdims=True))
+        metas.append(contract(mine, counts.astype(BF16), ((1,), (0,))))
+    meta_lane = lax.broadcasted_iota(jnp.int32, (contexts, HD), 1)
+    meta_ref[...] = jnp.zeros(meta_ref.shape, F32)
+    for b in range(parts):
+        marked = jnp.where(meta_lane == local_experts, flags, metas[b])
+        for c in range(contexts):
+            meta_ref[c, b:b + 1, :] = marked[c:c + 1]
+
+
+def count_choices(head, ids, contexts, local_experts, plan):
+    parts = len(ids)
+    return pl.pallas_call(
+        functools.partial(counts_kernel, local_experts, plan, parts),
+        name="count_choices",
+        in_specs=[SMEM] + [VMEM] * parts,
+        out_specs=VMEM,
+        out_shape=jax.ShapeDtypeStruct((contexts, parts + -parts % 8, HD), F32),
+        compiler_params=params(16),
+    )(head, *ids)
+
+
+def route_kernel(local_experts, experts, plan, parts, *refs):
+    id_refs, code_ref, spread_refs = refs[:parts], refs[parts], refs[parts + 1:]
+    tokens = id_refs[0].shape[1]
     t = lax.broadcasted_iota(jnp.int32, (tokens, tokens), 0)
     s = lax.broadcasted_iota(jnp.int32, (tokens, tokens), 1)
     earlier_mask = (t > s).astype(F32).astype(BF16)
@@ -357,17 +414,7 @@
     below = jnp.where(mates & (row < col), 1.0, 0.0).astype(BF16)
     ahead = jnp.where(mates & (row % local_experts < plan.ahead), 1.0, 0.0).astype(BF16)
     lanes = lax.broadcasted_iota(jnp.int32, (tokens, experts), 1)
-    owner_lane = lax.broadcasted_iota(jnp.int32, (tokens, owners), 1)
-    local_lane = lax.broadcasted_iota(jnp.int32, (tokens, HD), 1)
-    owner_row = lax.broadcasted_iota(jnp.int32, (contexts, owners), 1)
-    context_row = lax.broadcasted_iota(jnp.int32, (contexts, owners), 0)
-    mine = jnp.where(owner_row == context_row * parts + head, 1.0, 0.0).astype(BF16)
-    lane = lax.broadcasted_iota(jnp.int32, (owners, HD), 1)
-    pair_rows = [ref[...].astype(F32) for ref in id_refs]
-    id_rows = jnp.concatenate(pair_rows + [jnp.zeros((-2 * parts % 8, tokens), F32)] * (2 * parts % 8 > 0), axis=0)
-    id_cols = id_rows.T
-    flags = 0.0
-    metas = []
+    id_rows, id_cols = id_columns(id_refs)
     for b in range(parts):
         ids = [id_cols[:, 2 * b + j:2 * b + j + 1].astype(jnp.int32) for j in range(2)]
         chosen = [(i == lanes).astype(F32) for i in ids]
@@ -377,13 +424,6 @@
         places = [jnp.sum(position * c, axis=1, keepdims=True) for c in chosen]
         wide = jnp.concatenate(places + [jnp.zeros((tokens, HD - 2), F32)], axis=1)
         place_rows = wide.T[0:8]
-        parcel_counts = 0.0
-        for j in range(2):
-            parcel_counts = parcel_counts + contract(
-                (ids[j] // local_experts == owner_lane).astype(F32).astype(BF16),
-                (ids[j] % local_experts == local_lane).astype(F32).astype(BF16),
-                ((0,), (0,)),
-            )
         if b == 0:
             aheads = contract(counts, ahead, ((1,), (0,)))[0:1]
             slot_lane = lax.broadcasted_iota(jnp.int32, code_ref.shape, 1)
@@ -408,37 +448,21 @@
                 index = in_round(place_rows[j:j + 1].astype(jnp.int32), plan.out, k, owner)
                 hit = (slot == index) if hit is None else hit | (slot == index)
             spread_ref[b] = jnp.where(hit, 1.0, 0.0).astype(BF16)
-        total = jnp.sum(parcel_counts, axis=1, keepdims=True)
-        front = jnp.sum(jnp.where(lane < plan.ahead, parcel_counts, 0.0), axis=1, keepdims=True)
-        over = (total > sum(plan.out[:2])) | (
-            total - jnp.minimum(front, plan.back[0]) > plan.back[1]
-        )
-        flags = jnp.maximum(flags, jnp.max(jnp.where(over, 1.0, 0.0), axis=0, keepdims=True))
-        metas.append(contract(mine, parcel_counts.astype(BF16), ((1,), (0,))))
-    meta_lane = lax.broadcasted_iota(jnp.int32, (contexts, HD), 1)
-    meta_ref[...] = jnp.zeros(meta_ref.shape, F32)
-    for b in range(parts):
-        marked = jnp.where(meta_lane == local_experts, flags, metas[b])
-        for c in range(contexts):
-            meta_ref[c, b:b + 1, :] = marked[c:c + 1]
-
-
-def route(head, ids, contexts, local_experts, plan):
+
+
+def route(ids, contexts, local_experts, plan):
     parts = len(ids)
     tokens = ids[0].shape[1]
     owners = contexts * parts
     return pl.pallas_call(
-        functools.partial(route_kernel, local_experts, plan, parts),
+        functools.partial(route_kernel, local_experts, owners * local_experts, plan, parts),
         name="route",
-        in_specs=[SMEM] + [VMEM] * parts,
-        out_specs=[VMEM] * 5,
-        out_shape=[
-            pltpu.HBM((tokens, HD), jnp.int32),
-            jax.ShapeDtypeStruct((contexts, parts + -parts % 8, HD), F32),
-        ]
+        in_specs=[VMEM] * parts,
+        out_specs=[VMEM] * 4,
+        out_shape=[pltpu.HBM((tokens, HD), jnp.int32)]
         + [pltpu.HBM((parts, owners * rows, tokens), BF16) for rows in plan.out],
         compiler_params=params(24),
-    )(head, *ids)
+    )(*ids)
 
 
 def prefix_with_counts_kernel(piece_ref, meta_ref, out_ref):
@@ -674,8 +698,10 @@
 
 
 def combine_kernel(gates_ref, acc_ref, pick_ref, back_ref, out_ref):
-    owners, rows, step = back_ref.shape
-    flat = back_ref[...].reshape(owners * rows, step)
+    owners, rows, _ = back_ref.shape
+    step = out_ref.shape[1]
+    start = pl.multiple_of(pl.program_id(0) * step, step)
+    flat = back_ref[:, :, pl.ds(start, step)].reshape(owners * rows, step)
     total = acc_ref[...]
     for j in range(2):
         total = total + gates_ref[:, j:j + 1] * contract(pick_ref[j], flat, ((1,), (0,)))
@@ -684,7 +710,6 @@
 
 def combine(gates, acc, picks, back):
     tokens, width = acc.shape
-    owners, rows, _ = back.shape
     step = min(512, width)
 
     def whole(x):
@@ -699,7 +724,7 @@
             whole(gates),
             narrow,
             whole(picks),
-            pl.BlockSpec((owners, rows, step), lambda d: (0, 0, d)),
+            VMEM,
         ],
         out_specs=narrow,
         out_shape=jax.ShapeDtypeStruct((tokens, width), BF16),
@@ -965,11 +990,12 @@
     ids = turned([expert_ids.T] * parts, 1)
     states = block_states(keys, values, route_row)
     pieces = lax.all_to_all(states, "ctx", split_axis=0, concat_axis=0, tiled=True)
-    code, counts, *spreads = route(head, ids, contexts, local_experts, plan)
+    counts = count_choices(head, ids, contexts, local_experts, plan)
     before = prefix_with_counts(pieces.reshape(contexts, -1, HD), counts)
     carried = lax.all_to_all(before, "ctx", split_axis=0, concat_axis=0, tiled=True)
     cut = columns_by_turn(head, residual_in, parts)
     residuals = turned(cut, 1)
+    code, *spreads = route(ids, contexts, local_experts, plan)
     local = local_attention(queries, keys, values, route_row, route_col)
     meta, flag, parcels, own_streams = mix_and_pack(
         head,

time: 249 us -> 249 us (level)
    all_to_all x1, waiting for transfers between devices: 4.04 us -> 8.21 us  [body_compact(): lax.all_to_all(states, 'ctx', split_axis=0, concat_axis=0, tiled=True)]
    ppermute x9, waiting for transfers between devices: 37.2 us -> 33.6 us  [turned(): lax.ppermute(pieces[s], 'head', [(h, (h + step * s) % parts) for h in ran...]
    pallas_call x1 -> x2, Pallas kernels: 6.12 us -> 5.62 us  [the longest x1 3.67 us: route(): pl.pallas_call(functools.partial(route_kernel, local_experts, owners * lo...]
where the time goes in v4:
time: 249 us; the launch traced here: 248 us
  waiting for transfers between devices  102 us (41%)
  Pallas kernels  79.5 us (32%)
  starting transfers between devices  33 us (13%)
  blocking collectives  29.6 us (12%)
  local copies, waits for them, and re-layouts  2.52 us (1%)
    all_to_all x3, waiting for transfers between devices, everywhere(): lax.all_to_all(x, ('ctx', 'head'), split_axis=0, concat_axis=0, tiled=True)  60 us
    pallas_call x2, Pallas kernels, serve_experts(): pl.pallas_call(functools.partial(expert_kernel, first, taken, given, base...  43.7 us
    ppermute x9, waiting for transfers between devices, turned(): lax.ppermute(pieces[s], 'head', [(h, (h + step * s) % parts) for h in ran...  33.6 us
    all_to_all x1, blocking collectives, everywhere(): lax.all_to_all(x, ('ctx', 'head'), split_axis=0, concat_axis=0, tiled=True)  29.6 us
    all_to_all x3, starting transfers between devices, everywhere(): lax.all_to_all(x, ('ctx', 'head'), split_axis=0, concat_axis=0, tiled=True)  14 us
    all_to_all x1, waiting for transfers between devices, body_compact(): lax.all_to_all(states, 'ctx', split_axis=0, concat_axis=0, tiled=True)  8.21 us
    ppermute x9, starting transfers between devices, turned(): lax.ppermute(pieces[s], 'head', [(h, (h + step * s) % parts) for h in ran...  8 us
    all_to_all x1, starting transfers between devices, body_compact(): lax.all_to_all(states, 'ctx', split_axis=0, concat_axis=0, tiled=True)  7.44 us
  transfers between devices with their start and end apart: 14, of which 11 were waited for; matrix products, arithmetic and copies ran while one was open for 0% of the time, Pallas kernels for 17%

profile of v4, /device:TPU:0, one launch (start us, length us, event | category | flops | bytes accessed | tf_op | source)
XLA Modules:
  0.0 247.7 jit_solution(14465206366321108262)
XLA Ops:
  0.0 4.4 %block_states.1 = bf16[2048,128]{1,0:T(8,128)(2,1)} custom-call(bf16[1024,512]{1,0:T(8,128)(2,1)} %key_ref.3, bf16[1024,512]{1,0:T(8,128)(2,1)} %value_ref.3, s32[1,1024]{1,0:T(1,128)} %bitcast.8), custom_call_target="tpu_custom_call" | custom-call | tf_op jit(solution)/shard_map/block_states/pallas_call | solution.py:49
  4.4 7.4 %all-to-all-start.2 = ((bf16[8,256,128]{2,1,0:T(8,128)(2,1)}), bf16[8,256,128]{2,1,0:T(8,128)(2,1)S(1)}, u32[]{:S(2)}, u32[]{:S(2)}) async-start(bf16[8,256,128]{2,1,0:T(8,128)(2,1)} %bitcast.19), calls=%async_computation.2 | async-start | bytes 1048576 | tf_op jit(solution)/shard_map/all_to_all | solution.py:992
  11.9 1.6 collective-permute-start.1
  16.2 2.0 count_choices.1.meta_ref
  18.1 8.2 %all-to-all-done.2.piece_ref = bf16[8,256,128]{2,1,0:T(8,128)(2,1)S(1)} async-done(((bf16[8,256,128]{2,1,0:T(8,128)(2,1)}), bf16[8,256,128]{2,1,0:T(8,128)(2,1)S(1)}, u32[]{:S(2)}, u32[]{:S(2)}) %all-to-all-start.2) | async-done | bytes 524320 | tf_op jit(solution)/shard_map/all_to_all | solution.py:992
  27.2 3.6 %all-to-all-start.3 = ((bf16[8,264,128]{2,1,0:T(8,128)(2,1)}), bf16[8,264,128]{2,1,0:T(8,128)(2,1)S(1)}, u32[]{:S(2)}, u32[]{:S(2)}) async-start(bf16[8,264,128]{2,1,0:T(8,128)(2,1)} %prefix_with_counts.1), calls=%async_computation.3 | async-start | bytes 1081344 | tf_op jit(solution)/shard_map/all_to_all | solution.py:995
  35.2 6.0 %local_attention.1.local_ref = f32[1024,512]{1,0:T(8,128)S(1)} custom-call(bf16[1024,512]{1,0:T(8,128)(2,1)} %query_ref.3, bf16[1024,512]{1,0:T(8,128)(2,1)} %key_ref.3, bf16[1024,512]{1,0:T(8,128)(2,1)} %value_ref.3, s32[1,1024]{1,0:T(1,128)S(1)} %bitcast.10, s32[1024,1]{1,0:T(8,128)S(1)} %copy.15.route_col_ref), custom_call_target="tpu_custom_call" | custom-call | tf_op jit(solution)/shard_map/local_attention/pallas_call | solution.py:108
  41.2 3.7 %route.1 = (s32[256,128]{1,0:T(8,128)}, bf16[4,512,256]{2,1,0:T(8,128)(2,1)}, bf16[4,256,256]{2,1,0:T(8,128)(2,1)}, bf16[4,256,256]{2,1,0:T(8,128)(2,1)}) custom-call(s32[2,256]{1,0:T(2,128)S(1)} %bitcast.17, s32[2,256]{1,0:T(2,128)S(1)} %collective-permute-done.refs_1_, s32[2,256]{1,0:T(2,128)S(1)} %collective-permute-done.1.refs_2_, ...), custom_call_target="tpu_custom_call" | custom-call | tf_op jit(solution)/shard_map/route/pallas_call | solution.py:457
  45.9 5.7 %mix_and_pack.1 = (s32[32,128]{1,0:T(8,128)}, s32[1]{0:T(128)}, bf16[32,64,512]{2,1,0:T(8,128)(2,1)}, bf16[256,512]{1,0:T(8,128)(2,1)}, bf16[256,512]{1,0:T(8,12...) custom-call(s32[1]{0:T(128)} %bitcast.head_ref, bf16[1024,512]{1,0:T(8,128)(2,1)} %query_ref.3, ...), custom_call_target="tpu_custom_call" | custom-call | tf_op jit(solution)/shard_map/mix_and_pack/pallas_call | solution.py:581
  52.3 6.1 %all-to-all-start.4 = ((bf16[32,64,512]{2,1,0:T(8,128)(2,1)}), bf16[32,64,512]{2,1,0:T(8,128)(2,1)S(1)}, u32[]{:S(2)}, u32[]{:S(2)}) async-start(bf16[32,64,512]{2,1,0:T(8,128)(2,1)} %get-tuple-element.56), calls=%async_computation.4 | async-start | bytes 4194304 | tf_op jit(solution)/shard_map/all_to_all | solution.py:905
  58.4 2.8 %shard_map.119 = bf16[32,32,512]{2,1,0:T(8,128)(2,1)} custom-call(bf16[4,256,256]{2,1,0:T(8,128)(2,1)} %get-tuple-element.58.spread_ref, bf16[256,512]{1,0:T(8,128)(2,1)} %get-tuple-element.59.refs_0_, bf16[256,512]{1,0:T(8,128)(2,1)} %get-tuple-element.60.refs_1_, bf16[256,512]{1,0:T(8,128)(2,1)} %get-tuple-element.61.refs_2_, ...), custom_call_target="tpu_custom_call" | custom-call | tf_op jit(solution)/shard_map/pallas_call | solution.py:628
  61.2 46.0 %all-to-all-done.4.refs_0_ = bf16[32,64,512]{2,1,0:T(8,128)(2,1)S(1)} async-done(((bf16[32,64,512]{2,1,0:T(8,128)(2,1)}), bf16[32,64,512]{2,1,0:T(8,128)(2,1)S(1)}, u32[]{:S(2)}, u32[]{:S(2)}) %all-to-all-start.4) | async-done | bytes 2097184 | tf_op jit(solution)/shard_map/all_to_all | solution.py:905
  107.1 4.3 %all-to-all-start.6 = ((bf16[32,32,512]{2,1,0:T(8,128)(2,1)}), bf16[32,32,512]{2,1,0:T(8,128)(2,1)S(1)}, u32[]{:S(2)}, u32[]{:S(2)}) async-start(bf16[32,32,512]{2,1,0:T(8,128)(2,1)} %shard_map.119), calls=%async_computation.6 | async-start | bytes 2097152 | tf_op jit(solution)/shard_map/all_to_all | solution.py:905
  111.4 21.3 %shard_map.118 = (bf16[32,8,2048]{2,1,0:T(8,128)(2,1)}, bf16[32,16,2048]{2,1,0:T(8,128)(2,1)}) custom-call(s32[1]{0:T(128)} %get-tuple-element.53.flag_ref, s32[32,128]{1,0:T(8,128)S(1)} %copy-done.2, f32[1,2048]{1,0:T(1,128)S(1)} %bitcast.11, bf16[32,64,512]{2,1,0:T(8,128)(2,1)} %copy-done.7, bf16[8,2048,512]{2,1,0:T(8,128)(2,1)} %refs_3_.3, ...), custom_call_target="tpu_custom_call" | custom-call | tf_op jit(solution)/shard_map/pallas_call | solution.py:880
  132.7 4.7 %all-to-all-done.6.refs_1_ = bf16[32,32,512]{2,1,0:T(8,128)(2,1)S(1)} async-done(((bf16[32,32,512]{2,1,0:T(8,128)(2,1)}), bf16[32,32,512]{2,1,0:T(8,128)(2,1)S(1)}, u32[]{:S(2)}, u32[]{:S(2)}) %all-to-all-start.6) | async-done | bytes 1048608 | tf_op jit(solution)/shard_map/all_to_all | solution.py:905
  137.4 22.4 %shard_map.120 = (bf16[32,16,2048]{2,1,0:T(8,128)(2,1)}, bf16[32,8,2048]{2,1,0:T(8,128)(2,1)}) custom-call(s32[1]{0:T(128)} %get-tuple-element.53.flag_ref, s32[32,128]{1,0:T(8,128)S(1)} %copy-done.2, f32[1,2048]{1,0:T(1,128)S(1)} %bitcast.12, bf16[32,64,512]{2,1,0:T(8,128)(2,1)} %copy-done.7, bf16[32,32,512]{2,1,0:T(8,128)(2,1)S(1)} %all-to-all-done.6.refs_1_, ...), custom_call_target="tpu_custom_call" | custom-call | tf_op jit(solution)/shard_map/pallas_call | solution.py:880
  161.0 29.6 %all_to_all.44.back_ref = bf16[32,8,2048]{2,1,0:T(8,128)(2,1)S(1)} all-to-all(bf16[32,8,2048]{2,1,0:T(8,128)(2,1)S(1)} %copy-done.8), channel_id=1, replica_groups=mesh['ctx'=8,'head'=4] {'ctx','head'}, dimensions={0} | all-to-all | bytes 2097152 | tf_op jit(solution)/shard_map/all_to_all | solution.py:905
  190.7 3.6 %all-to-all-start.7 = ((bf16[32,16,2048]{2,1,0:T(8,128)(2,1)}), bf16[32,16,2048]{2,1,0:T(8,128)(2,1)S(1)}, u32[]{:S(2)}, u32[]{:S(2)}) async-start(bf16[32,16,2048]{2,1,0:T(8,128)(2,1)} %get-tuple-element.68), calls=%async_computation.7 | async-start | bytes 4194304 | tf_op jit(solution)/shard_map/all_to_all | solution.py:905
  194.3 1.5 collective-permute-start.6
  196.5 22.0 %collective-permute-done.6.refs_1_ = bf16[256,512]{1,0:T(8,128)(2,1)S(1)} collective-permute-done((bf16[256,512]{1,0:T(8,128)(2,1)}, bf16[256,512]{1,0:T(8,128)(2,1)S(1)}, u32[]{:S(2)}, u32[]{:S(2)}) %collective-permute-start.6) | collective-permute-done | bytes 262176 | tf_op jit(solution)/shard_map/ppermute | solution.py:986
  218.5 9.6 %collective-permute-done.7.refs_2_ = bf16[256,512]{1,0:T(8,128)(2,1)} collective-permute-done((bf16[256,512]{1,0:T(8,128)(2,1)}, bf16[256,512]{1,0:T(8,128)(2,1)}, u32[]{:S(2)}, u32[]{:S(2)}) %collective-permute-start.7) | collective-permute-done | bytes 262176 | tf_op jit(solution)/shard_map/ppermute | solution.py:986
  229.0 4.8 %combine_ahead.1 = (f32[256,2048]{1,0:T(8,128)}, bf16[2,256,512]{2,1,0:T(8,128)(2,1)}) custom-call(s32[1]{0:T(128)} %bitcast.head_ref, s32[1]{0:T(128)} %get-tuple-element.53.flag_ref, s32[256,128]{1,0:T(8,128)S(1)} %copy-done.1, f32[256,2]{1,0:T(8,128)S(1)} %copy.18.gates_ref, bf16[32,8,2048]{2,1,0:T(8,128)(2,1)S(1)} %all_to_all.44.back_ref, ...), custom_call_target="tpu_custom_call" | custom-call | tf_op jit(solution)/shard_map/combine_ahead/pallas_call | solution.py:687
  233.8 9.3 %all-to-all-done.7.back_ref = bf16[32,16,2048]{2,1,0:T(8,128)(2,1)S(1)} async-done(((bf16[32,16,2048]{2,1,0:T(8,128)(2,1)}), bf16[32,16,2048]{2,1,0:T(8,128)(2,1)S(1)}, u32[]{:S(2)}, u32[]{:S(2)}) %all-to-all-start.7) | async-done | bytes 2097184 | tf_op jit(solution)/shard_map/all_to_all | solution.py:905
  243.1 4.6 %combine.1 = bf16[256,2048]{1,0:T(8,128)(2,1)} custom-call(f32[256,2]{1,0:T(8,128)S(1)} %copy.18.gates_ref, f32[256,2048]{1,0:T(8,128)} %get-tuple-element.66.acc_ref, bf16[2,256,512]{2,1,0:T(8,128)(2,1)} %get-tuple-element.67.pick_ref, bf16[32,16,2048]{2,1,0:T(8,128)(2,1)S(1)} %all-to-all-done.7.back_ref), custom_call_target="tpu_custom_call" | custom-call | tf_op jit(solution)/shard_map/combine/pallas_call | solution.py:719
  (45 shorter events, 11.7 us)
Async XLA Ops:
  0.0 11.9 %copy-start.5 = (s32[256,2]{0,1:T(2,128)S(1)}, s32[256,2]{0,1:T(2,128)}, u32[]{:S(2)}) copy-start(s32[256,2]{0,1:T(2,128)} %param.23) | copy-start | bytes 6148
  4.4 26.5 %copy-start = (bf16[256,2048]{1,0:T(8,128)(2,1)S(1)}, bf16[256,2048]{1,0:T(8,128)(2,1)}, u32[]{:S(2)}) copy-start(bf16[256,2048]{1,0:T(8,128)(2,1)} %whole_ref.1) | copy-start | bytes 3145732
  4.4 30.5 %copy-start.3 = (s32[1024]{0:T(1024)S(1)}, s32[1024]{0:T(1024)}, u32[]{:S(2)}) copy-start(s32[1024]{0:T(1024)} %param.19) | copy-start | bytes 12292
  4.4 21.9 %all-to-all-start.2 = ((bf16[8,256,128]{2,1,0:T(8,128)(2,1)}), bf16[8,256,128]{2,1,0:T(8,128)(2,1)S(1)}, u32[]{:S(2)}, u32[]{:S(2)}) async-start(bf16[8,256,128]{2,1,0:T(8,128)(2,1)} %bitcast.19), calls=%async_computation.2 | async-start | bytes 1048576 | tf_op jit(solution)/shard_map/all_to_all | solution.py:992
  11.9 3.1 %collective-permute-start = (s32[2,256]{1,0:T(2,128)S(1)}, s32[2,256]{1,0:T(2,128)S(1)}, u32[]{:S(2)}, u32[]{:S(2)}) collective-permute-start(s32[2,256]{1,0:T(2,128)S(1)} %bitcast.13), channel_id=1, source_target_pairs={{0,1},{1,2},{2,3},{3,0},{4,5},{5,6},{6,7},{7,4},{8,9},{9,10},{10,1... | collective-permute-start | bytes 6152 | tf_op jit(solution)/shard_map/ppermute | solution.py:986
  11.9 3.7 %collective-permute-start.1 = (s32[2,256]{1,0:T(2,128)S(1)}, s32[2,256]{1,0:T(2,128)S(1)}, u32[]{:S(2)}, u32[]{:S(2)}) collective-permute-start(s32[2,256]{1,0:T(2,128)S(1)} %bitcast.14), channel_id=1, source_target_pairs={{0,2},{1,3},{2,0},{3,1},{4,6},{5,7},{6,4},{7,5},{8,10},{9,11},{10,... | collective-permute-start | bytes 6152 | tf_op jit(solution)/shard_map/ppermute | solution.py:986
  13.5 2.7 %collective-permute-start.2 = (s32[2,256]{1,0:T(2,128)S(1)}, s32[2,256]{1,0:T(2,128)S(1)}, u32[]{:S(2)}, u32[]{:S(2)}) collective-permute-start(s32[2,256]{1,0:T(2,128)S(1)} %bitcast.15), channel_id=1, source_target_pairs={{0,3},{1,0},{2,1},{3,2},{4,7},{5,4},{6,5},{7,6},{8,11},{9,8},{10,9... | collective-permute-start | bytes 6152 | tf_op jit(solution)/shard_map/ppermute | solution.py:986
  27.2 18.7 %all-to-all-start.3 = ((bf16[8,264,128]{2,1,0:T(8,128)(2,1)}), bf16[8,264,128]{2,1,0:T(8,128)(2,1)S(1)}, u32[]{:S(2)}, u32[]{:S(2)}) async-start(bf16[8,264,128]{2,1,0:T(8,128)(2,1)} %prefix_with_counts.1), calls=%async_computation.3 | async-start | bytes 1081344 | tf_op jit(solution)/shard_map/all_to_all | solution.py:995
  32.0 12.9 %collective-permute-start.3 = (bf16[256,512]{1,0:T(8,128)(2,1)}, bf16[256,512]{1,0:T(8,128)(2,1)S(1)}, u32[]{:S(2)}, u32[]{:S(2)}) collective-permute-start(bf16[256,512]{1,0:T(8,128)(2,1)} %get-tuple-element.49), channel_id=1, source_target_pairs={{0,1},{1,2},{2,3},{3,0},{4,5},{5,6},{6,7},{7,4},{8,9},{9,10},{10,1... | collective-permute-start | bytes 786440 | tf_op jit(solution)/shard_map/ppermute | solution.py:986
  32.0 12.9 %collective-permute-start.4 = (bf16[256,512]{1,0:T(8,128)(2,1)}, bf16[256,512]{1,0:T(8,128)(2,1)}, u32[]{:S(2)}, u32[]{:S(2)}) collective-permute-start(bf16[256,512]{1,0:T(8,128)(2,1)} %get-tuple-element.50), channel_id=1, source_target_pairs={{0,2},{1,3},{2,0},{3,1},{4,6},{5,7},{6,4},{7,5},{8,10},{9,11},{10,... | collective-permute-start | bytes 786440 | tf_op jit(solution)/shard_map/ppermute | solution.py:986
  33.4 12.1 %collective-permute-start.5 = (bf16[256,512]{1,0:T(8,128)(2,1)}, bf16[256,512]{1,0:T(8,128)(2,1)}, u32[]{:S(2)}, u32[]{:S(2)}) collective-permute-start(bf16[256,512]{1,0:T(8,128)(2,1)} %get-tuple-element.51), channel_id=1, source_target_pairs={{0,3},{1,0},{2,1},{3,2},{4,7},{5,4},{6,5},{7,6},{8,11},{9,8},{10,9... | collective-permute-start | bytes 786440 | tf_op jit(solution)/shard_map/ppermute | solution.py:986
  35.1 10.7 %copy-start.6 = (f32[512]{0:T(512)S(1)}, f32[512]{0:T(512)}, u32[]{:S(2)}) copy-start(f32[512]{0:T(512)} %param.20) | copy-start | bytes 6148
  44.9 1.0 copy-start.9
  52.3 54.8 %all-to-all-start.4 = ((bf16[32,64,512]{2,1,0:T(8,128)(2,1)}), bf16[32,64,512]{2,1,0:T(8,128)(2,1)S(1)}, u32[]{:S(2)}, u32[]{:S(2)}) async-start(bf16[32,64,512]{2,1,0:T(8,128)(2,1)} %get-tuple-element.56), calls=%async_computation.4 | async-start | bytes 4194304 | tf_op jit(solution)/shard_map/all_to_all | solution.py:905
  58.4 53.0 %copy-start.2 = (s32[32,128]{1,0:T(8,128)S(1)}, s32[32,128]{1,0:T(8,128)}, u32[]{:S(2)}) copy-start(s32[32,128]{1,0:T(8,128)} %get-tuple-element.55.meta_ref) | copy-start | bytes 49156
  58.4 53.0 %copy-start.4 = (f32[2048]{0:T(1024)S(1)}, f32[2048]{0:T(1024)}, u32[]{:S(2)}) copy-start(f32[2048]{0:T(1024)} %param.22) | copy-start | bytes 24580
  107.1 4.3 %copy-start.7 = (bf16[32,64,512]{2,1,0:T(8,128)(2,1)}, bf16[32,64,512]{2,1,0:T(8,128)(2,1)S(1)}, u32[]{:S(2)}) copy-start(bf16[32,64,512]{2,1,0:T(8,128)(2,1)S(1)} %all-to-all-done.4.refs_0_) | copy-start | bytes 6291460
  107.1 30.3 %all-to-all-start.6 = ((bf16[32,32,512]{2,1,0:T(8,128)(2,1)}), bf16[32,32,512]{2,1,0:T(8,128)(2,1)S(1)}, u32[]{:S(2)}, u32[]{:S(2)}) async-start(bf16[32,32,512]{2,1,0:T(8,128)(2,1)} %shard_map.119), calls=%async_computation.6 | async-start | bytes 2097152 | tf_op jit(solution)/shard_map/all_to_all | solution.py:905
  159.8 1.2 copy-start.8
  190.7 5.7 %copy-start.10 = (f32[256,2]{0,1:T(2,128)S(1)}, f32[256,2]{0,1:T(2,128)}, u32[]{:S(2)}) copy-start(f32[256,2]{0,1:T(2,128)} %param.24) | copy-start | bytes 6148
  190.7 52.5 %all-to-all-start.7 = ((bf16[32,16,2048]{2,1,0:T(8,128)(2,1)}), bf16[32,16,2048]{2,1,0:T(8,128)(2,1)S(1)}, u32[]{:S(2)}, u32[]{:S(2)}) async-start(bf16[32,16,2048]{2,1,0:T(8,128)(2,1)} %get-tuple-element.68), calls=%async_computation.7 | async-start | bytes 4194304 | tf_op jit(solution)/shard_map/all_to_all | solution.py:905
  194.3 24.2 %collective-permute-start.6 = (bf16[256,512]{1,0:T(8,128)(2,1)}, bf16[256,512]{1,0:T(8,128)(2,1)S(1)}, u32[]{:S(2)}, u32[]{:S(2)}) collective-permute-start(bf16[256,512]{1,0:T(8,128)(2,1)} %get-tuple-element.60.refs_1_), channel_id=1, source_target_pairs={{0,3},{1,0},{2,1},{3,2},{4,7},{5,4},{6,5},{7,6},{8,11},{9,8},{10,9... | collective-permute-start | bytes 786440 | tf_op jit(solution)/shard_map/ppermute | solution.py:986
  195.8 32.3 %collective-permute-start.7 = (bf16[256,512]{1,0:T(8,128)(2,1)}, bf16[256,512]{1,0:T(8,128)(2,1)}, u32[]{:S(2)}, u32[]{:S(2)}) collective-permute-start(bf16[256,512]{1,0:T(8,128)(2,1)} %get-tuple-element.61.refs_2_), channel_id=1, source_target_pairs={{0,2},{1,3},{2,0},{3,1},{4,6},{5,7},{6,4},{7,5},{8,10},{9,11},{10,... | collective-permute-start | bytes 786440 | tf_op jit(solution)/shard_map/ppermute | solution.py:986
  196.2 31.9 %collective-permute-start.8 = (bf16[256,512]{1,0:T(8,128)(2,1)}, bf16[256,512]{1,0:T(8,128)(2,1)}, u32[]{:S(2)}, u32[]{:S(2)}) collective-permute-start(bf16[256,512]{1,0:T(8,128)(2,1)} %get-tuple-element.62.refs_3_), channel_id=1, source_target_pairs={{0,1},{1,2},{2,3},{3,0},{4,5},{5,6},{6,7},{7,4},{8,9},{9,10},{10,1... | collective-permute-start | bytes 786440 | tf_op jit(solution)/shard_map/ppermute | solution.py:986
  (1 other events, 0.9 us)

commit v5 on v4

--- a/solution.py
+++ b/solution.py
@@ -35,27 +35,30 @@
 
 
 def state_kernel(key_ref, value_ref, route_ref, out_ref):
-    keys_t = key_ref[...].T
-    values = value_ref[...]
     route = route_ref[...]
-    for m in range(M):
-        mask = (route == m).astype(F32).astype(BF16)
-        out_ref[pl.ds(m * HD, HD), :] = contract(keys_t * mask, values, ((1,), (0,))).astype(BF16)
+    masks = [(route == m).astype(F32).astype(BF16) for m in range(M)]
+    for h in range(key_ref.shape[1] // HD):
+        keys_t = key_ref[:, h * HD:(h + 1) * HD].T
+        values = value_ref[:, h * HD:(h + 1) * HD]
+        for m in range(M):
+            found = contract(keys_t * masks[m], values, ((1,), (0,)))
+            out_ref[pl.ds((h * M + m) * HD, HD), :] = found.astype(BF16)
 
 
 def block_states(keys, values, route_row):
     length, width = keys.shape
     heads = width // HD
+    together = 2 if heads % 2 == 0 else 1
     return pl.pallas_call(
         state_kernel,
         name="block_states",
-        grid=(heads,),
+        grid=(heads // together,),
         in_specs=[
-            pl.BlockSpec((length, HD), lambda h: (0, h)),
-            pl.BlockSpec((length, HD), lambda h: (0, h)),
+            pl.BlockSpec((length, together * HD), lambda h: (0, h)),
+            pl.BlockSpec((length, together * HD), lambda h: (0, h)),
             pl.BlockSpec((1, length), lambda h: (0, 0)),
         ],
-        out_specs=pl.BlockSpec((M * HD, HD), lambda h: (h, 0)),
+        out_specs=pl.BlockSpec((together * M * HD, HD), lambda h: (h, 0)),
         out_shape=pltpu.HBM((heads * M * HD, HD), BF16),
         compiler_params=params(16),
     )(in_hbm(keys), in_hbm(values), in_hbm(route_row))
@@ -710,7 +713,7 @@
 
 def combine(gates, acc, picks, back):
     tokens, width = acc.shape
-    step = min(512, width)
+    step = min(1024, width)
 
     def whole(x):
         return pl.BlockSpec(x.shape, lambda d: (0,) * len(x.shape))

time: 249 us -> 247 us (level)
  transfers between devices with their start and end apart: 14 -> 14, of which waited for: 11 -> 10; matrix products, arithmetic and copies ran while one was open for 0% -> 0% of each run, Pallas kernels for 17% -> 17%
where the time goes in v5:
time: 247 us; the launch traced here: 246 us
  waiting for transfers between devices  102 us (41%)
  Pallas kernels  77.6 us (31%)
  starting transfers between devices  33 us (13%)
  blocking collectives  29.6 us (12%)
  local copies, waits for them, and re-layouts  2.52 us (1%)
    all_to_all x3, waiting for transfers between devices, everywhere(): lax.all_to_all(x, ('ctx', 'head'), split_axis=0, concat_axis=0, tiled=True)  60 us
    pallas_call x2, Pallas kernels, serve_experts(): pl.pallas_call(functools.partial(expert_kernel, first, taken, given, base...  43.7 us
    ppermute x9, waiting for transfers between devices, turned(): lax.ppermute(pieces[s], 'head', [(h, (h + step * s) % parts) for h in ran...  33.6 us
    all_to_all x1, blocking collectives, everywhere(): lax.all_to_all(x, ('ctx', 'head'), split_axis=0, concat_axis=0, tiled=True)  29.6 us
    all_to_all x3, starting transfers between devices, everywhere(): lax.all_to_all(x, ('ctx', 'head'), split_axis=0, concat_axis=0, tiled=True)  14 us
    all_to_all x1, waiting for transfers between devices, body_compact(): lax.all_to_all(states, 'ctx', split_axis=0, concat_axis=0, tiled=True)  8.2 us
    ppermute x9, starting transfers between devices, turned(): lax.ppermute(pieces[s], 'head', [(h, (h + step * s) % parts) for h in ran...  8.01 us
    all_to_all x1, starting transfers between devices, body_compact(): lax.all_to_all(states, 'ctx', split_axis=0, concat_axis=0, tiled=True)  7.44 us
  transfers between devices with their start and end apart: 14, of which 10 were waited for; matrix products, arithmetic and copies ran while one was open for 0% of the time, Pallas kernels for 17%

profile of v5, /device:TPU:0, one launch (start us, length us, event | category | flops | bytes accessed | tf_op | source)
XLA Modules:
  0.0 245.8 jit_solution(8901861756318508903)
XLA Ops:
  0.0 3.5 %block_states.1 = bf16[2048,128]{1,0:T(8,128)(2,1)} custom-call(bf16[1024,512]{1,0:T(8,128)(2,1)} %key_ref.3, bf16[1024,512]{1,0:T(8,128)(2,1)} %value_ref.3, s32[1,1024]{1,0:T(1,128)} %bitcast.8), custom_call_target="tpu_custom_call" | custom-call | tf_op jit(solution)/shard_map/block_states/pallas_call | solution.py:52
  3.5 7.4 %all-to-all-start.2 = ((bf16[8,256,128]{2,1,0:T(8,128)(2,1)}), bf16[8,256,128]{2,1,0:T(8,128)(2,1)S(1)}, u32[]{:S(2)}, u32[]{:S(2)}) async-start(bf16[8,256,128]{2,1,0:T(8,128)(2,1)} %bitcast.19), calls=%async_computation.2 | async-start | bytes 1048576 | tf_op jit(solution)/shard_map/all_to_all | solution.py:995
  11.0 1.6 collective-permute-start.1
  15.2 2.0 count_choices.1.meta_ref
  17.2 8.2 %all-to-all-done.2.piece_ref = bf16[8,256,128]{2,1,0:T(8,128)(2,1)S(1)} async-done(((bf16[8,256,128]{2,1,0:T(8,128)(2,1)}), bf16[8,256,128]{2,1,0:T(8,128)(2,1)S(1)}, u32[]{:S(2)}, u32[]{:S(2)}) %all-to-all-start.2) | async-done | bytes 524320 | tf_op jit(solution)/shard_map/all_to_all | solution.py:995
  26.3 3.6 %all-to-all-start.3 = ((bf16[8,264,128]{2,1,0:T(8,128)(2,1)}), bf16[8,264,128]{2,1,0:T(8,128)(2,1)S(1)}, u32[]{:S(2)}, u32[]{:S(2)}) async-start(bf16[8,264,128]{2,1,0:T(8,128)(2,1)} %prefix_with_counts.1), calls=%async_computation.3 | async-start | bytes 1081344 | tf_op jit(solution)/shard_map/all_to_all | solution.py:998
  34.2 6.0 %local_attention.1.local_ref = f32[1024,512]{1,0:T(8,128)S(1)} custom-call(bf16[1024,512]{1,0:T(8,128)(2,1)} %query_ref.3, bf16[1024,512]{1,0:T(8,128)(2,1)} %key_ref.3, bf16[1024,512]{1,0:T(8,128)(2,1)} %value_ref.3, s32[1,1024]{1,0:T(1,128)S(1)} %bitcast.10, s32[1024,1]{1,0:T(8,128)S(1)} %copy.15.route_col_ref), custom_call_target="tpu_custom_call" | custom-call | tf_op jit(solution)/shard_map/local_attention/pallas_call | solution.py:111
  40.3 3.7 %route.1 = (s32[256,128]{1,0:T(8,128)}, bf16[4,512,256]{2,1,0:T(8,128)(2,1)}, bf16[4,256,256]{2,1,0:T(8,128)(2,1)}, bf16[4,256,256]{2,1,0:T(8,128)(2,1)}) custom-call(s32[2,256]{1,0:T(2,128)S(1)} %bitcast.17, s32[2,256]{1,0:T(2,128)S(1)} %collective-permute-done.refs_1_, s32[2,256]{1,0:T(2,128)S(1)} %collective-permute-done.1.refs_2_, ...), custom_call_target="tpu_custom_call" | custom-call | tf_op jit(solution)/shard_map/route/pallas_call | solution.py:460
  44.9 5.7 %mix_and_pack.1 = (s32[32,128]{1,0:T(8,128)}, s32[1]{0:T(128)}, bf16[32,64,512]{2,1,0:T(8,128)(2,1)}, bf16[256,512]{1,0:T(8,128)(2,1)}, bf16[256,512]{1,0:T(8,12...) custom-call(s32[1]{0:T(128)} %bitcast.head_ref, bf16[1024,512]{1,0:T(8,128)(2,1)} %query_ref.3, ...), custom_call_target="tpu_custom_call" | custom-call | tf_op jit(solution)/shard_map/mix_and_pack/pallas_call | solution.py:584
  51.4 6.1 %all-to-all-start.4 = ((bf16[32,64,512]{2,1,0:T(8,128)(2,1)}), bf16[32,64,512]{2,1,0:T(8,128)(2,1)S(1)}, u32[]{:S(2)}, u32[]{:S(2)}) async-start(bf16[32,64,512]{2,1,0:T(8,128)(2,1)} %get-tuple-element.56), calls=%async_computation.4 | async-start | bytes 4194304 | tf_op jit(solution)/shard_map/all_to_all | solution.py:908
  57.5 2.8 %shard_map.119 = bf16[32,32,512]{2,1,0:T(8,128)(2,1)} custom-call(bf16[4,256,256]{2,1,0:T(8,128)(2,1)} %get-tuple-element.58.spread_ref, bf16[256,512]{1,0:T(8,128)(2,1)} %get-tuple-element.59.refs_0_, bf16[256,512]{1,0:T(8,128)(2,1)} %get-tuple-element.60.refs_1_, bf16[256,512]{1,0:T(8,128)(2,1)} %get-tuple-element.61.refs_2_, ...), custom_call_target="tpu_custom_call" | custom-call | tf_op jit(solution)/shard_map/pallas_call | solution.py:631
  60.2 46.0 %all-to-all-done.4.refs_0_ = bf16[32,64,512]{2,1,0:T(8,128)(2,1)S(1)} async-done(((bf16[32,64,512]{2,1,0:T(8,128)(2,1)}), bf16[32,64,512]{2,1,0:T(8,128)(2,1)S(1)}, u32[]{:S(2)}, u32[]{:S(2)}) %all-to-all-start.4) | async-done | bytes 2097184 | tf_op jit(solution)/shard_map/all_to_all | solution.py:908
  106.2 4.3 %all-to-all-start.6 = ((bf16[32,32,512]{2,1,0:T(8,128)(2,1)}), bf16[32,32,512]{2,1,0:T(8,128)(2,1)S(1)}, u32[]{:S(2)}, u32[]{:S(2)}) async-start(bf16[32,32,512]{2,1,0:T(8,128)(2,1)} %shard_map.119), calls=%async_computation.6 | async-start | bytes 2097152 | tf_op jit(solution)/shard_map/all_to_all | solution.py:908
  110.5 21.3 %shard_map.118 = (bf16[32,8,2048]{2,1,0:T(8,128)(2,1)}, bf16[32,16,2048]{2,1,0:T(8,128)(2,1)}) custom-call(s32[1]{0:T(128)} %get-tuple-element.53.flag_ref, s32[32,128]{1,0:T(8,128)S(1)} %copy-done.2, f32[1,2048]{1,0:T(1,128)S(1)} %bitcast.11, bf16[32,64,512]{2,1,0:T(8,128)(2,1)} %copy-done.7, bf16[8,2048,512]{2,1,0:T(8,128)(2,1)} %refs_3_.3, ...), custom_call_target="tpu_custom_call" | custom-call | tf_op jit(solution)/shard_map/pallas_call | solution.py:883
  131.7 4.7 %all-to-all-done.6.refs_1_ = bf16[32,32,512]{2,1,0:T(8,128)(2,1)S(1)} async-done(((bf16[32,32,512]{2,1,0:T(8,128)(2,1)}), bf16[32,32,512]{2,1,0:T(8,128)(2,1)S(1)}, u32[]{:S(2)}, u32[]{:S(2)}) %all-to-all-start.6) | async-done | bytes 1048608 | tf_op jit(solution)/shard_map/all_to_all | solution.py:908
  136.5 22.4 %shard_map.120 = (bf16[32,16,2048]{2,1,0:T(8,128)(2,1)}, bf16[32,8,2048]{2,1,0:T(8,128)(2,1)}) custom-call(s32[1]{0:T(128)} %get-tuple-element.53.flag_ref, s32[32,128]{1,0:T(8,128)S(1)} %copy-done.2, f32[1,2048]{1,0:T(1,128)S(1)} %bitcast.12, bf16[32,64,512]{2,1,0:T(8,128)(2,1)} %copy-done.7, bf16[32,32,512]{2,1,0:T(8,128)(2,1)S(1)} %all-to-all-done.6.refs_1_, ...), custom_call_target="tpu_custom_call" | custom-call | tf_op jit(solution)/shard_map/pallas_call | solution.py:883
  160.1 29.6 %all_to_all.44.back_ref = bf16[32,8,2048]{2,1,0:T(8,128)(2,1)S(1)} all-to-all(bf16[32,8,2048]{2,1,0:T(8,128)(2,1)S(1)} %copy-done.8), channel_id=1, replica_groups=mesh['ctx'=8,'head'=4] {'ctx','head'}, dimensions={0} | all-to-all | bytes 2097152 | tf_op jit(solution)/shard_map/all_to_all | solution.py:908
  189.7 3.6 %all-to-all-start.7 = ((bf16[32,16,2048]{2,1,0:T(8,128)(2,1)}), bf16[32,16,2048]{2,1,0:T(8,128)(2,1)S(1)}, u32[]{:S(2)}, u32[]{:S(2)}) async-start(bf16[32,16,2048]{2,1,0:T(8,128)(2,1)} %get-tuple-element.68), calls=%async_computation.7 | async-start | bytes 4194304 | tf_op jit(solution)/shard_map/all_to_all | solution.py:908
  193.3 1.5 collective-permute-start.6
  195.5 22.0 %collective-permute-done.6.refs_1_ = bf16[256,512]{1,0:T(8,128)(2,1)S(1)} collective-permute-done((bf16[256,512]{1,0:T(8,128)(2,1)}, bf16[256,512]{1,0:T(8,128)(2,1)S(1)}, u32[]{:S(2)}, u32[]{:S(2)}) %collective-permute-start.6) | collective-permute-done | bytes 262176 | tf_op jit(solution)/shard_map/ppermute | solution.py:989
  217.5 9.6 %collective-permute-done.7.refs_2_ = bf16[256,512]{1,0:T(8,128)(2,1)} collective-permute-done((bf16[256,512]{1,0:T(8,128)(2,1)}, bf16[256,512]{1,0:T(8,128)(2,1)}, u32[]{:S(2)}, u32[]{:S(2)}) %collective-permute-start.7) | collective-permute-done | bytes 262176 | tf_op jit(solution)/shard_map/ppermute | solution.py:989
  228.1 4.8 %combine_ahead.1 = (f32[256,2048]{1,0:T(8,128)}, bf16[2,256,512]{2,1,0:T(8,128)(2,1)}) custom-call(s32[1]{0:T(128)} %bitcast.head_ref, s32[1]{0:T(128)} %get-tuple-element.53.flag_ref, s32[256,128]{1,0:T(8,128)S(1)} %copy-done.1, f32[256,2]{1,0:T(8,128)S(1)} %copy.18.gates_ref, bf16[32,8,2048]{2,1,0:T(8,128)(2,1)S(1)} %all_to_all.44.back_ref, ...), custom_call_target="tpu_custom_call" | custom-call | tf_op jit(solution)/shard_map/combine_ahead/pallas_call | solution.py:690
  232.9 9.3 %all-to-all-done.7.back_ref = bf16[32,16,2048]{2,1,0:T(8,128)(2,1)S(1)} async-done(((bf16[32,16,2048]{2,1,0:T(8,128)(2,1)}), bf16[32,16,2048]{2,1,0:T(8,128)(2,1)S(1)}, u32[]{:S(2)}, u32[]{:S(2)}) %all-to-all-start.7) | async-done | bytes 2097184 | tf_op jit(solution)/shard_map/all_to_all | solution.py:908
  242.2 3.6 %combine.1 = bf16[256,2048]{1,0:T(8,128)(2,1)} custom-call(f32[256,2]{1,0:T(8,128)S(1)} %copy.18.gates_ref, f32[256,2048]{1,0:T(8,128)} %get-tuple-element.66.acc_ref, bf16[2,256,512]{2,1,0:T(8,128)(2,1)} %get-tuple-element.67.pick_ref, bf16[32,16,2048]{2,1,0:T(8,128)(2,1)S(1)} %all-to-all-done.7.back_ref), custom_call_target="tpu_custom_call" | custom-call | tf_op jit(solution)/shard_map/combine/pallas_call | solution.py:722
  (45 shorter events, 11.7 us)
Async XLA Ops:
  0.0 10.9 %copy-start.5 = (s32[256,2]{0,1:T(2,128)S(1)}, s32[256,2]{0,1:T(2,128)}, u32[]{:S(2)}) copy-start(s32[256,2]{0,1:T(2,128)} %param.23) | copy-start | bytes 6148
  3.5 26.4 %copy-start = (bf16[256,2048]{1,0:T(8,128)(2,1)S(1)}, bf16[256,2048]{1,0:T(8,128)(2,1)}, u32[]{:S(2)}) copy-start(bf16[256,2048]{1,0:T(8,128)(2,1)} %whole_ref.1) | copy-start | bytes 3145732
  3.5 30.5 %copy-start.3 = (s32[1024]{0:T(1024)S(1)}, s32[1024]{0:T(1024)}, u32[]{:S(2)}) copy-start(s32[1024]{0:T(1024)} %param.19) | copy-start | bytes 12292
  3.5 21.9 %all-to-all-start.2 = ((bf16[8,256,128]{2,1,0:T(8,128)(2,1)}), bf16[8,256,128]{2,1,0:T(8,128)(2,1)S(1)}, u32[]{:S(2)}, u32[]{:S(2)}) async-start(bf16[8,256,128]{2,1,0:T(8,128)(2,1)} %bitcast.19), calls=%async_computation.2 | async-start | bytes 1048576 | tf_op jit(solution)/shard_map/all_to_all | solution.py:995
  10.9 3.1 %collective-permute-start = (s32[2,256]{1,0:T(2,128)S(1)}, s32[2,256]{1,0:T(2,128)S(1)}, u32[]{:S(2)}, u32[]{:S(2)}) collective-permute-start(s32[2,256]{1,0:T(2,128)S(1)} %bitcast.13), channel_id=1, source_target_pairs={{0,1},{1,2},{2,3},{3,0},{4,5},{5,6},{6,7},{7,4},{8,9},{9,10},{10,1... | collective-permute-start | bytes 6152 | tf_op jit(solution)/shard_map/ppermute | solution.py:989
  11.0 3.7 %collective-permute-start.1 = (s32[2,256]{1,0:T(2,128)S(1)}, s32[2,256]{1,0:T(2,128)S(1)}, u32[]{:S(2)}, u32[]{:S(2)}) collective-permute-start(s32[2,256]{1,0:T(2,128)S(1)} %bitcast.14), channel_id=1, source_target_pairs={{0,2},{1,3},{2,0},{3,1},{4,6},{5,7},{6,4},{7,5},{8,10},{9,11},{10,... | collective-permute-start | bytes 6152 | tf_op jit(solution)/shard_map/ppermute | solution.py:989
  12.5 2.7 %collective-permute-start.2 = (s32[2,256]{1,0:T(2,128)S(1)}, s32[2,256]{1,0:T(2,128)S(1)}, u32[]{:S(2)}, u32[]{:S(2)}) collective-permute-start(s32[2,256]{1,0:T(2,128)S(1)} %bitcast.15), channel_id=1, source_target_pairs={{0,3},{1,0},{2,1},{3,2},{4,7},{5,4},{6,5},{7,6},{8,11},{9,8},{10,9... | collective-permute-start | bytes 6152 | tf_op jit(solution)/shard_map/ppermute | solution.py:989
  26.3 18.7 %all-to-all-start.3 = ((bf16[8,264,128]{2,1,0:T(8,128)(2,1)}), bf16[8,264,128]{2,1,0:T(8,128)(2,1)S(1)}, u32[]{:S(2)}, u32[]{:S(2)}) async-start(bf16[8,264,128]{2,1,0:T(8,128)(2,1)} %prefix_with_counts.1), calls=%async_computation.3 | async-start | bytes 1081344 | tf_op jit(solution)/shard_map/all_to_all | solution.py:998
  31.0 12.9 %collective-permute-start.3 = (bf16[256,512]{1,0:T(8,128)(2,1)}, bf16[256,512]{1,0:T(8,128)(2,1)S(1)}, u32[]{:S(2)}, u32[]{:S(2)}) collective-permute-start(bf16[256,512]{1,0:T(8,128)(2,1)} %get-tuple-element.49), channel_id=1, source_target_pairs={{0,1},{1,2},{2,3},{3,0},{4,5},{5,6},{6,7},{7,4},{8,9},{9,10},{10,1... | collective-permute-start | bytes 786440 | tf_op jit(solution)/shard_map/ppermute | solution.py:989
  31.0 12.9 %collective-permute-start.4 = (bf16[256,512]{1,0:T(8,128)(2,1)}, bf16[256,512]{1,0:T(8,128)(2,1)}, u32[]{:S(2)}, u32[]{:S(2)}) collective-permute-start(bf16[256,512]{1,0:T(8,128)(2,1)} %get-tuple-element.50), channel_id=1, source_target_pairs={{0,2},{1,3},{2,0},{3,1},{4,6},{5,7},{6,4},{7,5},{8,10},{9,11},{10,... | collective-permute-start | bytes 786440 | tf_op jit(solution)/shard_map/ppermute | solution.py:989
  32.5 12.1 %collective-permute-start.5 = (bf16[256,512]{1,0:T(8,128)(2,1)}, bf16[256,512]{1,0:T(8,128)(2,1)}, u32[]{:S(2)}, u32[]{:S(2)}) collective-permute-start(bf16[256,512]{1,0:T(8,128)(2,1)} %get-tuple-element.51), channel_id=1, source_target_pairs={{0,3},{1,0},{2,1},{3,2},{4,7},{5,4},{6,5},{7,6},{8,11},{9,8},{10,9... | collective-permute-start | bytes 786440 | tf_op jit(solution)/shard_map/ppermute | solution.py:989
  34.2 10.7 %copy-start.6 = (f32[512]{0:T(512)S(1)}, f32[512]{0:T(512)}, u32[]{:S(2)}) copy-start(f32[512]{0:T(512)} %param.20) | copy-start | bytes 6148
  43.9 1.0 copy-start.9
  51.4 54.8 %all-to-all-start.4 = ((bf16[32,64,512]{2,1,0:T(8,128)(2,1)}), bf16[32,64,512]{2,1,0:T(8,128)(2,1)S(1)}, u32[]{:S(2)}, u32[]{:S(2)}) async-start(bf16[32,64,512]{2,1,0:T(8,128)(2,1)} %get-tuple-element.56), calls=%async_computation.4 | async-start | bytes 4194304 | tf_op jit(solution)/shard_map/all_to_all | solution.py:908
  57.4 53.0 %copy-start.2 = (s32[32,128]{1,0:T(8,128)S(1)}, s32[32,128]{1,0:T(8,128)}, u32[]{:S(2)}) copy-start(s32[32,128]{1,0:T(8,128)} %get-tuple-element.55.meta_ref) | copy-start | bytes 49156
  57.4 53.0 %copy-start.4 = (f32[2048]{0:T(1024)S(1)}, f32[2048]{0:T(1024)}, u32[]{:S(2)}) copy-start(f32[2048]{0:T(1024)} %param.22) | copy-start | bytes 24580
  106.2 4.3 %copy-start.7 = (bf16[32,64,512]{2,1,0:T(8,128)(2,1)}, bf16[32,64,512]{2,1,0:T(8,128)(2,1)S(1)}, u32[]{:S(2)}) copy-start(bf16[32,64,512]{2,1,0:T(8,128)(2,1)S(1)} %all-to-all-done.4.refs_0_) | copy-start | bytes 6291460
  106.2 30.3 %all-to-all-start.6 = ((bf16[32,32,512]{2,1,0:T(8,128)(2,1)}), bf16[32,32,512]{2,1,0:T(8,128)(2,1)S(1)}, u32[]{:S(2)}, u32[]{:S(2)}) async-start(bf16[32,32,512]{2,1,0:T(8,128)(2,1)} %shard_map.119), calls=%async_computation.6 | async-start | bytes 2097152 | tf_op jit(solution)/shard_map/all_to_all | solution.py:908
  158.9 1.2 copy-start.8
  189.7 5.7 %copy-start.10 = (f32[256,2]{0,1:T(2,128)S(1)}, f32[256,2]{0,1:T(2,128)}, u32[]{:S(2)}) copy-start(f32[256,2]{0,1:T(2,128)} %param.24) | copy-start | bytes 6148
  189.7 52.5 %all-to-all-start.7 = ((bf16[32,16,2048]{2,1,0:T(8,128)(2,1)}), bf16[32,16,2048]{2,1,0:T(8,128)(2,1)S(1)}, u32[]{:S(2)}, u32[]{:S(2)}) async-start(bf16[32,16,2048]{2,1,0:T(8,128)(2,1)} %get-tuple-element.68), calls=%async_computation.7 | async-start | bytes 4194304 | tf_op jit(solution)/shard_map/all_to_all | solution.py:908
  193.3 24.2 %collective-permute-start.6 = (bf16[256,512]{1,0:T(8,128)(2,1)}, bf16[256,512]{1,0:T(8,128)(2,1)S(1)}, u32[]{:S(2)}, u32[]{:S(2)}) collective-permute-start(bf16[256,512]{1,0:T(8,128)(2,1)} %get-tuple-element.60.refs_1_), channel_id=1, source_target_pairs={{0,3},{1,0},{2,1},{3,2},{4,7},{5,4},{6,5},{7,6},{8,11},{9,8},{10,9... | collective-permute-start | bytes 786440 | tf_op jit(solution)/shard_map/ppermute | solution.py:989
  194.9 32.3 %collective-permute-start.7 = (bf16[256,512]{1,0:T(8,128)(2,1)}, bf16[256,512]{1,0:T(8,128)(2,1)}, u32[]{:S(2)}, u32[]{:S(2)}) collective-permute-start(bf16[256,512]{1,0:T(8,128)(2,1)} %get-tuple-element.61.refs_2_), channel_id=1, source_target_pairs={{0,2},{1,3},{2,0},{3,1},{4,6},{5,7},{6,4},{7,5},{8,10},{9,11},{10,... | collective-permute-start | bytes 786440 | tf_op jit(solution)/shard_map/ppermute | solution.py:989
  195.3 31.9 %collective-permute-start.8 = (bf16[256,512]{1,0:T(8,128)(2,1)}, bf16[256,512]{1,0:T(8,128)(2,1)}, u32[]{:S(2)}, u32[]{:S(2)}) collective-permute-start(bf16[256,512]{1,0:T(8,128)(2,1)} %get-tuple-element.62.refs_3_), channel_id=1, source_target_pairs={{0,1},{1,2},{2,3},{3,0},{4,5},{5,6},{6,7},{7,4},{8,9},{9,10},{10,1... | collective-permute-start | bytes 786440 | tf_op jit(solution)/shard_map/ppermute | solution.py:989
  (1 other events, 0.9 us)

commit v6 on v5

--- a/solution.py
+++ b/solution.py
@@ -676,7 +676,7 @@
         start = pl.multiple_of((head_ref[0] + s) % parts * step, step)
         acc_ref[:, pl.ds(start, step)] = acc_ref[:, pl.ds(start, step)] + stream_refs[s][...].astype(F32)
     for j, spread in enumerate(choices(code, plan, 1, owners)):
-        pick_ref[j] = spread
+        pick_ref[j * code.shape[0]:(j + 1) * code.shape[0], :] = spread
 
     @pl.when(flag_ref[0] > 0)
     def _():
@@ -694,7 +694,7 @@
         out_specs=[VMEM] * 2,
         out_shape=[
             pltpu.HBM((tokens, width), F32),
-            pltpu.HBM((2, tokens, owners * plan.back[1]), BF16),
+            pltpu.HBM((2 * tokens, owners * plan.back[1]), BF16),
         ],
         compiler_params=params(28),
     )(head, flag, code, gates, back, late, *streams)
@@ -705,9 +705,11 @@
     step = out_ref.shape[1]
     start = pl.multiple_of(pl.program_id(0) * step, step)
     flat = back_ref[:, :, pl.ds(start, step)].reshape(owners * rows, step)
+    tokens = acc_ref.shape[0]
+    found = contract(pick_ref[...], flat, ((1,), (0,)))
     total = acc_ref[...]
     for j in range(2):
-        total = total + gates_ref[:, j:j + 1] * contract(pick_ref[j], flat, ((1,), (0,)))
+        total = total + gates_ref[:, j:j + 1] * found[j * tokens:(j + 1) * tokens]
     out_ref[...] = total.astype(BF16)
 
 

time: 247 us -> 247 us (level)
  no operation moved by 1% of the time
where the time goes in v6:
time: 247 us; the launch traced here: 246 us
  waiting for transfers between devices  102 us (41%)
  Pallas kernels  77.6 us (31%)
  starting transfers between devices  33 us (13%)
  blocking collectives  29.6 us (12%)
  local copies, waits for them, and re-layouts  2.52 us (1%)
    all_to_all x3, waiting for transfers between devices, everywhere(): lax.all_to_all(x, ('ctx', 'head'), split_axis=0, concat_axis=0, tiled=True)  60 us
    pallas_call x2, Pallas kernels, serve_experts(): pl.pallas_call(functools.partial(expert_kernel, first, taken, given, base...  43.7 us
    ppermute x9, waiting for transfers between devices, turned(): lax.ppermute(pieces[s], 'head', [(h, (h + step * s) % parts) for h in ran...  33.6 us
    all_to_all x1, blocking collectives, everywhere(): lax.all_to_all(x, ('ctx', 'head'), split_axis=0, concat_axis=0, tiled=True)  29.6 us
    all_to_all x3, starting transfers between devices, everywhere(): lax.all_to_all(x, ('ctx', 'head'), split_axis=0, concat_axis=0, tiled=True)  14 us
    all_to_all x1, waiting for transfers between devices, body_compact(): lax.all_to_all(states, 'ctx', split_axis=0, concat_axis=0, tiled=True)  8.2 us
    ppermute x9, starting transfers between devices, turned(): lax.ppermute(pieces[s], 'head', [(h, (h + step * s) % parts) for h in ran...  8.01 us
    all_to_all x1, starting transfers between devices, body_compact(): lax.all_to_all(states, 'ctx', split_axis=0, concat_axis=0, tiled=True)  7.44 us
  transfers between devices with their start and end apart: 14, of which 10 were waited for; matrix products, arithmetic and copies ran while one was open for 0% of the time, Pallas kernels for 17%

profile of v6, /device:TPU:0, one launch (start us, length us, event | category | flops | bytes accessed | tf_op | source)
XLA Modules:
  0.0 245.8 jit_solution(2411330011979049240)
XLA Ops:
  0.0 3.5 %block_states.1 = bf16[2048,128]{1,0:T(8,128)(2,1)} custom-call(bf16[1024,512]{1,0:T(8,128)(2,1)} %key_ref.3, bf16[1024,512]{1,0:T(8,128)(2,1)} %value_ref.3, s32[1,1024]{1,0:T(1,128)} %bitcast.8), custom_call_target="tpu_custom_call" | custom-call | tf_op jit(solution)/shard_map/block_states/pallas_call | solution.py:52
  3.5 7.4 %all-to-all-start.2 = ((bf16[8,256,128]{2,1,0:T(8,128)(2,1)}), bf16[8,256,128]{2,1,0:T(8,128)(2,1)S(1)}, u32[]{:S(2)}, u32[]{:S(2)}) async-start(bf16[8,256,128]{2,1,0:T(8,128)(2,1)} %bitcast.19), calls=%async_computation.2 | async-start | bytes 1048576 | tf_op jit(solution)/shard_map/all_to_all | solution.py:997
  11.0 1.6 collective-permute-start.1
  15.2 2.0 count_choices.1.meta_ref
  17.2 8.2 %all-to-all-done.2.piece_ref = bf16[8,256,128]{2,1,0:T(8,128)(2,1)S(1)} async-done(((bf16[8,256,128]{2,1,0:T(8,128)(2,1)}), bf16[8,256,128]{2,1,0:T(8,128)(2,1)S(1)}, u32[]{:S(2)}, u32[]{:S(2)}) %all-to-all-start.2) | async-done | bytes 524320 | tf_op jit(solution)/shard_map/all_to_all | solution.py:997
  26.3 3.6 %all-to-all-start.3 = ((bf16[8,264,128]{2,1,0:T(8,128)(2,1)}), bf16[8,264,128]{2,1,0:T(8,128)(2,1)S(1)}, u32[]{:S(2)}, u32[]{:S(2)}) async-start(bf16[8,264,128]{2,1,0:T(8,128)(2,1)} %prefix_with_counts.1), calls=%async_computation.3 | async-start | bytes 1081344 | tf_op jit(solution)/shard_map/all_to_all | solution.py:1000
  34.2 6.0 %local_attention.1.local_ref = f32[1024,512]{1,0:T(8,128)S(1)} custom-call(bf16[1024,512]{1,0:T(8,128)(2,1)} %query_ref.3, bf16[1024,512]{1,0:T(8,128)(2,1)} %key_ref.3, bf16[1024,512]{1,0:T(8,128)(2,1)} %value_ref.3, s32[1,1024]{1,0:T(1,128)S(1)} %bitcast.10, s32[1024,1]{1,0:T(8,128)S(1)} %copy.15.route_col_ref), custom_call_target="tpu_custom_call" | custom-call | tf_op jit(solution)/shard_map/local_attention/pallas_call | solution.py:111
  40.3 3.7 %route.1 = (s32[256,128]{1,0:T(8,128)}, bf16[4,512,256]{2,1,0:T(8,128)(2,1)}, bf16[4,256,256]{2,1,0:T(8,128)(2,1)}, bf16[4,256,256]{2,1,0:T(8,128)(2,1)}) custom-call(s32[2,256]{1,0:T(2,128)S(1)} %bitcast.17, s32[2,256]{1,0:T(2,128)S(1)} %collective-permute-done.refs_1_, s32[2,256]{1,0:T(2,128)S(1)} %collective-permute-done.1.refs_2_, ...), custom_call_target="tpu_custom_call" | custom-call | tf_op jit(solution)/shard_map/route/pallas_call | solution.py:460
  44.9 5.7 %mix_and_pack.1 = (s32[32,128]{1,0:T(8,128)}, s32[1]{0:T(128)}, bf16[32,64,512]{2,1,0:T(8,128)(2,1)}, bf16[256,512]{1,0:T(8,128)(2,1)}, bf16[256,512]{1,0:T(8,12...) custom-call(s32[1]{0:T(128)} %bitcast.head_ref, bf16[1024,512]{1,0:T(8,128)(2,1)} %query_ref.3, ...), custom_call_target="tpu_custom_call" | custom-call | tf_op jit(solution)/shard_map/mix_and_pack/pallas_call | solution.py:584
  51.4 6.1 %all-to-all-start.4 = ((bf16[32,64,512]{2,1,0:T(8,128)(2,1)}), bf16[32,64,512]{2,1,0:T(8,128)(2,1)S(1)}, u32[]{:S(2)}, u32[]{:S(2)}) async-start(bf16[32,64,512]{2,1,0:T(8,128)(2,1)} %get-tuple-element.56), calls=%async_computation.4 | async-start | bytes 4194304 | tf_op jit(solution)/shard_map/all_to_all | solution.py:910
  57.5 2.8 %shard_map.119 = bf16[32,32,512]{2,1,0:T(8,128)(2,1)} custom-call(bf16[4,256,256]{2,1,0:T(8,128)(2,1)} %get-tuple-element.58.spread_ref, bf16[256,512]{1,0:T(8,128)(2,1)} %get-tuple-element.59.refs_0_, bf16[256,512]{1,0:T(8,128)(2,1)} %get-tuple-element.60.refs_1_, bf16[256,512]{1,0:T(8,128)(2,1)} %get-tuple-element.61.refs_2_, ...), custom_call_target="tpu_custom_call" | custom-call | tf_op jit(solution)/shard_map/pallas_call | solution.py:631
  60.2 46.0 %all-to-all-done.4.refs_0_ = bf16[32,64,512]{2,1,0:T(8,128)(2,1)S(1)} async-done(((bf16[32,64,512]{2,1,0:T(8,128)(2,1)}), bf16[32,64,512]{2,1,0:T(8,128)(2,1)S(1)}, u32[]{:S(2)}, u32[]{:S(2)}) %all-to-all-start.4) | async-done | bytes 2097184 | tf_op jit(solution)/shard_map/all_to_all | solution.py:910
  106.2 4.3 %all-to-all-start.6 = ((bf16[32,32,512]{2,1,0:T(8,128)(2,1)}), bf16[32,32,512]{2,1,0:T(8,128)(2,1)S(1)}, u32[]{:S(2)}, u32[]{:S(2)}) async-start(bf16[32,32,512]{2,1,0:T(8,128)(2,1)} %shard_map.119), calls=%async_computation.6 | async-start | bytes 2097152 | tf_op jit(solution)/shard_map/all_to_all | solution.py:910
  110.5 21.3 %shard_map.118 = (bf16[32,8,2048]{2,1,0:T(8,128)(2,1)}, bf16[32,16,2048]{2,1,0:T(8,128)(2,1)}) custom-call(s32[1]{0:T(128)} %get-tuple-element.53.flag_ref, s32[32,128]{1,0:T(8,128)S(1)} %copy-done.2, f32[1,2048]{1,0:T(1,128)S(1)} %bitcast.11, bf16[32,64,512]{2,1,0:T(8,128)(2,1)} %copy-done.7, bf16[8,2048,512]{2,1,0:T(8,128)(2,1)} %refs_3_.3, ...), custom_call_target="tpu_custom_call" | custom-call | tf_op jit(solution)/shard_map/pallas_call | solution.py:885
  131.7 4.7 %all-to-all-done.6.refs_1_ = bf16[32,32,512]{2,1,0:T(8,128)(2,1)S(1)} async-done(((bf16[32,32,512]{2,1,0:T(8,128)(2,1)}), bf16[32,32,512]{2,1,0:T(8,128)(2,1)S(1)}, u32[]{:S(2)}, u32[]{:S(2)}) %all-to-all-start.6) | async-done | bytes 1048608 | tf_op jit(solution)/shard_map/all_to_all | solution.py:910
  136.5 22.4 %shard_map.120 = (bf16[32,16,2048]{2,1,0:T(8,128)(2,1)}, bf16[32,8,2048]{2,1,0:T(8,128)(2,1)}) custom-call(s32[1]{0:T(128)} %get-tuple-element.53.flag_ref, s32[32,128]{1,0:T(8,128)S(1)} %copy-done.2, f32[1,2048]{1,0:T(1,128)S(1)} %bitcast.12, bf16[32,64,512]{2,1,0:T(8,128)(2,1)} %copy-done.7, bf16[32,32,512]{2,1,0:T(8,128)(2,1)S(1)} %all-to-all-done.6.refs_1_, ...), custom_call_target="tpu_custom_call" | custom-call | tf_op jit(solution)/shard_map/pallas_call | solution.py:885
  160.1 29.6 %all_to_all.44.back_ref = bf16[32,8,2048]{2,1,0:T(8,128)(2,1)S(1)} all-to-all(bf16[32,8,2048]{2,1,0:T(8,128)(2,1)S(1)} %copy-done.8), channel_id=1, replica_groups=mesh['ctx'=8,'head'=4] {'ctx','head'}, dimensions={0} | all-to-all | bytes 2097152 | tf_op jit(solution)/shard_map/all_to_all | solution.py:910
  189.7 3.6 %all-to-all-start.7 = ((bf16[32,16,2048]{2,1,0:T(8,128)(2,1)}), bf16[32,16,2048]{2,1,0:T(8,128)(2,1)S(1)}, u32[]{:S(2)}, u32[]{:S(2)}) async-start(bf16[32,16,2048]{2,1,0:T(8,128)(2,1)} %get-tuple-element.68), calls=%async_computation.7 | async-start | bytes 4194304 | tf_op jit(solution)/shard_map/all_to_all | solution.py:910
  193.3 1.5 collective-permute-start.6
  195.5 22.0 %collective-permute-done.6.refs_1_ = bf16[256,512]{1,0:T(8,128)(2,1)S(1)} collective-permute-done((bf16[256,512]{1,0:T(8,128)(2,1)}, bf16[256,512]{1,0:T(8,128)(2,1)S(1)}, u32[]{:S(2)}, u32[]{:S(2)}) %collective-permute-start.6) | collective-permute-done | bytes 262176 | tf_op jit(solution)/shard_map/ppermute | solution.py:991
  217.5 9.6 %collective-permute-done.7.refs_2_ = bf16[256,512]{1,0:T(8,128)(2,1)} collective-permute-done((bf16[256,512]{1,0:T(8,128)(2,1)}, bf16[256,512]{1,0:T(8,128)(2,1)}, u32[]{:S(2)}, u32[]{:S(2)}) %collective-permute-start.7) | collective-permute-done | bytes 262176 | tf_op jit(solution)/shard_map/ppermute | solution.py:991
  228.1 4.8 %combine_ahead.1 = (f32[256,2048]{1,0:T(8,128)}, bf16[512,512]{1,0:T(8,128)(2,1)}) custom-call(s32[1]{0:T(128)} %bitcast.head_ref, s32[1]{0:T(128)} %get-tuple-element.53.flag_ref, s32[256,128]{1,0:T(8,128)S(1)} %copy-done.1, f32[256,2]{1,0:T(8,128)S(1)} %copy.18.gates_ref, bf16[32,8,2048]{2,1,0:T(8,128)(2,1)S(1)} %all_to_all.44.back_ref, ...), custom_call_target="tpu_custom_call" | custom-call | tf_op jit(solution)/shard_map/combine_ahead/pallas_call | solution.py:690
  232.9 9.3 %all-to-all-done.7.back_ref = bf16[32,16,2048]{2,1,0:T(8,128)(2,1)S(1)} async-done(((bf16[32,16,2048]{2,1,0:T(8,128)(2,1)}), bf16[32,16,2048]{2,1,0:T(8,128)(2,1)S(1)}, u32[]{:S(2)}, u32[]{:S(2)}) %all-to-all-start.7) | async-done | bytes 2097184 | tf_op jit(solution)/shard_map/all_to_all | solution.py:910
  242.2 3.6 %combine.1 = bf16[256,2048]{1,0:T(8,128)(2,1)} custom-call(f32[256,2]{1,0:T(8,128)S(1)} %copy.18.gates_ref, f32[256,2048]{1,0:T(8,128)} %get-tuple-element.66.acc_ref, bf16[512,512]{1,0:T(8,128)(2,1)} %get-tuple-element.67.pick_ref, bf16[32,16,2048]{2,1,0:T(8,128)(2,1)S(1)} %all-to-all-done.7.back_ref), custom_call_target="tpu_custom_call" | custom-call | tf_op jit(solution)/shard_map/combine/pallas_call | solution.py:724
  (45 shorter events, 11.7 us)
Async XLA Ops:
  0.0 10.9 %copy-start.5 = (s32[256,2]{0,1:T(2,128)S(1)}, s32[256,2]{0,1:T(2,128)}, u32[]{:S(2)}) copy-start(s32[256,2]{0,1:T(2,128)} %param.23) | copy-start | bytes 6148
  3.5 26.4 %copy-start = (bf16[256,2048]{1,0:T(8,128)(2,1)S(1)}, bf16[256,2048]{1,0:T(8,128)(2,1)}, u32[]{:S(2)}) copy-start(bf16[256,2048]{1,0:T(8,128)(2,1)} %whole_ref.1) | copy-start | bytes 3145732
  3.5 30.5 %copy-start.3 = (s32[1024]{0:T(1024)S(1)}, s32[1024]{0:T(1024)}, u32[]{:S(2)}) copy-start(s32[1024]{0:T(1024)} %param.19) | copy-start | bytes 12292
  3.5 21.9 %all-to-all-start.2 = ((bf16[8,256,128]{2,1,0:T(8,128)(2,1)}), bf16[8,256,128]{2,1,0:T(8,128)(2,1)S(1)}, u32[]{:S(2)}, u32[]{:S(2)}) async-start(bf16[8,256,128]{2,1,0:T(8,128)(2,1)} %bitcast.19), calls=%async_computation.2 | async-start | bytes 1048576 | tf_op jit(solution)/shard_map/all_to_all | solution.py:997
  10.9 3.1 %collective-permute-start = (s32[2,256]{1,0:T(2,128)S(1)}, s32[2,256]{1,0:T(2,128)S(1)}, u32[]{:S(2)}, u32[]{:S(2)}) collective-permute-start(s32[2,256]{1,0:T(2,128)S(1)} %bitcast.13), channel_id=1, source_target_pairs={{0,1},{1,2},{2,3},{3,0},{4,5},{5,6},{6,7},{7,4},{8,9},{9,10},{10,1... | collective-permute-start | bytes 6152 | tf_op jit(solution)/shard_map/ppermute | solution.py:991
  11.0 3.7 %collective-permute-start.1 = (s32[2,256]{1,0:T(2,128)S(1)}, s32[2,256]{1,0:T(2,128)S(1)}, u32[]{:S(2)}, u32[]{:S(2)}) collective-permute-start(s32[2,256]{1,0:T(2,128)S(1)} %bitcast.14), channel_id=1, source_target_pairs={{0,2},{1,3},{2,0},{3,1},{4,6},{5,7},{6,4},{7,5},{8,10},{9,11},{10,... | collective-permute-start | bytes 6152 | tf_op jit(solution)/shard_map/ppermute | solution.py:991
  12.5 2.7 %collective-permute-start.2 = (s32[2,256]{1,0:T(2,128)S(1)}, s32[2,256]{1,0:T(2,128)S(1)}, u32[]{:S(2)}, u32[]{:S(2)}) collective-permute-start(s32[2,256]{1,0:T(2,128)S(1)} %bitcast.15), channel_id=1, source_target_pairs={{0,3},{1,0},{2,1},{3,2},{4,7},{5,4},{6,5},{7,6},{8,11},{9,8},{10,9... | collective-permute-start | bytes 6152 | tf_op jit(solution)/shard_map/ppermute | solution.py:991
  26.3 18.7 %all-to-all-start.3 = ((bf16[8,264,128]{2,1,0:T(8,128)(2,1)}), bf16[8,264,128]{2,1,0:T(8,128)(2,1)S(1)}, u32[]{:S(2)}, u32[]{:S(2)}) async-start(bf16[8,264,128]{2,1,0:T(8,128)(2,1)} %prefix_with_counts.1), calls=%async_computation.3 | async-start | bytes 1081344 | tf_op jit(solution)/shard_map/all_to_all | solution.py:1000
  31.0 12.9 %collective-permute-start.3 = (bf16[256,512]{1,0:T(8,128)(2,1)}, bf16[256,512]{1,0:T(8,128)(2,1)S(1)}, u32[]{:S(2)}, u32[]{:S(2)}) collective-permute-start(bf16[256,512]{1,0:T(8,128)(2,1)} %get-tuple-element.49), channel_id=1, source_target_pairs={{0,1},{1,2},{2,3},{3,0},{4,5},{5,6},{6,7},{7,4},{8,9},{9,10},{10,1... | collective-permute-start | bytes 786440 | tf_op jit(solution)/shard_map/ppermute | solution.py:991
  31.0 12.9 %collective-permute-start.4 = (bf16[256,512]{1,0:T(8,128)(2,1)}, bf16[256,512]{1,0:T(8,128)(2,1)}, u32[]{:S(2)}, u32[]{:S(2)}) collective-permute-start(bf16[256,512]{1,0:T(8,128)(2,1)} %get-tuple-element.50), channel_id=1, source_target_pairs={{0,2},{1,3},{2,0},{3,1},{4,6},{5,7},{6,4},{7,5},{8,10},{9,11},{10,... | collective-permute-start | bytes 786440 | tf_op jit(solution)/shard_map/ppermute | solution.py:991
  32.5 12.1 %collective-permute-start.5 = (bf16[256,512]{1,0:T(8,128)(2,1)}, bf16[256,512]{1,0:T(8,128)(2,1)}, u32[]{:S(2)}, u32[]{:S(2)}) collective-permute-start(bf16[256,512]{1,0:T(8,128)(2,1)} %get-tuple-element.51), channel_id=1, source_target_pairs={{0,3},{1,0},{2,1},{3,2},{4,7},{5,4},{6,5},{7,6},{8,11},{9,8},{10,9... | collective-permute-start | bytes 786440 | tf_op jit(solution)/shard_map/ppermute | solution.py:991
  34.2 10.7 %copy-start.6 = (f32[512]{0:T(512)S(1)}, f32[512]{0:T(512)}, u32[]{:S(2)}) copy-start(f32[512]{0:T(512)} %param.20) | copy-start | bytes 6148
  43.9 1.0 copy-start.9
  51.4 54.8 %all-to-all-start.4 = ((bf16[32,64,512]{2,1,0:T(8,128)(2,1)}), bf16[32,64,512]{2,1,0:T(8,128)(2,1)S(1)}, u32[]{:S(2)}, u32[]{:S(2)}) async-start(bf16[32,64,512]{2,1,0:T(8,128)(2,1)} %get-tuple-element.56), calls=%async_computation.4 | async-start | bytes 4194304 | tf_op jit(solution)/shard_map/all_to_all | solution.py:910
  57.4 53.0 %copy-start.2 = (s32[32,128]{1,0:T(8,128)S(1)}, s32[32,128]{1,0:T(8,128)}, u32[]{:S(2)}) copy-start(s32[32,128]{1,0:T(8,128)} %get-tuple-element.55.meta_ref) | copy-start | bytes 49156
  57.4 53.0 %copy-start.4 = (f32[2048]{0:T(1024)S(1)}, f32[2048]{0:T(1024)}, u32[]{:S(2)}) copy-start(f32[2048]{0:T(1024)} %param.22) | copy-start | bytes 24580
  106.2 4.3 %copy-start.7 = (bf16[32,64,512]{2,1,0:T(8,128)(2,1)}, bf16[32,64,512]{2,1,0:T(8,128)(2,1)S(1)}, u32[]{:S(2)}) copy-start(bf16[32,64,512]{2,1,0:T(8,128)(2,1)S(1)} %all-to-all-done.4.refs_0_) | copy-start | bytes 6291460
  106.2 30.3 %all-to-all-start.6 = ((bf16[32,32,512]{2,1,0:T(8,128)(2,1)}), bf16[32,32,512]{2,1,0:T(8,128)(2,1)S(1)}, u32[]{:S(2)}, u32[]{:S(2)}) async-start(bf16[32,32,512]{2,1,0:T(8,128)(2,1)} %shard_map.119), calls=%async_computation.6 | async-start | bytes 2097152 | tf_op jit(solution)/shard_map/all_to_all | solution.py:910
  158.9 1.2 copy-start.8
  189.7 5.7 %copy-start.10 = (f32[256,2]{0,1:T(2,128)S(1)}, f32[256,2]{0,1:T(2,128)}, u32[]{:S(2)}) copy-start(f32[256,2]{0,1:T(2,128)} %param.24) | copy-start | bytes 6148
  189.7 52.5 %all-to-all-start.7 = ((bf16[32,16,2048]{2,1,0:T(8,128)(2,1)}), bf16[32,16,2048]{2,1,0:T(8,128)(2,1)S(1)}, u32[]{:S(2)}, u32[]{:S(2)}) async-start(bf16[32,16,2048]{2,1,0:T(8,128)(2,1)} %get-tuple-element.68), calls=%async_computation.7 | async-start | bytes 4194304 | tf_op jit(solution)/shard_map/all_to_all | solution.py:910
  193.3 24.2 %collective-permute-start.6 = (bf16[256,512]{1,0:T(8,128)(2,1)}, bf16[256,512]{1,0:T(8,128)(2,1)S(1)}, u32[]{:S(2)}, u32[]{:S(2)}) collective-permute-start(bf16[256,512]{1,0:T(8,128)(2,1)} %get-tuple-element.60.refs_1_), channel_id=1, source_target_pairs={{0,3},{1,0},{2,1},{3,2},{4,7},{5,4},{6,5},{7,6},{8,11},{9,8},{10,9... | collective-permute-start | bytes 786440 | tf_op jit(solution)/shard_map/ppermute | solution.py:991
  194.9 32.3 %collective-permute-start.7 = (bf16[256,512]{1,0:T(8,128)(2,1)}, bf16[256,512]{1,0:T(8,128)(2,1)}, u32[]{:S(2)}, u32[]{:S(2)}) collective-permute-start(bf16[256,512]{1,0:T(8,128)(2,1)} %get-tuple-element.61.refs_2_), channel_id=1, source_target_pairs={{0,2},{1,3},{2,0},{3,1},{4,6},{5,7},{6,4},{7,5},{8,10},{9,11},{10,... | collective-permute-start | bytes 786440 | tf_op jit(solution)/shard_map/ppermute | solution.py:991
  195.3 31.9 %collective-permute-start.8 = (bf16[256,512]{1,0:T(8,128)(2,1)}, bf16[256,512]{1,0:T(8,128)(2,1)}, u32[]{:S(2)}, u32[]{:S(2)}) collective-permute-start(bf16[256,512]{1,0:T(8,128)(2,1)} %get-tuple-element.62.refs_3_), channel_id=1, source_target_pairs={{0,1},{1,2},{2,3},{3,0},{4,5},{5,6},{6,7},{7,4},{8,9},{9,10},{10,1... | collective-permute-start | bytes 786440 | tf_op jit(solution)/shard_map/ppermute | solution.py:991
  (1 other events, 0.9 us)
